TPU v7x, 256 devices: a whole 4x4x8 slice. The times are simulated.
256 devices in a mesh: grp: 4 (over x), cell: 64 (over z, y, core).
Axes of the slice: x: 4, y: 4, z: 8, core: 2. Of those that a mesh axis runs over, the one named last changes fastest.
Arguments:
- fields: bfloat16 [512, 32, 65536], P('grp', None, 'cell'), may hold values from -6 to 6
- scales: float32 [512, 32, 512], P('grp', None, 'cell'), may hold values from 0.25 to 4
- pod_basis: bfloat16 [65536, 64], P('cell'), may hold values from -0.0234375 to 0.0234375
- param_order: int32 [30], replicated, may hold values from 0 to 29, each once
Outputs:
- sobol_maps: float32 [30, 65536], P(None, 'cell')
- total_map: float32 [65536], P('cell')
Inputs may be any that keep to these rules, and one draw needn't show every extreme that they name: `param_order`: each parameter appears exactly once.
All inputs are finite; a program needn't handle non-finite values.
Results may differ from a plain program's by a relative error of at most 0.0003.
The roundings to bfloat16 on the way count: a program that leaves them out, or rounds other values in their place, can miss the bound.
Values sent between devices are 32-bit elements; how exact they have to be, the bound alone decides.
No kernel may reach another device: no remote copies, remote signals or barrier semaphores. Data moves between devices by JAX's collectives and lax.ppermute only.
A program may use at most 128 MiB of HBM per device.

v0:
```python
import jax
import jax.numpy as jnp
from jax import lax
from jax.sharding import PartitionSpec as P


def project(piece, scale_piece, basis_piece):
    rows, slots, cells = piece.shape
    blocks = scale_piece.shape[2]
    dequant = (
        piece.astype(jnp.float32).reshape(rows, slots, blocks, cells // blocks)
        * scale_piece[..., None]
    ).astype(jnp.bfloat16)
    flat = dequant.reshape(rows * slots, cells)
    return jnp.dot(flat, basis_piece, preferred_element_type=jnp.float32).reshape(
        rows, slots, basis_piece.shape[1]
    )


def moments(coefficients):
    first = coefficients[:, 0]
    second_set = coefficients[:, 1]
    swapped = coefficients[:, 2:] - first[:, None, :]
    cross = jnp.einsum("rk,rpl->pkl", second_set, swapped, precision=lax.Precision.HIGHEST)
    squares = jnp.dot(first.T, first, precision=lax.Precision.HIGHEST) + jnp.dot(
        second_set.T, second_set, precision=lax.Precision.HIGHEST
    )
    column_sums = jnp.sum(first, axis=0) + jnp.sum(second_set, axis=0)
    return (cross, squares, column_sums)


def finish(cross, squares, column_sums, row_total, param_order, pod_basis, cell_total):
    count = param_order.shape[0]
    slot_cov = cross / row_total
    selector = (param_order[:, None] == jnp.arange(count)[None, :]).astype(jnp.float32)
    param_cov = jnp.einsum("sp,skl->pkl", selector, slot_cov, precision=lax.Precision.HIGHEST)
    average = column_sums / (2.0 * row_total)
    covariance = squares / (2.0 * row_total) - average[:, None] * average[None, :]
    stacked = jnp.concatenate([param_cov, covariance[None]], axis=0)
    phi = pod_basis.astype(jnp.float32)
    products = jnp.einsum("xk,pkl->pxl", phi, stacked, precision=lax.Precision.HIGHEST)
    all_maps = cell_total * jnp.sum(products * phi[None], axis=2)
    return (all_maps[:-1], all_maps[-1])


def on_device(fields, scales, pod_basis, param_order):
    row_count = fields.shape[0]
    group_count = lax.axis_size("grp")
    cell_devices = lax.axis_size("cell")
    row_total = float(row_count * group_count)
    cell_total = float(fields.shape[2] * cell_devices)
    partial_modes = project(fields, scales, pod_basis)
    coefficients = lax.psum(partial_modes, "cell")
    cross, squares, column_sums = moments(coefficients)
    cross, squares, column_sums = lax.psum((cross, squares, column_sums), "grp")
    return finish(cross, squares, column_sums, row_total, param_order, pod_basis, cell_total)


def solution(mesh):
    placed = (P("grp", None, "cell"), P("grp", None, "cell"), P("cell", None), P())
    return jax.shard_map(
        on_device,
        mesh=mesh,
        in_specs=placed,
        out_specs=(P(None, "cell"), P("cell")),
        check_vma=False,
    )
```

profile of v0, /device:TPU:1, one launch (start us, length us, event | category | flops | bytes accessed | tf_op | source)
XLA Modules:
  0.0 303.9 jit_solution(6432894145977355311)
XLA Ops:
  7.2 0.0 all-reduce.4.cloned.1.call-start
  7.2 2.7 copy.6
  9.9 8.5 %mul.39 = f32[128,32,8,128]{3,2,1,0:T(8,128)} broadcast(f32[128,32,8]{2,1,0:T(8,128)S(1)} %copy.6), dimensions={0,1,2} | broadcast | bytes 16908288 | tf_op jit(solution)/shard_map/mul | solution.py:11
  18.4 0.0 copy-start
  18.4 18.0 %mul.40 = f32[128,32,1024]{2,1,0:T(8,128)} reshape(f32[128,32,8,128]{3,2,1,0:T(8,128)} %mul.39) | data formatting | bytes 33554432 | tf_op jit(solution)/shard_map/mul | solution.py:11
  36.5 0.0 copy-done
  36.5 10.5 %fusion = f32[128,32,64]{2,1,0:T(8,128)S(1)} fusion(f32[128,32,1024]{2,1,0:T(8,128)} %mul.40, bf16[128,32,1024]{2,1,0:T(8,128)(2,1)} %param.4, bf16[1024,64]{0,1:T(8,128)(2,1)S(1)} %copy-done), kind=kOutput, calls=%fused_computation.1 | convolution fusion | flops 549453824 | bytes 26345472 | tf_op jit(solution)/shard_map/dot_general | solution.py:15
  47.0 0.0 copy-start.2
  47.0 2.3 copy.10
  49.3 0.0 all-reduce.4.cloned.1.call-update
  49.3 0.0 all-reduce.6.cloned.1.call-start
  49.4 187.7 %all-reduce.4.cloned.1.call-done = f32[128,32,64]{0,2,1:T(8,128)} async-done(((f32[128,32,64]{0,2,1:T(8,128)}), f32[128,32,64]{0,2,1:T(8,128)}) %all-reduce.4.cloned.1.call-update) | async-done | bytes 1048592 | tf_op jit(solution)/shard_map/psum | solution.py:53
  237.1 0.9 slice_reduce_fusion.1
  238.0 3.1 %convolution_bitcast_fusion = f32[30,64,64]{1,2,0:T(8,128)} fusion(f32[128,32,64]{0,2,1:T(8,128)} %all-reduce.4.cloned.1.call-done, f32[128,64]{0,1:T(8,128)S(1)} %get-tuple-element.6), kind=kOutput, calls=%fused_computation.4 | convolution fusion | flops 188989440 | bytes 1540096 | tf_op jit(solution)/shard_map/rk,rpl->pkl/dot_general | solution.py:24
  241.1 0.0 all-reduce.6.cloned.1.call-update
  241.1 1.0 fusion.17
  242.1 1.0 convolution_add_fusion
  243.2 14.3 %all-reduce = (f32[64,64]{1,0:T(8,128)S(1)}, f32[64]{0:T(128)S(1)}) all-reduce(f32[64,64]{1,0:T(8,128)S(1)} %convolution_add_fusion, f32[64]{0:T(128)S(1)} %add.15), channel_id=1, replica_groups=mesh['grp'=4,'cell'=64] {'grp'}, use_global_device_ids=true, to_apply=%region_2.0 | all-reduce | flops 4160 | bytes 33280 | tf_op jit(solution)/shard_map/psum | solution.py:55
  257.5 0.1 subtract_bitcast_fusion
  257.6 0.1 copy.8
  257.6 31.6 %all-reduce.6.cloned.1.call-done = f32[30,64,64]{1,2,0:T(8,128)} async-done(((f32[30,64,64]{1,2,0:T(8,128)}), f32[30,64,64]{1,2,0:T(8,128)}) %all-reduce.6.cloned.1.call-update) | async-done | bytes 491536 | tf_op jit(solution)/shard_map/psum | solution.py:55
  289.2 1.3 broadcast_multiply_fusion
  290.5 0.9 copy.11
  291.4 0.0 copy-done.2
  291.4 0.7 fusion.13
  292.1 0.6 copy.12
  292.7 3.7 %fusion.1 = f32[31,1024]{1,0:T(8,128)S(1)} fusion(f32[1024,64]{0,1:T(8,128)S(1)} %convert_element_type.14, f32[1,64,64]{1,2,0:T(8,128)S(1)} %copy.8, f32[30,64,64]{1,2,0:T(8,128)S(1)} %copy.12, bf16[1024,64]{0,1:T(8,128)(2,1)S(1)} %copy-done), kind=kOutput, calls=%fused_computation.3 | convolution fusion | flops 1564439552 | bytes 1028096 | tf_op jit(solution)/shard_map/xk,pkl->pxl/dot_general | solution.py:41
  296.5 0.0 copy-start.1
  296.5 0.6 slice.24
  297.1 0.0 copy-done.1
  (4 shorter events, 0.0 us)
Async XLA Ops:
  7.2 230.0 %all-reduce.4.cloned.1.call-start = ((), (), s32[]{:S(2)}) async-start(), calls=%async_computation | async-start | bytes 2097152 | tf_op jit(solution)/shard_map/psum | solution.py:53
  18.4 18.1 %copy-start = (bf16[1024,64]{0,1:T(8,128)(2,1)S(1)}, bf16[1024,64]{0,1:T(8,128)(2,1)}, u32[]{:S(2)}) copy-start(bf16[1024,64]{0,1:T(8,128)(2,1)} %param.6) | copy-start | bytes 393220
  47.0 244.5 %copy-start.2 = (s32[30]{0:T(128)S(1)}, s32[30]{0:T(128)}, u32[]{:S(2)}) copy-start(s32[30]{0:T(128)} %param.7) | copy-start | bytes 364
  49.3 239.9 %all-reduce.6.cloned.1.call-start = ((), (), s32[]{:S(2)}) async-start(), calls=%async_computation.1 | async-start | bytes 1966080 | tf_op jit(solution)/shard_map/psum | solution.py:55
  296.5 0.7 copy-start.1
Sparse Core Ops, SparseCore 0:
  49.4 187.6 all-reduce.3
  241.2 47.9 all-reduce.5
where the time goes:
time: 305 us; the launch traced here: 304 us
  waiting for transfers between devices  219 us (72%)
  local copies, waits for them, and re-layouts  33.8 us (11%)
  matrix products  20 us (7%)
  blocking collectives  14.3 us (5%)
  between operations  14.2 us (5%)
    psum x1, waiting for transfers between devices, on_device(): coefficients = lax.psum(partial_modes, 'cell')  188 us
    psum x1, waiting for transfers between devices, on_device(): cross, squares, column_sums = lax.psum((cross, squares, column_sums), 'grp')  31.6 us
    mul x2, local copies, waits for them, and re-layouts, project(): piece.astype(jnp.float32).reshape(rows, slots, blocks, cells // blocks)  26.5 us
    psum x1, blocking collectives, on_device(): cross, squares, column_sums = lax.psum((cross, squares, column_sums), 'grp')  14.3 us
    dot_general x1, matrix products, project(): jnp.dot(flat, basis_piece, preferred_element_type=jnp.float32)  10.5 us
  transfers between devices with their start and end apart: 2, of which 2 were waited for; matrix products, arithmetic and copies ran while one was open for 1% of the time, Pallas kernels for 0%

commit v1 on v0

v1 whole, which is shorter than its diff:
```python
import jax
import jax.numpy as jnp
from jax import lax
from jax.experimental import pallas as pl
from jax.experimental.pallas import tpu as pltpu
from jax.sharding import Mesh, PartitionSpec as P

HIGHEST = lax.Precision.HIGHEST
F32 = jnp.float32
BF16 = jnp.bfloat16
VMEM = pl.BlockSpec(memory_space=pltpu.VMEM)
SMEM = pl.BlockSpec(memory_space=pltpu.SMEM)


def project_kernel(half_ref, first_ref, second_ref, scale_ref, basis_ref, out_ref, by_block, dequant, weights):
    step = pl.program_id(0)
    rows, slots, cells = first_ref.shape
    blocks = scale_ref.shape[0] // slots
    lanes = cells // blocks
    modes = basis_ref.shape[0]
    packed = out_ref.shape[0] // slots

    @pl.when(step == 0)
    def _():
        for block in range(blocks):
            by_block[block] = scale_ref[pl.ds(block, slots, stride=blocks), :]
        turned = basis_ref[...].astype(F32).T.astype(BF16)
        weights[...] = jnp.zeros_like(weights)
        weights[:cells, :modes] = turned
        weights[cells:, modes:] = turned

    start = half_ref[0] * (2 * packed) + step * rows
    turn = lax.rem(128 - start, 128)
    for block in range(blocks):
        rolled = pltpu.roll(by_block[block], turn, 1)
        for which, source in enumerate((first_ref, second_ref)):
            for row in range(rows):
                lane = which * packed + row
                scale = jnp.broadcast_to(rolled[:, lane : lane + 1], (slots, lanes))
                piece = source[row, :, block * lanes : (block + 1) * lanes]
                column = which * cells + block * lanes
                dequant[row * slots : (row + 1) * slots, column : column + lanes] = (
                    piece.astype(F32) * scale
                ).astype(BF16)
    modes_out = jnp.dot(dequant[...], weights[...], preferred_element_type=F32)
    slot = lax.broadcasted_iota(jnp.int32, (slots, 2 * modes), 0)
    for row in range(rows):
        tile = modes_out[row * slots : (row + 1) * slots]
        tile = tile - jnp.where(slot >= 2, jnp.broadcast_to(tile[:1], tile.shape), 0.0)
        out_ref[pl.ds(step * rows + row, slots, stride=packed), :] = tile


def project(half, fields, scales, basis):
    rows, slots, cells = fields.shape
    modes = basis.shape[0]
    packed = rows // 4
    step = 8
    steps = packed // step
    grid_spec = pltpu.PrefetchScalarGridSpec(
        num_scalar_prefetch=1,
        grid=(steps,),
        in_specs=[
            pl.BlockSpec((step, slots, cells), lambda i, h: (h[0] * 2 * steps + i, 0, 0)),
            pl.BlockSpec((step, slots, cells), lambda i, h: (h[0] * 2 * steps + steps + i, 0, 0)),
            pl.BlockSpec(scales.shape, lambda i, h: (0, 0)),
            pl.BlockSpec(basis.shape, lambda i, h: (0, 0)),
        ],
        out_specs=pl.BlockSpec((slots * packed, 2 * modes), lambda i, h: (0, 0)),
        scratch_shapes=[
            pltpu.VMEM((scales.shape[0] // slots, slots, rows), F32),
            pltpu.VMEM((step * slots, 2 * cells), BF16),
            pltpu.VMEM((2 * cells, 2 * modes), BF16),
        ],
    )
    return pl.pallas_call(
        project_kernel,
        grid_spec=grid_spec,
        out_shape=jax.ShapeDtypeStruct((slots * packed, 2 * modes), F32),
        cost_estimate=pl.CostEstimate(
            flops=rows * slots * cells * modes, bytes_accessed=rows * slots * cells, transcendentals=0
        ),
        name="project",
    )(half, fields, fields, scales, basis)


def moments_kernel(where_ref, parts_ref, second_ref, keep_ref, send_ref):
    slot, half = where_ref[0], where_ref[1]
    own = parts_ref[0]
    for source in range(1, parts_ref.shape[0]):
        own = own + parts_ref[source]
    second = second_ref[0]
    for source in range(1, second_ref.shape[0]):
        second = second + second_ref[source]
    left = jnp.where(slot == 0, own, second)
    wide = lax.dot_general(left, own, (((0,), (0,)), ((), ())), precision=HIGHEST, preferred_element_type=F32)
    matrix = wide[:64, :64] + wide[64:, 64:]
    sums = jnp.sum(own, axis=0, keepdims=True)
    sums = sums[:, :64] + sums[:, 64:]
    low = jnp.concatenate([sums[:, 32:], sums[:, :32]], axis=1)
    row = lax.broadcasted_iota(jnp.int32, matrix.shape, 0)
    lane = lax.broadcasted_iota(jnp.int32, matrix.shape, 1)
    spare = (slot < 2) & (lane < 32)
    matrix = jnp.where(spare & (row == 32), jnp.broadcast_to(sums, matrix.shape), matrix)
    matrix = jnp.where(spare & (row == 33), jnp.broadcast_to(low, matrix.shape), matrix)
    upper = jnp.concatenate([matrix[:16], matrix[16:32]], axis=1)
    lower = jnp.concatenate([matrix[32:48], matrix[48:]], axis=1)
    keep_ref[...] = jnp.where(half == 0, upper, lower)
    send_ref[...] = jnp.where(half == 0, lower, upper)


def moments(where, parts, second):
    out = jax.ShapeDtypeStruct((16, 128), F32)
    return pl.pallas_call(
        moments_kernel,
        in_specs=[SMEM, VMEM, VMEM],
        out_specs=(VMEM, VMEM),
        out_shape=(out, out),
        name="moments",
    )(where, parts, second)


def three(value):
    high = value.astype(BF16)
    rest = value - high.astype(F32)
    middle = rest.astype(BF16)
    return high, middle, (rest - middle.astype(F32)).astype(BF16)


def maps_kernel(rows_total, cell_total, half_ref, order_ref, mine_ref, other_ref, basis_ref, maps_ref, total_ref):
    half = half_ref[0]
    mine, other = mine_ref[...], other_ref[...]
    halves = (jnp.where(half == 0, mine, other), jnp.where(half == 0, other, mine))
    slots = mine.shape[0]
    modes, cells = basis_ref.shape
    phi = basis_ref[...]
    none = jnp.zeros_like(phi)
    right_first = jnp.concatenate([phi, phi, phi, none], axis=0)
    right_second = jnp.concatenate([phi, phi, none, phi], axis=0)
    phi32 = phi.astype(F32)

    def quadratic(pieces):
        count = pieces[0].shape[0]
        result = None
        for part, piece in enumerate(pieces):
            flat = piece.reshape(count * 16, 128)
            lane = lax.broadcasted_iota(jnp.int32, flat.shape, 1)
            high = flat.astype(BF16).astype(F32)
            rest = flat - high
            middle = rest.astype(BF16).astype(F32)
            low = (rest - middle).astype(BF16)
            turned = pltpu.roll(middle, 64, 1)
            for side, right in enumerate((right_first, right_second)):
                front = jnp.where((lane < 64) == (side == 0), high, turned).astype(BF16)
                left = jnp.concatenate([front, low], axis=1)
                product = jnp.dot(left, right, preferred_element_type=F32).reshape(count, 16, cells)
                first = 32 * part + 16 * side
                term = jnp.sum(product * phi32[None, first : first + 16], axis=1)
                result = term if result is None else result + term
        return result

    group = 8
    for start in range(0, slots, group):
        found = cell_total / rows_total * quadratic([h[start : start + group] for h in halves])
        for slot in range(max(start, 2), start + group):
            maps_ref[pl.ds(order_ref[slot - 2], 1), :] = found[slot - start : slot - start + 1]

    both = [h[0] + h[1] for h in halves]
    sums = both[1][0:1, :64]
    low = both[1][1:2, :64]
    lane1 = lax.broadcasted_iota(jnp.int32, sums.shape, 1)
    sums = jnp.where(lane1 < 32, sums, jnp.concatenate([low[:, 32:], low[:, :32]], axis=1))
    average = sums / (2.0 * rows_total)
    outer = lax.dot_general(average, average, (((0,), (0,)), ((), ())), precision=HIGHEST, preferred_element_type=F32)
    lane = lax.broadcasted_iota(jnp.int32, both[0].shape, 1)
    column = jnp.where(lane < 64, lane, lane - 64)
    weight = jnp.where(column < 32, 1.0, 2.0)
    outer_upper = jnp.concatenate([outer[:16], outer[16:32]], axis=1)
    outer_lower = jnp.concatenate([outer[32:48], outer[48:]], axis=1)
    upper = (both[0] / (2.0 * rows_total) - outer_upper) * weight
    lower = jnp.where(column < 32, 0.0, both[1] / (2.0 * rows_total) - outer_lower)
    total = quadratic([upper[None], lower[None]])
    total_ref[...] = cell_total * total


def make_maps(rows_total, cell_total, half, order, mine, other, basis):
    cells = basis.shape[1]
    params = order.shape[0]

    def kernel(*refs):
        maps_kernel(rows_total, cell_total, *refs)

    return pl.pallas_call(
        kernel,
        in_specs=[SMEM, SMEM, VMEM, VMEM, VMEM],
        out_specs=(VMEM, VMEM),
        out_shape=(jax.ShapeDtypeStruct((params, cells), F32), jax.ShapeDtypeStruct((1, cells), F32)),
        name="maps",
    )(half, order, mine, other, basis)


def shifted(value, axis, size, shift):
    return lax.ppermute(value, axis, [(i, (i + shift) % size) for i in range(size)])


def on_device(fields, scales, pod_basis, param_order):
    rows, slots, cells = fields.shape
    blocks = scales.shape[2]
    modes = pod_basis.shape[1]
    sizes = {name: lax.axis_size(name) for name in ("grp", "z", "y", "core")}
    rows_total = float(rows * sizes["grp"])
    cell_total = float(cells * sizes["z"] * sizes["y"] * sizes["core"])
    core = lax.axis_index("core").astype(jnp.int32)
    slot = (lax.axis_index("z") * sizes["y"] + lax.axis_index("y")).astype(jnp.int32)
    by_slot = jnp.transpose(scales, (1, 2, 0)).reshape(slots * blocks, rows)
    basis = pod_basis.T
    packed = rows // 4

    theirs = project((1 - core)[None], fields, by_slot, basis)
    got = shifted(theirs, "core", 2, 1)
    ours = project(core[None], fields, by_slot, basis)
    halves = (ours + got).reshape(slots, packed, 2 * modes)

    parts = lax.all_to_all(halves, ("z", "y"), 0, 0, tiled=True)
    second = halves[1]
    second = second + sum(shifted(second, "y", sizes["y"], s) for s in range(1, sizes["y"]))
    second = jnp.broadcast_to(second[None], (sizes["z"], packed, 2 * modes))
    second = lax.all_to_all(second, "z", 0, 0, tiled=True)

    keep, send = moments(jnp.stack([slot, core]), parts, second)
    piece = keep + shifted(send, "core", 2, 1)
    piece = piece + sum(shifted(piece, "grp", sizes["grp"], s) for s in range(1, sizes["grp"]))
    copies = jnp.broadcast_to(piece[None], (slots,) + piece.shape)
    mine = lax.all_to_all(copies, ("z", "y"), 0, 0, tiled=True)
    other = shifted(mine, "core", 2, 1)
    sobol, total = make_maps(rows_total, cell_total, core[None], param_order, mine, other, basis)
    return sobol, total.reshape(cells)


def solution(mesh):
    split = Mesh(mesh.devices.reshape(4, 8, 4, 2), ("grp", "z", "y", "core"))
    cell = ("z", "y", "core")
    return jax.shard_map(
        on_device,
        mesh=split,
        in_specs=(P("grp", None, cell), P("grp", None, cell), P(cell, None), P()),
        out_specs=(P(None, cell), P(cell)),
        check_vma=False,
    )
```

time: 305 us -> 105 us (0.34)
  waiting for transfers between devices: 219 us -> 21.3 us
  local copies, waits for them, and re-layouts: 33.8 us -> 2.25 us
  Pallas kernels: 0 us -> 24.1 us
  starting transfers between devices: 0.08 us -> 22.2 us
  matrix products: 20 us -> 0 us
  blocking collectives: 14.3 us -> 30.2 us
  between operations: 14.2 us -> 0.67 us
    psum x2 -> x0, waiting for transfers between devices: 219 us -> none  [the longest x1 188 us: on_device(): coefficients = lax.psum(partial_modes, 'cell')]
    all_to_all x0 -> x2, blocking collectives: none -> 30.2 us  [the longest x1 16 us: on_device(): second = lax.all_to_all(second, 'z', 0, 0, tiled=True)]
    mul x2 -> x0, local copies, waits for them, and re-layouts: 26.5 us -> none  [project(): piece.astype(jnp.float32).reshape(rows, slots, blocks, cells // blocks)]
    pallas_call x0 -> x4, Pallas kernels: none -> 24.1 us  [the longest x2 17.9 us: project(): pl.pallas_call(project_kernel, grid_spec=grid_spec, out_shape=jax.ShapeDt...]
    dot_general x6 -> x0, matrix products: 20 us -> none  [the longest x1 10.5 us: project(): jnp.dot(flat, basis_piece, preferred_element_type=jnp.float32)]
    ppermute x0 -> x9, starting transfers between devices: none -> 18.3 us  [shifted(): lax.ppermute(value, axis, [(i, (i + shift) % size) for i in range(size)])]
    psum x1 -> x0, blocking collectives: 14.3 us -> none  [on_device(): cross, squares, column_sums = lax.psum((cross, squares, column_sums), 'grp')]
    all_to_all x0 -> x1, waiting for transfers between devices: none -> 12.8 us  [on_device(): parts = lax.all_to_all(halves, ('z', 'y'), 0, 0, tiled=True)]
  transfers between devices with their start and end apart: 2 -> 10, of which waited for: 2 -> 8; matrix products, arithmetic and copies ran while one was open for 1% -> 1% of each run, Pallas kernels for 0% -> 9%
where the time goes in v1:
time: 105 us
  blocking collectives  30.2 us (29%)
  Pallas kernels  24.1 us (23%)
  starting transfers between devices  22.2 us (21%)
  waiting for transfers between devices  21.3 us (20%)
  other arithmetic  3.96 us (4%)
  local copies, waits for them, and re-layouts  2.25 us (2%)
    ppermute x9, starting transfers between devices, shifted(): lax.ppermute(value, axis, [(i, (i + shift) % size) for i in range(size)])  18.3 us
    pallas_call x2, Pallas kernels, project(): pl.pallas_call(project_kernel, grid_spec=grid_spec, out_shape=jax.ShapeDt...  17.9 us
    all_to_all x1, blocking collectives, on_device(): second = lax.all_to_all(second, 'z', 0, 0, tiled=True)  16 us
    all_to_all x1, blocking collectives, on_device(): mine = lax.all_to_all(copies, ('z', 'y'), 0, 0, tiled=True)  14.2 us
    all_to_all x1, waiting for transfers between devices, on_device(): parts = lax.all_to_all(halves, ('z', 'y'), 0, 0, tiled=True)  12.8 us
    ppermute x9, waiting for transfers between devices, shifted(): lax.ppermute(value, axis, [(i, (i + shift) % size) for i in range(size)])  8.54 us
    pallas_call x1, Pallas kernels, make_maps(): pl.pallas_call(kernel, in_specs=[SMEM, SMEM, VMEM, VMEM, VMEM], out_specs...  4.08 us
    all_to_all x1, starting transfers between devices, on_device(): parts = lax.all_to_all(halves, ('z', 'y'), 0, 0, tiled=True)  3.89 us
  transfers between devices with their start and end apart: 10, of which 8 were waited for; matrix products, arithmetic and copies ran while one was open for 1% of the time, Pallas kernels for 9%

profile of v1, /device:TPU:1, one launch (start us, length us, event | category | flops | bytes accessed | tf_op | source)
XLA Modules:
  0.0 104.7 jit_solution(12859463290022076473)
XLA Ops:
  0.6 9.0 %project.3 = f32[1024,128]{1,0:T(8,128)} custom-call(s32[1]{0:T(128)} %bitcast.5.half_ref, bf16[128,32,1024]{2,1,0:T(8,128)(2,1)} %second_ref.3, bf16[128,32,1024]{2,1,0:T(8,128)(2,1)} %second_ref.3, f32[256,128]{1,0:T(8,128)} %bitcast.12, bf16[64,1024]{1,0:T(8,128)(2,1)} %bitcast.9), custom_call_target="tpu_custom_call" | custom-call | flops 268435456 | bytes 4194304 | tf_op jit(solution)/shard_map/project/pallas_call | solution.py:75
  9.6 3.2 %collective-permute-start = (f32[1024,128]{1,0:T(8,128)}, f32[1024,128]{1,0:T(8,128)S(1)}, u32[]{:S(2)}, u32[]{:S(2)}) collective-permute-start(f32[1024,128]{1,0:T(8,128)} %project.3), channel_id=1, source_target_pairs={{0,1},{1,0},{2,3},{3,2},{4,5},{5,4},{6,7},{7,6},{8,9},{9,8},{10,11... | collective-permute-start | bytes 1572872 | tf_op jit(solution)/shard_map/ppermute | solution.py:202
  12.8 8.9 %project.2 = f32[1024,128]{1,0:T(8,128)} custom-call(s32[1]{0:T(128)} %bitcast.half_ref.refs_0_, bf16[128,32,1024]{2,1,0:T(8,128)(2,1)} %second_ref.3, bf16[128,32,1024]{2,1,0:T(8,128)(2,1)} %second_ref.3, f32[256,128]{1,0:T(8,128)} %bitcast.13, bf16[64,1024]{1,0:T(8,128)(2,1)} %bitcast.10), custom_call_target="tpu_custom_call" | custom-call | flops 268435456 | bytes 4194304 | tf_op jit(solution)/shard_map/project/pallas_call | solution.py:75
  21.8 0.0 collective-permute-done
  21.8 1.9 %add.28 = f32[1024,128]{1,0:T(8,128)} add(f32[1024,128]{1,0:T(8,128)} %project.2, f32[1024,128]{1,0:T(8,128)S(1)} %collective-permute-done) | non-fusion elementwise | flops 131072 | bytes 1572864 | tf_op jit(solution)/shard_map/add | solution.py:221
  23.7 0.7 slice.5
  24.4 1.0 collective-permute-start.3
  25.4 0.4 collective-permute-start.2
  25.7 0.7 collective-permute-start.1
  26.4 0.6 collective-permute-done.3
  27.0 2.5 %collective-permute-done.2 = f32[32,128]{1,0:T(8,128)S(1)} collective-permute-done((f32[32,128]{1,0:T(8,128)S(1)}, f32[32,128]{1,0:T(8,128)S(1)}, u32[]{:S(2)}, u32[]{:S(2)}) %collective-permute-start.2) | collective-permute-done | bytes 16416 | tf_op jit(solution)/shard_map/ppermute | solution.py:202
  29.5 0.2 collective-permute-done.1
  29.6 0.7 add_add_fusion
  30.4 16.0 %all_to_all.15.second_ref = f32[8,32,128]{2,1,0:T(8,128)} all-to-all(f32[8,32,128]{2,1,0:T(8,128)S(1)} %broadcast_in_dim.10), channel_id=1, replica_groups=mesh['grp'=4,'z'=8,'y'=4,'core'=2] {'z'}, dimensions={0} | all-to-all | bytes 262144 | tf_op jit(solution)/shard_map/all_to_all | solution.py:227
  46.4 3.9 %all-to-all-start = ((f32[32,32,128]{2,1,0:T(8,128)}), f32[32,32,128]{2,1,0:T(8,128)S(1)}, u32[]{:S(2)}, u32[]{:S(2)}) async-start(f32[32,32,128]{2,1,0:T(8,128)} %bitcast.7), calls=%async_computation | async-start | bytes 1048576 | tf_op jit(solution)/shard_map/all_to_all | solution.py:223
  50.3 0.6 pad_add_fusion.where_ref
  51.0 12.8 %all-to-all-done.parts_ref = f32[32,32,128]{2,1,0:T(8,128)S(1)} async-done(((f32[32,32,128]{2,1,0:T(8,128)}), f32[32,32,128]{2,1,0:T(8,128)S(1)}, u32[]{:S(2)}, u32[]{:S(2)}) %all-to-all-start) | async-done | bytes 524320 | tf_op jit(solution)/shard_map/all_to_all | solution.py:223
  63.8 0.0 copy-start
  63.8 0.8 copy-done
  64.5 2.1 %moments.1 = (f32[16,128]{1,0:T(8,128)}, f32[16,128]{1,0:T(8,128)}) custom-call(s32[2]{0:T(128)} %pad_add_fusion.where_ref, f32[32,32,128]{2,1,0:T(8,128)} %copy-done, f32[8,32,128]{2,1,0:T(8,128)} %all_to_all.15.second_ref), custom_call_target="tpu_custom_call" | custom-call | tf_op jit(solution)/shard_map/moments/pallas_call | solution.py:113
  66.7 5.7 %collective-permute-start.4 = (f32[16,128]{1,0:T(8,128)}, f32[16,128]{1,0:T(8,128)S(1)}, u32[]{:S(2)}, u32[]{:S(2)}) collective-permute-start(f32[16,128]{1,0:T(8,128)} %get-tuple-element.7), channel_id=1, source_target_pairs={{0,1},{1,0},{2,3},{3,2},{4,5},{5,4},{6,7},{7,6},{8,9},{9,8},{10,11... | collective-permute-start | bytes 24584 | tf_op jit(solution)/shard_map/ppermute | solution.py:202
  72.3 1.0 collective-permute-done.4
  73.4 0.7 add.32
  74.1 2.5 %collective-permute-start.7 = (f32[16,128]{1,0:T(8,128)S(1)}, f32[16,128]{1,0:T(8,128)S(1)}, u32[]{:S(2)}, u32[]{:S(2)}) collective-permute-start(f32[16,128]{1,0:T(8,128)S(1)} %add.32), channel_id=1, source_target_pairs={{0,192},{64,0},{128,64},{192,128},{1,193},{65,1},{129,65},{193,129... | collective-permute-start | bytes 24584 | tf_op jit(solution)/shard_map/ppermute | solution.py:202
  76.5 0.5 collective-permute-start.6
  77.1 0.6 collective-permute-start.5
  77.7 0.0 collective-permute-done.7
  77.7 2.9 %collective-permute-done.6 = f32[16,128]{1,0:T(8,128)S(1)} collective-permute-done((f32[16,128]{1,0:T(8,128)S(1)}, f32[16,128]{1,0:T(8,128)S(1)}, u32[]{:S(2)}, u32[]{:S(2)}) %collective-permute-start.6) | collective-permute-done | bytes 8224 | tf_op jit(solution)/shard_map/ppermute | solution.py:202
  80.5 0.2 collective-permute-done.5
  80.8 14.2 %all_to_all.16.refs_2_ = f32[32,16,128]{2,1,0:T(8,128)S(1)} all-to-all(f32[32,16,128]{2,1,0:T(8,128)S(1)} %broadcast_in_dim.22), channel_id=1, replica_groups=mesh['grp'=4,'z'=8,'y'=4,'core'=2] {'z','y'}, dimensions={0} | all-to-all | bytes 524288 | tf_op jit(solution)/shard_map/all_to_all | solution.py:233
  95.0 0.0 copy-start.1
  95.0 3.8 %collective-permute-start.8 = (f32[32,16,128]{2,1,0:T(8,128)S(1)}, f32[32,16,128]{2,1,0:T(8,128)S(1)}, u32[]{:S(2)}, u32[]{:S(2)}) collective-permute-start(f32[32,16,128]{2,1,0:T(8,128)S(1)} %all_to_all.16.refs_2_), channel_id=1, source_target_pairs={{0,1},{1,0},{2,3},{3,2},{4,5},{5,4},{6,7},{7,6},{8,9},{9,8},{10,11... | collective-permute-start | bytes 786440 | tf_op jit(solution)/shard_map/ppermute | solution.py:202
  98.7 1.2 %collective-permute-done.8.refs_3_ = f32[32,16,128]{2,1,0:T(8,128)S(1)} collective-permute-done((f32[32,16,128]{2,1,0:T(8,128)S(1)}, f32[32,16,128]{2,1,0:T(8,128)S(1)}, u32[]{:S(2)}, u32[]{:S(2)}) %collective-permute-start.8) | collective-permute-done | bytes 262176 | tf_op jit(solution)/shard_map/ppermute | solution.py:202
  99.9 0.0 copy-done.1
  99.9 0.0 copy-start.2
  99.9 0.7 copy-done.2
  100.6 4.1 %maps.1 = (f32[30,1024]{1,0:T(8,128)}, f32[1,1024]{1,0:T(1,128)}) custom-call(s32[1]{0:T(128)} %bitcast.half_ref.refs_0_, s32[30]{0:T(128)} %refs_1_.1, f32[32,16,128]{2,1,0:T(8,128)} %copy-done.1, f32[32,16,128]{2,1,0:T(8,128)} %copy-done.2, bf16[64,1024]{1,0:T(8,128)(2,1)} %bitcast.11), custom_call_target="tpu_custom_call" | custom-call | tf_op jit(solution)/shard_map/maps/pallas_call | solution.py:192
  (3 shorter events, 0.0 us)
Async XLA Ops:
  9.6 12.2 %collective-permute-start = (f32[1024,128]{1,0:T(8,128)}, f32[1024,128]{1,0:T(8,128)S(1)}, u32[]{:S(2)}, u32[]{:S(2)}) collective-permute-start(f32[1024,128]{1,0:T(8,128)} %project.3), channel_id=1, source_target_pairs={{0,1},{1,0},{2,3},{3,2},{4,5},{5,4},{6,7},{7,6},{8,9},{9,8},{10,11... | collective-permute-start | bytes 1572872 | tf_op jit(solution)/shard_map/ppermute | solution.py:202
  24.4 2.6 %collective-permute-start.3 = (f32[32,128]{1,0:T(8,128)S(1)}, f32[32,128]{1,0:T(8,128)S(1)}, u32[]{:S(2)}, u32[]{:S(2)}) collective-permute-start(f32[32,128]{1,0:T(8,128)S(1)} %slice.5), channel_id=1, source_target_pairs={{0,6},{2,0},{4,2},{6,4},{1,7},{3,1},{5,3},{7,5},{8,14},{10,8},{12,... | collective-permute-start | bytes 49160 | tf_op jit(solution)/shard_map/ppermute | solution.py:202
  25.4 4.1 %collective-permute-start.2 = (f32[32,128]{1,0:T(8,128)S(1)}, f32[32,128]{1,0:T(8,128)S(1)}, u32[]{:S(2)}, u32[]{:S(2)}) collective-permute-start(f32[32,128]{1,0:T(8,128)S(1)} %slice.5), channel_id=1, source_target_pairs={{0,4},{2,6},{4,0},{6,2},{1,5},{3,7},{5,1},{7,3},{8,12},{10,14},{12... | collective-permute-start | bytes 49160 | tf_op jit(solution)/shard_map/ppermute | solution.py:202
  25.7 3.9 %collective-permute-start.1 = (f32[32,128]{1,0:T(8,128)S(1)}, f32[32,128]{1,0:T(8,128)S(1)}, u32[]{:S(2)}, u32[]{:S(2)}) collective-permute-start(f32[32,128]{1,0:T(8,128)S(1)} %slice.5), channel_id=1, source_target_pairs={{0,2},{2,4},{4,6},{6,0},{1,3},{3,5},{5,7},{7,1},{8,10},{10,12},{12... | collective-permute-start | bytes 49160 | tf_op jit(solution)/shard_map/ppermute | solution.py:202
  46.4 17.3 %all-to-all-start = ((f32[32,32,128]{2,1,0:T(8,128)}), f32[32,32,128]{2,1,0:T(8,128)S(1)}, u32[]{:S(2)}, u32[]{:S(2)}) async-start(f32[32,32,128]{2,1,0:T(8,128)} %bitcast.7), calls=%async_computation | async-start | bytes 1048576 | tf_op jit(solution)/shard_map/all_to_all | solution.py:223
  63.8 0.8 copy-start
  66.7 6.7 %collective-permute-start.4 = (f32[16,128]{1,0:T(8,128)}, f32[16,128]{1,0:T(8,128)S(1)}, u32[]{:S(2)}, u32[]{:S(2)}) collective-permute-start(f32[16,128]{1,0:T(8,128)} %get-tuple-element.7), channel_id=1, source_target_pairs={{0,1},{1,0},{2,3},{3,2},{4,5},{5,4},{6,7},{7,6},{8,9},{9,8},{10,11... | collective-permute-start | bytes 24584 | tf_op jit(solution)/shard_map/ppermute | solution.py:202
  74.1 3.6 %collective-permute-start.7 = (f32[16,128]{1,0:T(8,128)S(1)}, f32[16,128]{1,0:T(8,128)S(1)}, u32[]{:S(2)}, u32[]{:S(2)}) collective-permute-start(f32[16,128]{1,0:T(8,128)S(1)} %add.32), channel_id=1, source_target_pairs={{0,192},{64,0},{128,64},{192,128},{1,193},{65,1},{129,65},{193,129... | collective-permute-start | bytes 24584 | tf_op jit(solution)/shard_map/ppermute | solution.py:202
  76.5 4.0 %collective-permute-start.6 = (f32[16,128]{1,0:T(8,128)S(1)}, f32[16,128]{1,0:T(8,128)S(1)}, u32[]{:S(2)}, u32[]{:S(2)}) collective-permute-start(f32[16,128]{1,0:T(8,128)S(1)} %add.32), channel_id=1, source_target_pairs={{0,128},{64,192},{128,0},{192,64},{1,129},{65,193},{129,1},{193,65... | collective-permute-start | bytes 24584 | tf_op jit(solution)/shard_map/ppermute | solution.py:202
  77.1 3.7 %collective-permute-start.5 = (f32[16,128]{1,0:T(8,128)S(1)}, f32[16,128]{1,0:T(8,128)S(1)}, u32[]{:S(2)}, u32[]{:S(2)}) collective-permute-start(f32[16,128]{1,0:T(8,128)S(1)} %add.32), channel_id=1, source_target_pairs={{0,64},{64,128},{128,192},{192,0},{1,65},{65,129},{129,193},{193,1... | collective-permute-start | bytes 24584 | tf_op jit(solution)/shard_map/ppermute | solution.py:202
  95.0 4.9 %copy-start.1 = (f32[32,16,128]{2,1,0:T(8,128)}, f32[32,16,128]{2,1,0:T(8,128)S(1)}, u32[]{:S(2)}) copy-start(f32[32,16,128]{2,1,0:T(8,128)S(1)} %all_to_all.16.refs_2_) | copy-start | bytes 786436
  95.0 4.9 %collective-permute-start.8 = (f32[32,16,128]{2,1,0:T(8,128)S(1)}, f32[32,16,128]{2,1,0:T(8,128)S(1)}, u32[]{:S(2)}, u32[]{:S(2)}) collective-permute-start(f32[32,16,128]{2,1,0:T(8,128)S(1)} %all_to_all.16.refs_2_), channel_id=1, source_target_pairs={{0,1},{1,0},{2,3},{3,2},{4,5},{5,4},{6,7},{7,6},{8,9},{9,8},{10,11... | collective-permute-start | bytes 786440 | tf_op jit(solution)/shard_map/ppermute | solution.py:202
  99.9 0.7 copy-start.2

commit v2 on v1

--- a/solution.py
+++ b/solution.py
@@ -1,3 +1,5 @@
+import functools
+
 import jax
 import jax.numpy as jnp
 from jax import lax
@@ -12,75 +14,107 @@
 SMEM = pl.BlockSpec(memory_space=pltpu.SMEM)
 
 
-def project_kernel(half_ref, first_ref, second_ref, scale_ref, basis_ref, out_ref, by_block, dequant, weights):
-    step = pl.program_id(0)
-    rows, slots, cells = first_ref.shape
+def project_kernel(chunk, half_ref, fields_ref, scale_ref, basis_ref, out_ref, buffer, weights, spread, scales3, result, in_sems, out_sems):
+    rows, slots, cells = buffer.shape
+    packed = rows // 2
+    modes = basis_ref.shape[0]
     blocks = scale_ref.shape[0] // slots
     lanes = cells // blocks
-    modes = basis_ref.shape[0]
-    packed = out_ref.shape[0] // slots
-
-    @pl.when(step == 0)
-    def _():
-        for block in range(blocks):
-            by_block[block] = scale_ref[pl.ds(block, slots, stride=blocks), :]
-        turned = basis_ref[...].astype(F32).T.astype(BF16)
-        weights[...] = jnp.zeros_like(weights)
-        weights[:cells, :modes] = turned
-        weights[cells:, modes:] = turned
-
-    start = half_ref[0] * (2 * packed) + step * rows
-    turn = lax.rem(128 - start, 128)
+    chunks = packed // chunk
+    base = half_ref[0] * rows
+
+    def fetch(index, which):
+        first = which * packed + index * chunk
+        return pltpu.make_async_copy(
+            fields_ref.at[pl.ds(base + first, chunk)], buffer.at[pl.ds(first, chunk)], in_sems.at[index, which]
+        )
+
+    def put(index):
+        return pltpu.make_async_copy(
+            result.at[index], out_ref.at[:, pl.ds(index * chunk, chunk)], out_sems.at[index]
+        )
+
+    for index in range(chunks):
+        for which in range(2):
+            fetch(index, which).start()
+
+    turned = basis_ref[...].astype(F32).T.astype(BF16)
+    none = jnp.zeros_like(turned)
+    weights[0] = jnp.concatenate([turned, none], axis=1)
+    weights[1] = jnp.concatenate([none, turned], axis=1)
+    block_of_row = lax.broadcasted_iota(jnp.int32, (256, lanes), 0) % blocks
     for block in range(blocks):
-        rolled = pltpu.roll(by_block[block], turn, 1)
-        for which, source in enumerate((first_ref, second_ref)):
-            for row in range(rows):
-                lane = which * packed + row
-                scale = jnp.broadcast_to(rolled[:, lane : lane + 1], (slots, lanes))
-                piece = source[row, :, block * lanes : (block + 1) * lanes]
-                column = which * cells + block * lanes
-                dequant[row * slots : (row + 1) * slots, column : column + lanes] = (
-                    piece.astype(F32) * scale
-                ).astype(BF16)
-    modes_out = jnp.dot(dequant[...], weights[...], preferred_element_type=F32)
+        spread[:, block * lanes : (block + 1) * lanes] = jnp.where(block_of_row == block, 1.0, 0.0).astype(BF16)
+    by_row = scale_ref[...].T
+    high = by_row.astype(BF16).astype(F32)
+    rest = by_row - high
+    middle = rest.astype(BF16).astype(F32)
+    low = rest - middle
+    lane = lax.broadcasted_iota(jnp.int32, (by_row.shape[0], 128), 1)
+    for column in range(2):
+        cut = slice(column * 128, (column + 1) * 128)
+        turned_middle = pltpu.roll(middle[:, cut], 64, 1)
+        scales3[2 * column, :, :128] = jnp.where(lane < 64, high[:, cut], turned_middle)
+        scales3[2 * column, :, 128:] = low[:, cut]
+        scales3[2 * column + 1, :, :128] = jnp.where(lane < 64, turned_middle, high[:, cut])
+        scales3[2 * column + 1, :, 128:] = low[:, cut]
+
+    slot8 = lax.broadcasted_iota(jnp.int32, (8, 256), 0)
+    lane8 = lax.broadcasted_iota(jnp.int32, (8, 256), 1)
+    own = (lane8 % 64) // 8 == slot8
+    masks = (own & (lane8 < 192), own & ((lane8 < 128) | (lane8 >= 192)))
     slot = lax.broadcasted_iota(jnp.int32, (slots, 2 * modes), 0)
-    for row in range(rows):
-        tile = modes_out[row * slots : (row + 1) * slots]
-        tile = tile - jnp.where(slot >= 2, jnp.broadcast_to(tile[:1], tile.shape), 0.0)
-        out_ref[pl.ds(step * rows + row, slots, stride=packed), :] = tile
+    for index in range(chunks):
+        total = None
+        for which in range(2):
+            fetch(index, which).wait()
+            first = which * packed + index * chunk
+            left = []
+            for row in range(chunk):
+                for q in range(slots // 8):
+                    line = jnp.broadcast_to(scales3[q, pl.ds(base + first + row, 1), :], (8, 256))
+                    left.append(jnp.where(masks[q % 2], line, 0.0))
+            left = jnp.concatenate(left, axis=0).astype(BF16)
+            scale = jnp.dot(left, spread[...], preferred_element_type=F32)
+            piece = buffer[first : first + chunk].reshape(chunk * slots, cells)
+            dequant = (piece.astype(F32) * scale).astype(BF16)
+            part = jnp.dot(dequant, weights[which], preferred_element_type=F32)
+            total = part if total is None else total + part
+        for row in range(chunk):
+            tile = total[row * slots : (row + 1) * slots]
+            tile = tile - jnp.where(slot >= 2, jnp.broadcast_to(tile[:1], tile.shape), 0.0)
+            result[index, :, row, :] = tile
+        put(index).start()
+    for index in range(chunks):
+        put(index).wait()
 
 
 def project(half, fields, scales, basis):
     rows, slots, cells = fields.shape
     modes = basis.shape[0]
     packed = rows // 4
-    step = 8
-    steps = packed // step
-    grid_spec = pltpu.PrefetchScalarGridSpec(
-        num_scalar_prefetch=1,
-        grid=(steps,),
-        in_specs=[
-            pl.BlockSpec((step, slots, cells), lambda i, h: (h[0] * 2 * steps + i, 0, 0)),
-            pl.BlockSpec((step, slots, cells), lambda i, h: (h[0] * 2 * steps + steps + i, 0, 0)),
-            pl.BlockSpec(scales.shape, lambda i, h: (0, 0)),
-            pl.BlockSpec(basis.shape, lambda i, h: (0, 0)),
+    chunk = 8
+    chunks = packed // chunk
+    return pl.pallas_call(
+        functools.partial(project_kernel, chunk),
+        in_specs=[SMEM, pl.BlockSpec(memory_space=pltpu.HBM), VMEM, VMEM],
+        out_specs=pl.BlockSpec(memory_space=pl.ANY),
+        out_shape=jax.ShapeDtypeStruct((slots, packed, 2 * modes), F32),
+        scratch_shapes=[
+            pltpu.VMEM((rows // 2, slots, cells), BF16),
+            pltpu.VMEM((2, cells, 2 * modes), BF16),
+            pltpu.VMEM((256, cells), BF16),
+            pltpu.VMEM((slots // 8, rows, 256), F32),
+            pltpu.VMEM((chunks, slots, chunk, 2 * modes), F32),
+            pltpu.SemaphoreType.DMA((chunks, 2)),
+            pltpu.SemaphoreType.DMA((chunks,)),
         ],
-        out_specs=pl.BlockSpec((slots * packed, 2 * modes), lambda i, h: (0, 0)),
-        scratch_shapes=[
-            pltpu.VMEM((scales.shape[0] // slots, slots, rows), F32),
-            pltpu.VMEM((step * slots, 2 * cells), BF16),
-            pltpu.VMEM((2 * cells, 2 * modes), BF16),
-        ],
-    )
-    return pl.pallas_call(
-        project_kernel,
-        grid_spec=grid_spec,
-        out_shape=jax.ShapeDtypeStruct((slots * packed, 2 * modes), F32),
+        compiler_params=pltpu.CompilerParams(vmem_limit_bytes=32 << 20),
         cost_estimate=pl.CostEstimate(
             flops=rows * slots * cells * modes, bytes_accessed=rows * slots * cells, transcendentals=0
         ),
         name="project",
-    )(half, fields, fields, scales, basis)
+    )(half, fields, scales, basis)
 
 
 def moments_kernel(where_ref, parts_ref, second_ref, keep_ref, send_ref):
@@ -115,6 +149,8 @@
         in_specs=[SMEM, VMEM, VMEM],
         out_specs=(VMEM, VMEM),
         out_shape=(out, out),
+        compiler_params=pltpu.CompilerParams(vmem_limit_bytes=16 << 20),
+        cost_estimate=pl.CostEstimate(flops=1 << 22, bytes_accessed=1 << 20, transcendentals=0),
         name="moments",
     )(where, parts, second)
 
@@ -194,6 +230,8 @@
         in_specs=[SMEM, SMEM, VMEM, VMEM, VMEM],
         out_specs=(VMEM, VMEM),
         out_shape=(jax.ShapeDtypeStruct((params, cells), F32), jax.ShapeDtypeStruct((1, cells), F32)),
+        compiler_params=pltpu.CompilerParams(vmem_limit_bytes=32 << 20),
+        cost_estimate=pl.CostEstimate(flops=1 << 28, bytes_accessed=1 << 20, transcendentals=0),
         name="maps",
     )(half, order, mine, other, basis)
 
@@ -218,13 +256,13 @@
     theirs = project((1 - core)[None], fields, by_slot, basis)
     got = shifted(theirs, "core", 2, 1)
     ours = project(core[None], fields, by_slot, basis)
-    halves = (ours + got).reshape(slots, packed, 2 * modes)
+    halves = ours + got
 
     parts = lax.all_to_all(halves, ("z", "y"), 0, 0, tiled=True)
     second = halves[1]
     second = second + sum(shifted(second, "y", sizes["y"], s) for s in range(1, sizes["y"]))
-    second = jnp.broadcast_to(second[None], (sizes["z"], packed, 2 * modes))
-    second = lax.all_to_all(second, "z", 0, 0, tiled=True)
+    second = second + sum(shifted(second, "z", sizes["z"], s) for s in range(1, sizes["z"] // 2))
+    second = jnp.stack([second, shifted(second, "z", sizes["z"], sizes["z"] // 2)])
 
     keep, send = moments(jnp.stack([slot, core]), parts, second)
     piece = keep + shifted(send, "core", 2, 1)

time: 105 us -> 90.6 us (0.86)
  blocking collectives: 30.2 us -> 14.5 us
  starting transfers between devices: 22.2 us -> 34.7 us
  Pallas kernels: 24.1 us -> 14 us
  local copies, waits for them, and re-layouts: 2.25 us -> 5.94 us
  waiting for transfers between devices: 21.3 us -> 18.5 us
  other arithmetic: 3.96 us -> 1.7 us
    all_to_all x1 -> x0, blocking collectives: 16 us -> none  [on_device(): second = lax.all_to_all(second, 'z', 0, 0, tiled=True)]
    all_to_all x1, waiting for transfers between devices: 12.8 us -> 0.01 us  [on_device(): parts = lax.all_to_all(halves, ('z', 'y'), 0, 0, tiled=True)]
    ppermute x9 -> x13, waiting for transfers between devices: 8.54 us -> 18.5 us  [shifted(): lax.ppermute(value, axis, [(i, (i + shift) % size) for i in range(size)])]
    pallas_call x2, Pallas kernels: 17.9 us -> 9.45 us  [project(): pl.pallas_call(functools.partial(project_kernel, chunk), in_specs=[SMEM,...]
    ppermute x9 -> x13, starting transfers between devices: 18.3 us -> 25.2 us  [shifted(): lax.ppermute(value, axis, [(i, (i + shift) % size) for i in range(size)])]
    all_to_all x1, starting transfers between devices: 3.89 us -> 9.49 us  [on_device(): parts = lax.all_to_all(halves, ('z', 'y'), 0, 0, tiled=True)]
    unnamed x6 -> x12, local copies, waits for them, and re-layouts: 1.49 us -> 5.2 us
    pallas_call x1, Pallas kernels: 2.11 us -> 0.97 us  [moments(): pl.pallas_call(moments_kernel, in_specs=[SMEM, VMEM, VMEM], out_specs=(VM...]
  transfers between devices with their start and end apart: 10 -> 14, of which waited for: 8 -> 10; matrix products, arithmetic and copies ran while one was open for 1% -> 2% of each run, Pallas kernels for 9% -> 5%
where the time goes in v2:
time: 90.6 us; the launch traced here: 90.1 us
  starting transfers between devices  34.7 us (38%)
  waiting for transfers between devices  18.5 us (20%)
  blocking collectives  14.5 us (16%)
  Pallas kernels  14 us (15%)
  local copies, waits for them, and re-layouts  5.94 us (7%)
  other arithmetic  1.7 us (2%)
    ppermute x13, starting transfers between devices, shifted(): lax.ppermute(value, axis, [(i, (i + shift) % size) for i in range(size)])  25.2 us
    ppermute x13, waiting for transfers between devices, shifted(): lax.ppermute(value, axis, [(i, (i + shift) % size) for i in range(size)])  18.5 us
    all_to_all x1, blocking collectives, on_device(): mine = lax.all_to_all(copies, ('z', 'y'), 0, 0, tiled=True)  14.5 us
    all_to_all x1, starting transfers between devices, on_device(): parts = lax.all_to_all(halves, ('z', 'y'), 0, 0, tiled=True)  9.49 us
    pallas_call x2, Pallas kernels, project(): pl.pallas_call(functools.partial(project_kernel, chunk), in_specs=[SMEM,...  9.45 us
    unnamed x12, local copies, waits for them, and re-layouts  5.2 us
    pallas_call x1, Pallas kernels, make_maps(): pl.pallas_call(kernel, in_specs=[SMEM, SMEM, VMEM, VMEM, VMEM], out_specs...  3.58 us
  transfers between devices with their start and end apart: 14, of which 10 were waited for; matrix products, arithmetic and copies ran while one was open for 2% of the time, Pallas kernels for 5%

profile of v2, /device:TPU:1, one launch (start us, length us, event | category | flops | bytes accessed | tf_op | source)
XLA Modules:
  0.0 90.1 jit_solution(702746920807176150)
XLA Ops:
  0.6 0.0 copy-start
  0.6 3.4 %copy-done = bf16[128,32,1024]{2,1,0:T(8,128)(2,1)S(1)} copy-done((bf16[128,32,1024]{2,1,0:T(8,128)(2,1)S(1)}, bf16[128,32,1024]{2,1,0:T(8,128)(2,1)}, u32[]{:S(2)}) %copy-start) | copy-done | bytes 8388632
  4.0 0.0 copy-start.2
  4.0 0.9 %copy-done.2 = f32[128,32,8]{0,2,1:T(8,128)S(1)} copy-done((f32[128,32,8]{0,2,1:T(8,128)S(1)}, f32[128,32,8]{0,2,1:T(8,128)}, u32[]{:S(2)}) %copy-start.2) | copy-done | bytes 131096
  4.9 0.0 copy-start.3
  4.9 0.9 %copy-done.3 = bf16[1024,64]{0,1:T(8,128)(2,1)S(1)} copy-done((bf16[1024,64]{0,1:T(8,128)(2,1)S(1)}, bf16[1024,64]{0,1:T(8,128)(2,1)}, u32[]{:S(2)}) %copy-start.3) | copy-done | bytes 131096
  5.8 0.0 copy-start.1
  5.8 4.7 %project.3 = f32[32,32,128]{2,1,0:T(8,128)S(1)} custom-call(s32[1]{0:T(128)} %bitcast.5.half_ref, bf16[128,32,1024]{2,1,0:T(8,128)(2,1)S(1)} %copy-done, f32[256,128]{1,0:T(8,128)S(1)} %bitcast.14, bf16[64,1024]{1,0:T(8,128)(2,1)S(1)} %bitcast.16), custom_call_target="tpu_custom_call" | custom-call | flops 268435456 | bytes 4194304 | tf_op jit(solution)/shard_map/project/pallas_call | solution.py:98
  10.6 0.0 copy-start.4
  10.6 0.0 copy-start.5
  10.6 3.3 %collective-permute-start = (f32[32,32,128]{2,1,0:T(8,128)S(1)}, f32[32,32,128]{2,1,0:T(8,128)S(1)}, u32[]{:S(2)}, u32[]{:S(2)}) collective-permute-start(f32[32,32,128]{2,1,0:T(8,128)S(1)} %project.3), channel_id=1, source_target_pairs={{0,1},{1,0},{2,3},{3,2},{4,5},{5,4},{6,7},{7,6},{8,9},{9,8},{10,11... | collective-permute-start | bytes 1572872 | tf_op jit(solution)/shard_map/ppermute | solution.py:240
  13.9 0.0 copy-done.1
  13.9 4.7 %project.2 = f32[32,32,128]{2,1,0:T(8,128)S(1)} custom-call(s32[1]{0:T(128)} %bitcast.half_ref.refs_0_, bf16[128,32,1024]{2,1,0:T(8,128)(2,1)S(1)} %copy-done.1, f32[256,128]{1,0:T(8,128)S(1)} %bitcast.15, bf16[64,1024]{1,0:T(8,128)(2,1)S(1)} %bitcast.17), custom_call_target="tpu_custom_call" | custom-call | flops 268435456 | bytes 4194304 | tf_op jit(solution)/shard_map/project/pallas_call | solution.py:98
  18.6 0.0 collective-permute-done
  18.7 0.9 add.37
  19.5 9.5 %all-to-all-start = ((f32[32,32,128]{2,1,0:T(8,128)}), f32[32,32,128]{2,1,0:T(8,128)S(1)}, u32[]{:S(2)}, u32[]{:S(2)}) async-start(f32[32,32,128]{2,1,0:T(8,128)} %add.37), calls=%async_computation | async-start | bytes 1048576 | tf_op jit(solution)/shard_map/all_to_all | solution.py:261
  29.0 0.7 slice_bitcast_fusion
  29.8 2.4 %collective-permute-start.3 = (f32[32,128]{1,0:T(8,128)S(1)}, f32[32,128]{1,0:T(8,128)S(1)}, u32[]{:S(2)}, u32[]{:S(2)}) collective-permute-start(f32[32,128]{1,0:T(8,128)S(1)} %slice_bitcast_fusion), channel_id=1, source_target_pairs={{0,6},{2,0},{4,2},{6,4},{1,7},{3,1},{5,3},{7,5},{8,14},{10,8},{12,... | collective-permute-start | bytes 49160 | tf_op jit(solution)/shard_map/ppermute | solution.py:240
  32.2 0.6 collective-permute-start.2
  32.8 0.6 collective-permute-start.1
  33.4 0.0 collective-permute-done.3
  33.4 3.6 %collective-permute-done.2 = f32[32,128]{1,0:T(8,128)S(1)} collective-permute-done((f32[32,128]{1,0:T(8,128)S(1)}, f32[32,128]{1,0:T(8,128)S(1)}, u32[]{:S(2)}, u32[]{:S(2)}) %collective-permute-start.2) | collective-permute-done | bytes 16416 | tf_op jit(solution)/shard_map/ppermute | solution.py:240
  37.0 0.3 collective-permute-done.1
  37.2 0.7 add_add_fusion.1
  38.0 2.7 %collective-permute-start.6 = (f32[32,128]{1,0:T(8,128)S(1)}, f32[32,128]{1,0:T(8,128)S(1)}, u32[]{:S(2)}, u32[]{:S(2)}) collective-permute-start(f32[32,128]{1,0:T(8,128)S(1)} %add_add_fusion.1), channel_id=1, source_target_pairs={{0,24},{8,32},{16,40},{24,48},{32,56},{40,0},{48,8},{56,16},{1,25}... | collective-permute-start | bytes 49160 | tf_op jit(solution)/shard_map/ppermute | solution.py:240
  40.7 4.1 %collective-permute-start.5 = (f32[32,128]{1,0:T(8,128)S(1)}, f32[32,128]{1,0:T(8,128)S(1)}, u32[]{:S(2)}, u32[]{:S(2)}) collective-permute-start(f32[32,128]{1,0:T(8,128)S(1)} %add_add_fusion.1), channel_id=1, source_target_pairs={{0,16},{8,24},{16,32},{24,40},{32,48},{40,56},{48,0},{56,8},{1,17}... | collective-permute-start | bytes 49160 | tf_op jit(solution)/shard_map/ppermute | solution.py:240
  44.8 0.2 collective-permute-start.4
  45.0 0.2 collective-permute-done.6
  45.3 0.9 %collective-permute-done.5 = f32[32,128]{1,0:T(8,128)S(1)} collective-permute-done((f32[32,128]{1,0:T(8,128)S(1)}, f32[32,128]{1,0:T(8,128)S(1)}, u32[]{:S(2)}, u32[]{:S(2)}) %collective-permute-start.5) | collective-permute-done | bytes 16416 | tf_op jit(solution)/shard_map/ppermute | solution.py:240
  46.2 2.6 %collective-permute-done.4 = f32[32,128]{1,0:T(8,128)S(1)} collective-permute-done((f32[32,128]{1,0:T(8,128)S(1)}, f32[32,128]{1,0:T(8,128)S(1)}, u32[]{:S(2)}, u32[]{:S(2)}) %collective-permute-start.4) | collective-permute-done | bytes 16416 | tf_op jit(solution)/shard_map/ppermute | solution.py:240
  48.8 0.7 collective-permute-start.7
  49.5 0.1 pad_add_fusion.where_ref
  49.6 5.8 %collective-permute-done.7 = f32[32,128]{1,0:T(8,128)S(1)} collective-permute-done((f32[32,128]{1,0:T(8,128)S(1)}, f32[32,128]{1,0:T(8,128)S(1)}, u32[]{:S(2)}, u32[]{:S(2)}) %collective-permute-start.7) | collective-permute-done | bytes 16416 | tf_op jit(solution)/shard_map/ppermute | solution.py:240
  55.4 0.0 all-to-all-done.parts_ref
  55.4 1.0 %moments.1 = (f32[16,128]{1,0:T(8,128)S(1)}, f32[16,128]{1,0:T(8,128)S(1)}) custom-call(s32[2]{0:T(128)S(1)} %pad_add_fusion.where_ref, f32[32,32,128]{2,1,0:T(8,128)S(1)} %all-to-all-done.parts_ref, f32[2,32,128]{2,1,0:T(8,128)S(1)} %pad_maximum_fusion.second_ref), custom_call_target="tpu_custom_call" | custom-call | flops 4194304 | bytes 1048576 | tf_op jit(solution)/shard_map/moments/pallas_call | solution.py:147
  56.3 3.1 %collective-permute-start.8 = (f32[16,128]{1,0:T(8,128)S(1)}, f32[16,128]{1,0:T(8,128)S(1)}, u32[]{:S(2)}, u32[]{:S(2)}) collective-permute-start(f32[16,128]{1,0:T(8,128)S(1)} %get-tuple-element.7), channel_id=1, source_target_pairs={{0,1},{1,0},{2,3},{3,2},{4,5},{5,4},{6,7},{7,6},{8,9},{9,8},{10,11... | collective-permute-start | bytes 24584 | tf_op jit(solution)/shard_map/ppermute | solution.py:240
  59.5 0.8 collective-permute-done.8
  60.3 2.5 %collective-permute-start.11 = (f32[16,128]{1,0:T(8,128)S(1)}, f32[16,128]{1,0:T(8,128)S(1)}, u32[]{:S(2)}, u32[]{:S(2)}) collective-permute-start(f32[16,128]{1,0:T(8,128)S(1)} %add.44), channel_id=1, source_target_pairs={{0,192},{64,0},{128,64},{192,128},{1,193},{65,1},{129,65},{193,129... | collective-permute-start | bytes 24584 | tf_op jit(solution)/shard_map/ppermute | solution.py:240
  62.8 0.5 collective-permute-start.10
  63.3 0.6 collective-permute-start.9
  63.9 0.0 collective-permute-done.11
  63.9 2.9 %collective-permute-done.10 = f32[16,128]{1,0:T(8,128)S(1)} collective-permute-done((f32[16,128]{1,0:T(8,128)S(1)}, f32[16,128]{1,0:T(8,128)S(1)}, u32[]{:S(2)}, u32[]{:S(2)}) %collective-permute-start.10) | collective-permute-done | bytes 8224 | tf_op jit(solution)/shard_map/ppermute | solution.py:240
  66.8 0.2 collective-permute-done.9
  67.1 14.5 %all_to_all.10.refs_2_ = f32[32,16,128]{2,1,0:T(8,128)S(1)} all-to-all(f32[32,16,128]{2,1,0:T(8,128)S(1)} %broadcast_in_dim.15), channel_id=1, replica_groups=mesh['grp'=4,'z'=8,'y'=4,'core'=2] {'z','y'}, dimensions={0} | all-to-all | bytes 524288 | tf_op jit(solution)/shard_map/all_to_all | solution.py:271
  81.6 3.8 %collective-permute-start.12 = (f32[32,16,128]{2,1,0:T(8,128)S(1)}, f32[32,16,128]{2,1,0:T(8,128)S(1)}, u32[]{:S(2)}, u32[]{:S(2)}) collective-permute-start(f32[32,16,128]{2,1,0:T(8,128)S(1)} %all_to_all.10.refs_2_), channel_id=1, source_target_pairs={{0,1},{1,0},{2,3},{3,2},{4,5},{5,4},{6,7},{7,6},{8,9},{9,8},{10,11... | collective-permute-start | bytes 786440 | tf_op jit(solution)/shard_map/ppermute | solution.py:240
  85.4 1.2 %collective-permute-done.12.refs_3_ = f32[32,16,128]{2,1,0:T(8,128)S(1)} collective-permute-done((f32[32,16,128]{2,1,0:T(8,128)S(1)}, f32[32,16,128]{2,1,0:T(8,128)S(1)}, u32[]{:S(2)}, u32[]{:S(2)}) %collective-permute-start.12) | collective-permute-done | bytes 262176 | tf_op jit(solution)/shard_map/ppermute | solution.py:240
  86.5 0.0 copy-done.4
  86.5 0.0 copy-done.5
  86.5 3.6 %maps.1 = (f32[30,1024]{1,0:T(8,128)}, f32[1,1024]{1,0:T(1,128)}) custom-call(s32[1]{0:T(128)} %bitcast.half_ref.refs_0_, s32[30]{0:T(128)S(1)} %copy-done.5, f32[32,16,128]{2,1,0:T(8,128)S(1)} %all_to_all.10.refs_2_, f32[32,16,128]{2,1,0:T(8,128)S(1)} %collective-permute-done.12.refs_3_, bf16[64,1024]{1,0:T(8,128)(2,1)S(1)} %bitcast.18), custom_call_target="tpu_custom_call" | custom-call | flops 268435456 | bytes 1048576 | tf_op jit(solution)/shard_map/maps/pallas_call | solution.py:228
  (5 shorter events, 0.0 us)
Async XLA Ops:
  0.6 3.4 %copy-start = (bf16[128,32,1024]{2,1,0:T(8,128)(2,1)S(1)}, bf16[128,32,1024]{2,1,0:T(8,128)(2,1)}, u32[]{:S(2)}) copy-start(bf16[128,32,1024]{2,1,0:T(8,128)(2,1)} %fields_ref.3) | copy-start | bytes 25165828
  4.0 0.9 %copy-start.2 = (f32[128,32,8]{0,2,1:T(8,128)S(1)}, f32[128,32,8]{0,2,1:T(8,128)}, u32[]{:S(2)}) copy-start(f32[128,32,8]{0,2,1:T(8,128)} %param.5) | copy-start | bytes 393220
  4.9 0.9 %copy-start.3 = (bf16[1024,64]{0,1:T(8,128)(2,1)S(1)}, bf16[1024,64]{0,1:T(8,128)(2,1)}, u32[]{:S(2)}) copy-start(bf16[1024,64]{0,1:T(8,128)(2,1)} %param.6) | copy-start | bytes 393220
  5.8 8.1 %copy-start.1 = (bf16[128,32,1024]{2,1,0:T(8,128)(2,1)S(1)}, bf16[128,32,1024]{2,1,0:T(8,128)(2,1)}, u32[]{:S(2)}) copy-start(bf16[128,32,1024]{2,1,0:T(8,128)(2,1)} %fields_ref.3) | copy-start | bytes 25165828
  10.6 76.0 %copy-start.4 = (bf16[1024,64]{0,1:T(8,128)(2,1)S(1)}, bf16[1024,64]{0,1:T(8,128)(2,1)}, u32[]{:S(2)}) copy-start(bf16[1024,64]{0,1:T(8,128)(2,1)} %param.6) | copy-start | bytes 393220
  10.6 76.0 %copy-start.5 = (s32[30]{0:T(128)S(1)}, s32[30]{0:T(128)}, u32[]{:S(2)}) copy-start(s32[30]{0:T(128)} %refs_1_.1) | copy-start | bytes 364
  10.6 8.1 %collective-permute-start = (f32[32,32,128]{2,1,0:T(8,128)S(1)}, f32[32,32,128]{2,1,0:T(8,128)S(1)}, u32[]{:S(2)}, u32[]{:S(2)}) collective-permute-start(f32[32,32,128]{2,1,0:T(8,128)S(1)} %project.3), channel_id=1, source_target_pairs={{0,1},{1,0},{2,3},{3,2},{4,5},{5,4},{6,7},{7,6},{8,9},{9,8},{10,11... | collective-permute-start | bytes 1572872 | tf_op jit(solution)/shard_map/ppermute | solution.py:240
  19.5 35.8 %all-to-all-start = ((f32[32,32,128]{2,1,0:T(8,128)}), f32[32,32,128]{2,1,0:T(8,128)S(1)}, u32[]{:S(2)}, u32[]{:S(2)}) async-start(f32[32,32,128]{2,1,0:T(8,128)} %add.37), calls=%async_computation | async-start | bytes 1048576 | tf_op jit(solution)/shard_map/all_to_all | solution.py:261
  29.8 3.6 %collective-permute-start.3 = (f32[32,128]{1,0:T(8,128)S(1)}, f32[32,128]{1,0:T(8,128)S(1)}, u32[]{:S(2)}, u32[]{:S(2)}) collective-permute-start(f32[32,128]{1,0:T(8,128)S(1)} %slice_bitcast_fusion), channel_id=1, source_target_pairs={{0,6},{2,0},{4,2},{6,4},{1,7},{3,1},{5,3},{7,5},{8,14},{10,8},{12,... | collective-permute-start | bytes 49160 | tf_op jit(solution)/shard_map/ppermute | solution.py:240
  32.2 4.8 %collective-permute-start.2 = (f32[32,128]{1,0:T(8,128)S(1)}, f32[32,128]{1,0:T(8,128)S(1)}, u32[]{:S(2)}, u32[]{:S(2)}) collective-permute-start(f32[32,128]{1,0:T(8,128)S(1)} %slice_bitcast_fusion), channel_id=1, source_target_pairs={{0,4},{2,6},{4,0},{6,2},{1,5},{3,7},{5,1},{7,3},{8,12},{10,14},{12... | collective-permute-start | bytes 49160 | tf_op jit(solution)/shard_map/ppermute | solution.py:240
  32.8 4.5 %collective-permute-start.1 = (f32[32,128]{1,0:T(8,128)S(1)}, f32[32,128]{1,0:T(8,128)S(1)}, u32[]{:S(2)}, u32[]{:S(2)}) collective-permute-start(f32[32,128]{1,0:T(8,128)S(1)} %slice_bitcast_fusion), channel_id=1, source_target_pairs={{0,2},{2,4},{4,6},{6,0},{1,3},{3,5},{5,7},{7,1},{8,10},{10,12},{12... | collective-permute-start | bytes 49160 | tf_op jit(solution)/shard_map/ppermute | solution.py:240
  38.0 7.3 %collective-permute-start.6 = (f32[32,128]{1,0:T(8,128)S(1)}, f32[32,128]{1,0:T(8,128)S(1)}, u32[]{:S(2)}, u32[]{:S(2)}) collective-permute-start(f32[32,128]{1,0:T(8,128)S(1)} %add_add_fusion.1), channel_id=1, source_target_pairs={{0,24},{8,32},{16,40},{24,48},{32,56},{40,0},{48,8},{56,16},{1,25}... | collective-permute-start | bytes 49160 | tf_op jit(solution)/shard_map/ppermute | solution.py:240
  40.7 5.5 %collective-permute-start.5 = (f32[32,128]{1,0:T(8,128)S(1)}, f32[32,128]{1,0:T(8,128)S(1)}, u32[]{:S(2)}, u32[]{:S(2)}) collective-permute-start(f32[32,128]{1,0:T(8,128)S(1)} %add_add_fusion.1), channel_id=1, source_target_pairs={{0,16},{8,24},{16,32},{24,40},{32,48},{40,56},{48,0},{56,8},{1,17}... | collective-permute-start | bytes 49160 | tf_op jit(solution)/shard_map/ppermute | solution.py:240
  44.8 4.0 %collective-permute-start.4 = (f32[32,128]{1,0:T(8,128)S(1)}, f32[32,128]{1,0:T(8,128)S(1)}, u32[]{:S(2)}, u32[]{:S(2)}) collective-permute-start(f32[32,128]{1,0:T(8,128)S(1)} %add_add_fusion.1), channel_id=1, source_target_pairs={{0,8},{8,16},{16,24},{24,32},{32,40},{40,48},{48,56},{56,0},{1,9},... | collective-permute-start | bytes 49160 | tf_op jit(solution)/shard_map/ppermute | solution.py:240
  48.8 6.6 %collective-permute-start.7 = (f32[32,128]{1,0:T(8,128)S(1)}, f32[32,128]{1,0:T(8,128)S(1)}, u32[]{:S(2)}, u32[]{:S(2)}) collective-permute-start(f32[32,128]{1,0:T(8,128)S(1)} %add_add_fusion), channel_id=1, source_target_pairs={{0,32},{8,40},{16,48},{24,56},{32,0},{40,8},{48,16},{56,24},{1,33}... | collective-permute-start | bytes 49160 | tf_op jit(solution)/shard_map/ppermute | solution.py:240
  56.3 4.0 %collective-permute-start.8 = (f32[16,128]{1,0:T(8,128)S(1)}, f32[16,128]{1,0:T(8,128)S(1)}, u32[]{:S(2)}, u32[]{:S(2)}) collective-permute-start(f32[16,128]{1,0:T(8,128)S(1)} %get-tuple-element.7), channel_id=1, source_target_pairs={{0,1},{1,0},{2,3},{3,2},{4,5},{5,4},{6,7},{7,6},{8,9},{9,8},{10,11... | collective-permute-start | bytes 24584 | tf_op jit(solution)/shard_map/ppermute | solution.py:240
  60.3 3.6 %collective-permute-start.11 = (f32[16,128]{1,0:T(8,128)S(1)}, f32[16,128]{1,0:T(8,128)S(1)}, u32[]{:S(2)}, u32[]{:S(2)}) collective-permute-start(f32[16,128]{1,0:T(8,128)S(1)} %add.44), channel_id=1, source_target_pairs={{0,192},{64,0},{128,64},{192,128},{1,193},{65,1},{129,65},{193,129... | collective-permute-start | bytes 24584 | tf_op jit(solution)/shard_map/ppermute | solution.py:240
  62.8 4.0 %collective-permute-start.10 = (f32[16,128]{1,0:T(8,128)S(1)}, f32[16,128]{1,0:T(8,128)S(1)}, u32[]{:S(2)}, u32[]{:S(2)}) collective-permute-start(f32[16,128]{1,0:T(8,128)S(1)} %add.44), channel_id=1, source_target_pairs={{0,128},{64,192},{128,0},{192,64},{1,129},{65,193},{129,1},{193,65... | collective-permute-start | bytes 24584 | tf_op jit(solution)/shard_map/ppermute | solution.py:240
  63.3 3.7 %collective-permute-start.9 = (f32[16,128]{1,0:T(8,128)S(1)}, f32[16,128]{1,0:T(8,128)S(1)}, u32[]{:S(2)}, u32[]{:S(2)}) collective-permute-start(f32[16,128]{1,0:T(8,128)S(1)} %add.44), channel_id=1, source_target_pairs={{0,64},{64,128},{128,192},{192,0},{1,65},{65,129},{129,193},{193,1... | collective-permute-start | bytes 24584 | tf_op jit(solution)/shard_map/ppermute | solution.py:240
  81.6 4.9 %collective-permute-start.12 = (f32[32,16,128]{2,1,0:T(8,128)S(1)}, f32[32,16,128]{2,1,0:T(8,128)S(1)}, u32[]{:S(2)}, u32[]{:S(2)}) collective-permute-start(f32[32,16,128]{2,1,0:T(8,128)S(1)} %all_to_all.10.refs_2_), channel_id=1, source_target_pairs={{0,1},{1,0},{2,3},{3,2},{4,5},{5,4},{6,7},{7,6},{8,9},{9,8},{10,11... | collective-permute-start | bytes 786440 | tf_op jit(solution)/shard_map/ppermute | solution.py:240

commit v3 on v2

--- a/solution.py
+++ b/solution.py
@@ -14,29 +14,35 @@
 SMEM = pl.BlockSpec(memory_space=pltpu.SMEM)
 
 
-def project_kernel(chunk, half_ref, fields_ref, scale_ref, basis_ref, out_ref, buffer, weights, spread, scales3, result, in_sems, out_sems):
-    rows, slots, cells = buffer.shape
+def project_kernel(chunk, first_slot, halves, *refs):
+    half_ref, fields_ref, scale_ref, basis_ref = refs[:4]
+    refs = refs[4:]
+    base_ref = None
+    if first_slot:
+        base_ref, refs = refs[0], refs[1:]
+    outs, refs = refs[:halves], refs[halves:]
+    buffer, weights, spread, scales3, sems = refs
+    _, rows, slots, cells = buffer.shape
     packed = rows // 2
     modes = basis_ref.shape[0]
-    blocks = scale_ref.shape[0] // slots
-    lanes = cells // blocks
+    lanes = 128
+    blocks = cells // lanes
     chunks = packed // chunk
-    base = half_ref[0] * rows
-
-    def fetch(index, which):
+    groups = slots // 8
+    bases = [(half_ref[0] if i == 0 else 1 - half_ref[0]) * rows for i in range(halves)]
+
+    def fetch(part, index, which):
         first = which * packed + index * chunk
         return pltpu.make_async_copy(
-            fields_ref.at[pl.ds(base + first, chunk)], buffer.at[pl.ds(first, chunk)], in_sems.at[index, which]
+            fields_ref.at[pl.ds(bases[part] + first, chunk), first_slot : first_slot + slots],
+            buffer.at[part, pl.ds(first, chunk)],
+            sems.at[part, index, which],
         )
 
-    def put(index):
-        return pltpu.make_async_copy(
-            result.at[index], out_ref.at[:, pl.ds(index * chunk, chunk)], out_sems.at[index]
-        )
-
-    for index in range(chunks):
-        for which in range(2):
-            fetch(index, which).start()
+    for part in range(halves):
+        for index in range(chunks):
+            for which in range(2):
+                fetch(part, index, which).start()
 
     turned = basis_ref[...].astype(F32).T.astype(BF16)
     none = jnp.zeros_like(turned)
@@ -51,70 +57,76 @@
     middle = rest.astype(BF16).astype(F32)
     low = rest - middle
     lane = lax.broadcasted_iota(jnp.int32, (by_row.shape[0], 128), 1)
-    for column in range(2):
-        cut = slice(column * 128, (column + 1) * 128)
+    group_of = [first_slot // 8 + g for g in range(groups)]
+    for g, q in enumerate(group_of):
+        cut = slice(q // 2 * 128, q // 2 * 128 + 128)
         turned_middle = pltpu.roll(middle[:, cut], 64, 1)
-        scales3[2 * column, :, :128] = jnp.where(lane < 64, high[:, cut], turned_middle)
-        scales3[2 * column, :, 128:] = low[:, cut]
-        scales3[2 * column + 1, :, :128] = jnp.where(lane < 64, turned_middle, high[:, cut])
-        scales3[2 * column + 1, :, 128:] = low[:, cut]
+        if q % 2 == 0:
+            scales3[g, :, :128] = jnp.where(lane < 64, high[:, cut], turned_middle)
+        else:
+            scales3[g, :, :128] = jnp.where(lane < 64, turned_middle, high[:, cut])
+        scales3[g, :, 128:] = low[:, cut]
 
     slot8 = lax.broadcasted_iota(jnp.int32, (8, 256), 0)
     lane8 = lax.broadcasted_iota(jnp.int32, (8, 256), 1)
     own = (lane8 % 64) // 8 == slot8
     masks = (own & (lane8 < 192), own & ((lane8 < 128) | (lane8 >= 192)))
     slot = lax.broadcasted_iota(jnp.int32, (slots, 2 * modes), 0)
-    for index in range(chunks):
-        total = None
-        for which in range(2):
-            fetch(index, which).wait()
-            first = which * packed + index * chunk
-            left = []
+    for part in range(halves):
+        for index in range(chunks):
+            total = None
+            for which in range(2):
+                fetch(part, index, which).wait()
+                first = which * packed + index * chunk
+                left = []
+                for row in range(chunk):
+                    for g, q in enumerate(group_of):
+                        line = jnp.broadcast_to(scales3[g, pl.ds(bases[part] + first + row, 1), :], (8, 256))
+                        left.append(jnp.where(masks[q % 2], line, 0.0))
+                left = jnp.concatenate(left, axis=0).astype(BF16)
+                scale = jnp.dot(left, spread[...], preferred_element_type=F32)
+                piece = buffer[part, first : first + chunk].astype(F32).reshape(chunk * slots, cells)
+                dequant = (piece * scale).astype(BF16)
+                product = jnp.dot(dequant, weights[which], preferred_element_type=F32)
+                total = product if total is None else total + product
+            tiles = []
             for row in range(chunk):
-                for q in range(slots // 8):
-                    line = jnp.broadcast_to(scales3[q, pl.ds(base + first + row, 1), :], (8, 256))
-                    left.append(jnp.where(masks[q % 2], line, 0.0))
-            left = jnp.concatenate(left, axis=0).astype(BF16)
-            scale = jnp.dot(left, spread[...], preferred_element_type=F32)
-            piece = buffer[first : first + chunk].reshape(chunk * slots, cells)
-            dequant = (piece.astype(F32) * scale).astype(BF16)
-            part = jnp.dot(dequant, weights[which], preferred_element_type=F32)
-            total = part if total is None else total + part
-        for row in range(chunk):
-            tile = total[row * slots : (row + 1) * slots]
-            tile = tile - jnp.where(slot >= 2, jnp.broadcast_to(tile[:1], tile.shape), 0.0)
-            result[index, :, row, :] = tile
-        put(index).start()
-    for index in range(chunks):
-        put(index).wait()
-
-
-def project(half, fields, scales, basis):
+                tile = total[row * slots : (row + 1) * slots]
+                if base_ref is None:
+                    tile = tile - jnp.where(slot >= 2, jnp.broadcast_to(tile[:1], tile.shape), 0.0)
+                else:
+                    line = base_ref[0, index * chunk + row : index * chunk + row + 1, :]
+                    tile = tile - jnp.broadcast_to(line, tile.shape)
+                tiles.append(tile)
+            outs[part][:, index * chunk : (index + 1) * chunk, :] = jnp.swapaxes(jnp.stack(tiles), 0, 1)
+
+def project(half, fields, scales, basis, base=None):
     rows, slots, cells = fields.shape
     modes = basis.shape[0]
     packed = rows // 4
-    chunk = 8
+    first_slot, count, halves = (0, 8, 2) if base is None else (8, slots - 8, 1)
+    chunk = 16 if base is None else 8
     chunks = packed // chunk
+    out = jax.ShapeDtypeStruct((count, packed, 2 * modes), F32)
+    extra = [] if base is None else [base]
     return pl.pallas_call(
-        functools.partial(project_kernel, chunk),
-        in_specs=[SMEM, pl.BlockSpec(memory_space=pltpu.HBM), VMEM, VMEM],
-        out_specs=pl.BlockSpec(memory_space=pl.ANY),
-        out_shape=jax.ShapeDtypeStruct((slots, packed, 2 * modes), F32),
+        functools.partial(project_kernel, chunk, first_slot, halves),
+        in_specs=[SMEM, pl.BlockSpec(memory_space=pl.ANY), VMEM, VMEM] + [VMEM] * len(extra),
+        out_specs=[VMEM] * halves,
+        out_shape=[out] * halves,
         scratch_shapes=[
-            pltpu.VMEM((rows // 2, slots, cells), BF16),
+            pltpu.VMEM((halves, rows // 2, count, cells), BF16),
             pltpu.VMEM((2, cells, 2 * modes), BF16),
             pltpu.VMEM((256, cells), BF16),
-            pltpu.VMEM((slots // 8, rows, 256), F32),
-            pltpu.VMEM((chunks, slots, chunk, 2 * modes), F32),
-            pltpu.SemaphoreType.DMA((chunks, 2)),
-            pltpu.SemaphoreType.DMA((chunks,)),
+            pltpu.VMEM((count // 8, rows, 256), F32),
+            pltpu.SemaphoreType.DMA((halves, chunks, 2)),
         ],
-        compiler_params=pltpu.CompilerParams(vmem_limit_bytes=32 << 20),
+        compiler_params=pltpu.CompilerParams(vmem_limit_bytes=52 << 20),
         cost_estimate=pl.CostEstimate(
-            flops=rows * slots * cells * modes, bytes_accessed=rows * slots * cells, transcendentals=0
+            flops=halves * rows * count * cells * modes, bytes_accessed=halves * rows * count * cells, transcendentals=0
         ),
-        name="project",
-    )(half, fields, scales, basis)
+        name="first" if base is None else "rest",
+    )(half, fields, scales, basis, *extra)
 
 
 def moments_kernel(where_ref, parts_ref, second_ref, keep_ref, send_ref):
@@ -253,14 +265,16 @@
     basis = pod_basis.T
     packed = rows // 4
 
-    theirs = project((1 - core)[None], fields, by_slot, basis)
-    got = shifted(theirs, "core", 2, 1)
-    ours = project(core[None], fields, by_slot, basis)
-    halves = ours + got
-
+    theirs_first, ours_first = project((1 - core)[None], fields, by_slot, basis)
+    near_first = ours_first + shifted(theirs_first, "core", 2, 1)
+    (theirs_rest,) = project((1 - core)[None], fields, by_slot, basis, theirs_first)
+    second = near_first[1]
+    second = second + sum(shifted(second, "y", sizes["y"], s) for s in range(1, sizes["y"]))
+    got_rest = shifted(theirs_rest, "core", 2, 1)
+    (ours_rest,) = project(core[None], fields, by_slot, basis, ours_first)
+    halves = jnp.concatenate([near_first, ours_rest + got_rest], axis=0)
+    halves, second = lax.optimization_barrier((halves, second))
     parts = lax.all_to_all(halves, ("z", "y"), 0, 0, tiled=True)
-    second = halves[1]
-    second = second + sum(shifted(second, "y", sizes["y"], s) for s in range(1, sizes["y"]))
     second = second + sum(shifted(second, "z", sizes["z"], s) for s in range(1, sizes["z"] // 2))
     second = jnp.stack([second, shifted(second, "z", sizes["z"], sizes["z"] // 2)])
 

time: 90.6 us -> 92.2 us (1.018)
  local copies, waits for them, and re-layouts: 5.94 us -> 1.84 us
  starting transfers between devices: 34.7 us -> 38.5 us
  Pallas kernels: 14 us -> 17.5 us
  waiting for transfers between devices: 18.5 us -> 15.2 us
  blocking collectives: 14.5 us -> 17 us
    pallas_call x2 -> x3, Pallas kernels: 9.45 us -> 12.9 us  [project(): pl.pallas_call(functools.partial(project_kernel, chunk, first_slot, halve...]
    unnamed x12 -> x10, local copies, waits for them, and re-layouts: 5.2 us -> 1.81 us
    ppermute x13 -> x14, waiting for transfers between devices: 18.5 us -> 15.2 us  [shifted(): lax.ppermute(value, axis, [(i, (i + shift) % size) for i in range(size)])]
    ppermute x13 -> x14, starting transfers between devices: 25.2 us -> 28.3 us  [shifted(): lax.ppermute(value, axis, [(i, (i + shift) % size) for i in range(size)])]
    all_to_all x1, blocking collectives: 14.5 us -> 17 us  [on_device(): mine = lax.all_to_all(copies, ('z', 'y'), 0, 0, tiled=True)]
  transfers between devices with their start and end apart: 14 -> 15, of which waited for: 10 -> 7; matrix products, arithmetic and copies ran while one was open for 2% -> 0% of each run, Pallas kernels for 5% -> 10%
where the time goes in v3:
time: 92.2 us; the launch traced here: 91.9 us
  starting transfers between devices  38.5 us (42%)
  Pallas kernels  17.5 us (19%)
  blocking collectives  17 us (18%)
  waiting for transfers between devices  15.2 us (16%)
  local copies, waits for them, and re-layouts  1.84 us (2%)
  other arithmetic  1.02 us (1%)
    ppermute x14, starting transfers between devices, shifted(): lax.ppermute(value, axis, [(i, (i + shift) % size) for i in range(size)])  28.3 us
    all_to_all x1, blocking collectives, on_device(): mine = lax.all_to_all(copies, ('z', 'y'), 0, 0, tiled=True)  17 us
    ppermute x14, waiting for transfers between devices, shifted(): lax.ppermute(value, axis, [(i, (i + shift) % size) for i in range(size)])  15.2 us
    pallas_call x3, Pallas kernels, project(): pl.pallas_call(functools.partial(project_kernel, chunk, first_slot, halve...  12.9 us
    all_to_all x1, starting transfers between devices, on_device(): parts = lax.all_to_all(halves, ('z', 'y'), 0, 0, tiled=True)  10.3 us
    pallas_call x1, Pallas kernels, make_maps(): pl.pallas_call(kernel, in_specs=[SMEM, SMEM, VMEM, VMEM, VMEM], out_specs...  3.58 us
  transfers between devices with their start and end apart: 15, of which 7 were waited for; matrix products, arithmetic and copies ran while one was open for 0% of the time, Pallas kernels for 10%

profile of v3, /device:TPU:1, one launch (start us, length us, event | category | flops | bytes accessed | tf_op | source)
XLA Modules:
  0.0 91.9 jit_solution(3736987955938286177)
XLA Ops:
  0.6 0.0 copy-start
  0.6 0.9 copy-done
  1.5 0.0 copy-start.2
  1.5 0.9 copy-done.2
  2.4 0.0 copy-start.1
  2.4 0.0 copy-start.3
  2.4 4.2 %first.1 = (f32[8,32,128]{2,1,0:T(8,128)S(1)}, f32[8,32,128]{2,1,0:T(8,128)S(1)}) custom-call(s32[1]{0:T(128)} %bitcast.2.refs_0_, bf16[128,32,1024]{2,1,0:T(8,128)(2,1)} %refs_1_.6, f32[256,128]{1,0:T(8,128)S(1)} %bitcast.14, bf16[64,1024]{1,0:T(8,128)(2,1)S(1)} %bitcast.17), custom_call_target="tpu_custom_call" | custom-call | flops 134217728 | bytes 2097152 | tf_op jit(solution)/shard_map/first/pallas_call | solution.py:112
  6.6 3.3 %collective-permute-start = (f32[8,32,128]{2,1,0:T(8,128)S(1)}, f32[8,32,128]{2,1,0:T(8,128)S(1)}, u32[]{:S(2)}, u32[]{:S(2)}) collective-permute-start(f32[8,32,128]{2,1,0:T(8,128)S(1)} %get-tuple-element.11.refs_4_), channel_id=1, source_target_pairs={{0,1},{1,0},{2,3},{3,2},{4,5},{5,4},{6,7},{7,6},{8,9},{9,8},{10,11... | collective-permute-start | bytes 393224 | tf_op jit(solution)/shard_map/ppermute | solution.py:252
  10.0 4.4 %rest.3 = f32[24,32,128]{2,1,0:T(8,128)S(1)} custom-call(s32[1]{0:T(128)} %bitcast.2.refs_0_, bf16[128,32,1024]{2,1,0:T(8,128)(2,1)} %refs_1_.6, f32[256,128]{1,0:T(8,128)S(1)} %bitcast.15, bf16[64,1024]{1,0:T(8,128)(2,1)S(1)} %bitcast.18, f32[8,32,128]{2,1,0:T(8,128)S(1)} %get-tuple-element.11.refs_4_), custom_call_target="tpu_custom_call" | custom-call | flops 201326592 | bytes 3145728 | tf_op jit(solution)/shard_map/rest/pallas_call | solution.py:112
  14.3 0.0 copy-start.4
  14.4 0.1 collective-permute-start.1
  14.5 0.0 collective-permute-done
  14.5 1.1 %collective-permute-start.4 = (f32[32,128]{1,0:T(8,128)S(1)}, f32[32,128]{1,0:T(8,128)S(1)}, u32[]{:S(2)}, u32[]{:S(2)}) collective-permute-start(f32[32,128]{1,0:T(8,128)S(1)} %slice_bitcast_fusion), channel_id=1, source_target_pairs={{0,6},{2,0},{4,2},{6,4},{1,7},{3,1},{5,3},{7,5},{8,14},{10,8},{12,... | collective-permute-start | bytes 49160 | tf_op jit(solution)/shard_map/ppermute | solution.py:252
  15.6 0.3 collective-permute-start.3
  16.0 0.7 collective-permute-start.2
  16.6 0.0 copy-done.1
  16.6 0.0 copy-done.3
  16.7 4.4 %rest.2 = f32[24,32,128]{2,1,0:T(8,128)S(1)} custom-call(s32[1]{0:T(128)} %bitcast.refs_0_, bf16[128,32,1024]{2,1,0:T(8,128)(2,1)} %refs_1_.6, f32[256,128]{1,0:T(8,128)S(1)} %bitcast.16, bf16[64,1024]{1,0:T(8,128)(2,1)S(1)} %bitcast.19, f32[8,32,128]{2,1,0:T(8,128)S(1)} %get-tuple-element.10.refs_4_), custom_call_target="tpu_custom_call" | custom-call | flops 201326592 | bytes 3145728 | tf_op jit(solution)/shard_map/rest/pallas_call | solution.py:112
  21.0 0.0 collective-permute-done.4
  21.1 0.0 collective-permute-done.3
  21.1 0.0 collective-permute-done.2
  21.1 0.0 collective-permute-done.1
  21.1 0.1 add.41
  21.2 0.8 pad_maximum_fusion
  22.0 10.3 %all-to-all-start = ((f32[32,32,128]{2,1,0:T(8,128)}), f32[32,32,128]{2,1,0:T(8,128)S(1)}, u32[]{:S(2)}, u32[]{:S(2)}) async-start(f32[32,32,128]{2,1,0:T(8,128)} %pad_maximum_fusion), calls=%async_computation | async-start | bytes 1048576 | tf_op jit(solution)/shard_map/all_to_all | solution.py:277
  32.3 3.1 %collective-permute-start.7 = (f32[32,128]{1,0:T(8,128)S(1)}, f32[32,128]{1,0:T(8,128)S(1)}, u32[]{:S(2)}, u32[]{:S(2)}) collective-permute-start(f32[32,128]{1,0:T(8,128)S(1)} %add_add_fusion.1), channel_id=1, source_target_pairs={{0,24},{8,32},{16,40},{24,48},{32,56},{40,0},{48,8},{56,16},{1,25}... | collective-permute-start | bytes 49160 | tf_op jit(solution)/shard_map/ppermute | solution.py:252
  35.4 2.4 %collective-permute-start.6 = (f32[32,128]{1,0:T(8,128)S(1)}, f32[32,128]{1,0:T(8,128)S(1)}, u32[]{:S(2)}, u32[]{:S(2)}) collective-permute-start(f32[32,128]{1,0:T(8,128)S(1)} %add_add_fusion.1), channel_id=1, source_target_pairs={{0,16},{8,24},{16,32},{24,40},{32,48},{40,56},{48,0},{56,8},{1,17}... | collective-permute-start | bytes 49160 | tf_op jit(solution)/shard_map/ppermute | solution.py:252
  37.8 0.3 collective-permute-start.5
  38.1 6.3 %collective-permute-done.7 = f32[32,128]{1,0:T(8,128)S(1)} collective-permute-done((f32[32,128]{1,0:T(8,128)S(1)}, f32[32,128]{1,0:T(8,128)S(1)}, u32[]{:S(2)}, u32[]{:S(2)}) %collective-permute-start.7) | collective-permute-done | bytes 16416 | tf_op jit(solution)/shard_map/ppermute | solution.py:252
  44.4 1.9 %collective-permute-done.6 = f32[32,128]{1,0:T(8,128)S(1)} collective-permute-done((f32[32,128]{1,0:T(8,128)S(1)}, f32[32,128]{1,0:T(8,128)S(1)}, u32[]{:S(2)}, u32[]{:S(2)}) %collective-permute-start.6) | collective-permute-done | bytes 16416 | tf_op jit(solution)/shard_map/ppermute | solution.py:252
  46.2 0.0 collective-permute-done.5
  46.2 4.5 %collective-permute-start.8 = (f32[32,128]{1,0:T(8,128)S(1)}, f32[32,128]{1,0:T(8,128)S(1)}, u32[]{:S(2)}, u32[]{:S(2)}) collective-permute-start(f32[32,128]{1,0:T(8,128)S(1)} %add_add_fusion), channel_id=1, source_target_pairs={{0,32},{8,40},{16,48},{24,56},{32,0},{40,8},{48,16},{56,24},{1,33}... | collective-permute-start | bytes 49160 | tf_op jit(solution)/shard_map/ppermute | solution.py:252
  50.7 0.1 pad_add_fusion.where_ref
  50.8 2.0 %collective-permute-done.8 = f32[32,128]{1,0:T(8,128)S(1)} collective-permute-done((f32[32,128]{1,0:T(8,128)S(1)}, f32[32,128]{1,0:T(8,128)S(1)}, u32[]{:S(2)}, u32[]{:S(2)}) %collective-permute-start.8) | collective-permute-done | bytes 16416 | tf_op jit(solution)/shard_map/ppermute | solution.py:252
  52.8 0.0 all-to-all-done.parts_ref
  52.8 1.0 %moments.1 = (f32[16,128]{1,0:T(8,128)S(1)}, f32[16,128]{1,0:T(8,128)S(1)}) custom-call(s32[2]{0:T(128)S(1)} %pad_add_fusion.where_ref, f32[32,32,128]{2,1,0:T(8,128)S(1)} %all-to-all-done.parts_ref, f32[2,32,128]{2,1,0:T(8,128)S(1)} %pad_maximum_fusion.1.second_ref), custom_call_target="tpu_custom_call" | custom-call | flops 4194304 | bytes 1048576 | tf_op jit(solution)/shard_map/moments/pallas_call | solution.py:159
  53.8 5.0 %collective-permute-start.9 = (f32[16,128]{1,0:T(8,128)S(1)}, f32[16,128]{1,0:T(8,128)S(1)}, u32[]{:S(2)}, u32[]{:S(2)}) collective-permute-start(f32[16,128]{1,0:T(8,128)S(1)} %get-tuple-element.15), channel_id=1, source_target_pairs={{0,1},{1,0},{2,3},{3,2},{4,5},{5,4},{6,7},{7,6},{8,9},{9,8},{10,11... | collective-permute-start | bytes 24584 | tf_op jit(solution)/shard_map/ppermute | solution.py:252
  58.8 0.8 collective-permute-done.9
  59.6 2.5 %collective-permute-start.12 = (f32[16,128]{1,0:T(8,128)S(1)}, f32[16,128]{1,0:T(8,128)S(1)}, u32[]{:S(2)}, u32[]{:S(2)}) collective-permute-start(f32[16,128]{1,0:T(8,128)S(1)} %add.48), channel_id=1, source_target_pairs={{0,192},{64,0},{128,64},{192,128},{1,193},{65,1},{129,65},{193,129... | collective-permute-start | bytes 24584 | tf_op jit(solution)/shard_map/ppermute | solution.py:252
  62.1 0.5 collective-permute-start.11
  62.6 0.6 collective-permute-start.10
  63.2 0.0 collective-permute-done.12
  63.2 2.9 %collective-permute-done.11 = f32[16,128]{1,0:T(8,128)S(1)} collective-permute-done((f32[16,128]{1,0:T(8,128)S(1)}, f32[16,128]{1,0:T(8,128)S(1)}, u32[]{:S(2)}, u32[]{:S(2)}) %collective-permute-start.11) | collective-permute-done | bytes 8224 | tf_op jit(solution)/shard_map/ppermute | solution.py:252
  66.1 0.2 collective-permute-done.10
  66.4 17.0 %all_to_all.10.refs_2_ = f32[32,16,128]{2,1,0:T(8,128)S(1)} all-to-all(f32[32,16,128]{2,1,0:T(8,128)S(1)} %broadcast_in_dim.16), channel_id=1, replica_groups=mesh['grp'=4,'z'=8,'y'=4,'core'=2] {'z','y'}, dimensions={0} | all-to-all | bytes 524288 | tf_op jit(solution)/shard_map/all_to_all | solution.py:285
  83.4 3.8 %collective-permute-start.13 = (f32[32,16,128]{2,1,0:T(8,128)S(1)}, f32[32,16,128]{2,1,0:T(8,128)S(1)}, u32[]{:S(2)}, u32[]{:S(2)}) collective-permute-start(f32[32,16,128]{2,1,0:T(8,128)S(1)} %all_to_all.10.refs_2_), channel_id=1, source_target_pairs={{0,1},{1,0},{2,3},{3,2},{4,5},{5,4},{6,7},{7,6},{8,9},{9,8},{10,11... | collective-permute-start | bytes 786440 | tf_op jit(solution)/shard_map/ppermute | solution.py:252
  87.2 1.2 %collective-permute-done.13.refs_3_ = f32[32,16,128]{2,1,0:T(8,128)S(1)} collective-permute-done((f32[32,16,128]{2,1,0:T(8,128)S(1)}, f32[32,16,128]{2,1,0:T(8,128)S(1)}, u32[]{:S(2)}, u32[]{:S(2)}) %collective-permute-start.13) | collective-permute-done | bytes 262176 | tf_op jit(solution)/shard_map/ppermute | solution.py:252
  88.3 0.0 copy-done.4
  88.3 3.6 %maps.1 = (f32[30,1024]{1,0:T(8,128)}, f32[1,1024]{1,0:T(1,128)}) custom-call(s32[1]{0:T(128)} %bitcast.refs_0_, s32[30]{0:T(128)S(1)} %copy-done.4, f32[32,16,128]{2,1,0:T(8,128)S(1)} %all_to_all.10.refs_2_, f32[32,16,128]{2,1,0:T(8,128)S(1)} %collective-permute-done.13.refs_3_, bf16[64,1024]{1,0:T(8,128)(2,1)S(1)} %bitcast.20), custom_call_target="tpu_custom_call" | custom-call | flops 268435456 | bytes 1048576 | tf_op jit(solution)/shard_map/maps/pallas_call | solution.py:240
  (8 shorter events, 0.1 us)
Async XLA Ops:
  0.6 0.9 copy-start
  1.5 0.9 copy-start.2
  2.4 14.2 %copy-start.1 = (f32[128,32,8]{0,2,1:T(8,128)S(1)}, f32[128,32,8]{0,2,1:T(8,128)}, u32[]{:S(2)}) copy-start(f32[128,32,8]{0,2,1:T(8,128)} %param.5) | copy-start | bytes 393220
  2.4 14.2 %copy-start.3 = (bf16[1024,64]{0,1:T(8,128)(2,1)S(1)}, bf16[1024,64]{0,1:T(8,128)(2,1)}, u32[]{:S(2)}) copy-start(bf16[1024,64]{0,1:T(8,128)(2,1)} %param.6) | copy-start | bytes 393220
  6.6 7.8 %collective-permute-start = (f32[8,32,128]{2,1,0:T(8,128)S(1)}, f32[8,32,128]{2,1,0:T(8,128)S(1)}, u32[]{:S(2)}, u32[]{:S(2)}) collective-permute-start(f32[8,32,128]{2,1,0:T(8,128)S(1)} %get-tuple-element.11.refs_4_), channel_id=1, source_target_pairs={{0,1},{1,0},{2,3},{3,2},{4,5},{5,4},{6,7},{7,6},{8,9},{9,8},{10,11... | collective-permute-start | bytes 393224 | tf_op jit(solution)/shard_map/ppermute | solution.py:252
  14.3 74.0 %copy-start.4 = (s32[30]{0:T(128)S(1)}, s32[30]{0:T(128)}, u32[]{:S(2)}) copy-start(s32[30]{0:T(128)} %refs_1_.7) | copy-start | bytes 364
  14.4 6.7 %collective-permute-start.1 = (f32[24,32,128]{2,1,0:T(8,128)S(1)}, f32[24,32,128]{2,1,0:T(8,128)S(1)}, u32[]{:S(2)}, u32[]{:S(2)}) collective-permute-start(f32[24,32,128]{2,1,0:T(8,128)S(1)} %rest.3), channel_id=1, source_target_pairs={{0,1},{1,0},{2,3},{3,2},{4,5},{5,4},{6,7},{7,6},{8,9},{9,8},{10,11... | collective-permute-start | bytes 1179656 | tf_op jit(solution)/shard_map/ppermute | solution.py:252
  14.5 6.5 %collective-permute-start.4 = (f32[32,128]{1,0:T(8,128)S(1)}, f32[32,128]{1,0:T(8,128)S(1)}, u32[]{:S(2)}, u32[]{:S(2)}) collective-permute-start(f32[32,128]{1,0:T(8,128)S(1)} %slice_bitcast_fusion), channel_id=1, source_target_pairs={{0,6},{2,0},{4,2},{6,4},{1,7},{3,1},{5,3},{7,5},{8,14},{10,8},{12,... | collective-permute-start | bytes 49160 | tf_op jit(solution)/shard_map/ppermute | solution.py:252
  15.6 5.5 %collective-permute-start.3 = (f32[32,128]{1,0:T(8,128)S(1)}, f32[32,128]{1,0:T(8,128)S(1)}, u32[]{:S(2)}, u32[]{:S(2)}) collective-permute-start(f32[32,128]{1,0:T(8,128)S(1)} %slice_bitcast_fusion), channel_id=1, source_target_pairs={{0,4},{2,6},{4,0},{6,2},{1,5},{3,7},{5,1},{7,3},{8,12},{10,14},{12... | collective-permute-start | bytes 49160 | tf_op jit(solution)/shard_map/ppermute | solution.py:252
  16.0 5.1 %collective-permute-start.2 = (f32[32,128]{1,0:T(8,128)S(1)}, f32[32,128]{1,0:T(8,128)S(1)}, u32[]{:S(2)}, u32[]{:S(2)}) collective-permute-start(f32[32,128]{1,0:T(8,128)S(1)} %slice_bitcast_fusion), channel_id=1, source_target_pairs={{0,2},{2,4},{4,6},{6,0},{1,3},{3,5},{5,7},{7,1},{8,10},{10,12},{12... | collective-permute-start | bytes 49160 | tf_op jit(solution)/shard_map/ppermute | solution.py:252
  22.0 30.8 %all-to-all-start = ((f32[32,32,128]{2,1,0:T(8,128)}), f32[32,32,128]{2,1,0:T(8,128)S(1)}, u32[]{:S(2)}, u32[]{:S(2)}) async-start(f32[32,32,128]{2,1,0:T(8,128)} %pad_maximum_fusion), calls=%async_computation | async-start | bytes 1048576 | tf_op jit(solution)/shard_map/all_to_all | solution.py:277
  32.3 12.1 %collective-permute-start.7 = (f32[32,128]{1,0:T(8,128)S(1)}, f32[32,128]{1,0:T(8,128)S(1)}, u32[]{:S(2)}, u32[]{:S(2)}) collective-permute-start(f32[32,128]{1,0:T(8,128)S(1)} %add_add_fusion.1), channel_id=1, source_target_pairs={{0,24},{8,32},{16,40},{24,48},{32,56},{40,0},{48,8},{56,16},{1,25}... | collective-permute-start | bytes 49160 | tf_op jit(solution)/shard_map/ppermute | solution.py:252
  35.4 10.8 %collective-permute-start.6 = (f32[32,128]{1,0:T(8,128)S(1)}, f32[32,128]{1,0:T(8,128)S(1)}, u32[]{:S(2)}, u32[]{:S(2)}) collective-permute-start(f32[32,128]{1,0:T(8,128)S(1)} %add_add_fusion.1), channel_id=1, source_target_pairs={{0,16},{8,24},{16,32},{24,40},{32,48},{40,56},{48,0},{56,8},{1,17}... | collective-permute-start | bytes 49160 | tf_op jit(solution)/shard_map/ppermute | solution.py:252
  37.8 8.4 %collective-permute-start.5 = (f32[32,128]{1,0:T(8,128)S(1)}, f32[32,128]{1,0:T(8,128)S(1)}, u32[]{:S(2)}, u32[]{:S(2)}) collective-permute-start(f32[32,128]{1,0:T(8,128)S(1)} %add_add_fusion.1), channel_id=1, source_target_pairs={{0,8},{8,16},{16,24},{24,32},{32,40},{40,48},{48,56},{56,0},{1,9},... | collective-permute-start | bytes 49160 | tf_op jit(solution)/shard_map/ppermute | solution.py:252
  46.2 6.6 %collective-permute-start.8 = (f32[32,128]{1,0:T(8,128)S(1)}, f32[32,128]{1,0:T(8,128)S(1)}, u32[]{:S(2)}, u32[]{:S(2)}) collective-permute-start(f32[32,128]{1,0:T(8,128)S(1)} %add_add_fusion), channel_id=1, source_target_pairs={{0,32},{8,40},{16,48},{24,56},{32,0},{40,8},{48,16},{56,24},{1,33}... | collective-permute-start | bytes 49160 | tf_op jit(solution)/shard_map/ppermute | solution.py:252
  53.8 5.8 %collective-permute-start.9 = (f32[16,128]{1,0:T(8,128)S(1)}, f32[16,128]{1,0:T(8,128)S(1)}, u32[]{:S(2)}, u32[]{:S(2)}) collective-permute-start(f32[16,128]{1,0:T(8,128)S(1)} %get-tuple-element.15), channel_id=1, source_target_pairs={{0,1},{1,0},{2,3},{3,2},{4,5},{5,4},{6,7},{7,6},{8,9},{9,8},{10,11... | collective-permute-start | bytes 24584 | tf_op jit(solution)/shard_map/ppermute | solution.py:252
  59.6 3.6 %collective-permute-start.12 = (f32[16,128]{1,0:T(8,128)S(1)}, f32[16,128]{1,0:T(8,128)S(1)}, u32[]{:S(2)}, u32[]{:S(2)}) collective-permute-start(f32[16,128]{1,0:T(8,128)S(1)} %add.48), channel_id=1, source_target_pairs={{0,192},{64,0},{128,64},{192,128},{1,193},{65,1},{129,65},{193,129... | collective-permute-start | bytes 24584 | tf_op jit(solution)/shard_map/ppermute | solution.py:252
  62.1 4.0 %collective-permute-start.11 = (f32[16,128]{1,0:T(8,128)S(1)}, f32[16,128]{1,0:T(8,128)S(1)}, u32[]{:S(2)}, u32[]{:S(2)}) collective-permute-start(f32[16,128]{1,0:T(8,128)S(1)} %add.48), channel_id=1, source_target_pairs={{0,128},{64,192},{128,0},{192,64},{1,129},{65,193},{129,1},{193,65... | collective-permute-start | bytes 24584 | tf_op jit(solution)/shard_map/ppermute | solution.py:252
  62.6 3.7 %collective-permute-start.10 = (f32[16,128]{1,0:T(8,128)S(1)}, f32[16,128]{1,0:T(8,128)S(1)}, u32[]{:S(2)}, u32[]{:S(2)}) collective-permute-start(f32[16,128]{1,0:T(8,128)S(1)} %add.48), channel_id=1, source_target_pairs={{0,64},{64,128},{128,192},{192,0},{1,65},{65,129},{129,193},{193,1... | collective-permute-start | bytes 24584 | tf_op jit(solution)/shard_map/ppermute | solution.py:252
  83.4 4.9 %collective-permute-start.13 = (f32[32,16,128]{2,1,0:T(8,128)S(1)}, f32[32,16,128]{2,1,0:T(8,128)S(1)}, u32[]{:S(2)}, u32[]{:S(2)}) collective-permute-start(f32[32,16,128]{2,1,0:T(8,128)S(1)} %all_to_all.10.refs_2_), channel_id=1, source_target_pairs={{0,1},{1,0},{2,3},{3,2},{4,5},{5,4},{6,7},{7,6},{8,9},{9,8},{10,11... | collective-permute-start | bytes 786440 | tf_op jit(solution)/shard_map/ppermute | solution.py:252

commit v4 on v2

--- a/solution.py
+++ b/solution.py
@@ -14,24 +14,20 @@
 SMEM = pl.BlockSpec(memory_space=pltpu.SMEM)
 
 
-def project_kernel(chunk, half_ref, fields_ref, scale_ref, basis_ref, out_ref, buffer, weights, spread, scales3, result, in_sems, out_sems):
+def project_kernel(chunk, where_ref, fields_ref, scale_ref, basis_ref, out_ref, buffer, weights, spread, scales3, sems):
     rows, slots, cells = buffer.shape
     packed = rows // 2
     modes = basis_ref.shape[0]
-    blocks = scale_ref.shape[0] // slots
-    lanes = cells // blocks
+    lanes = 128
+    blocks = cells // lanes
     chunks = packed // chunk
-    base = half_ref[0] * rows
+    groups = slots // 8
+    base = where_ref[0] * rows
 
     def fetch(index, which):
         first = which * packed + index * chunk
         return pltpu.make_async_copy(
-            fields_ref.at[pl.ds(base + first, chunk)], buffer.at[pl.ds(first, chunk)], in_sems.at[index, which]
-        )
-
-    def put(index):
-        return pltpu.make_async_copy(
-            result.at[index], out_ref.at[:, pl.ds(index * chunk, chunk)], out_sems.at[index]
+            fields_ref.at[pl.ds(base + first, chunk)], buffer.at[pl.ds(first, chunk)], sems.at[index, which]
         )
 
     for index in range(chunks):
@@ -51,13 +47,14 @@
     middle = rest.astype(BF16).astype(F32)
     low = rest - middle
     lane = lax.broadcasted_iota(jnp.int32, (by_row.shape[0], 128), 1)
-    for column in range(2):
-        cut = slice(column * 128, (column + 1) * 128)
+    for q in range(groups):
+        cut = slice(q // 2 * 128, q // 2 * 128 + 128)
         turned_middle = pltpu.roll(middle[:, cut], 64, 1)
-        scales3[2 * column, :, :128] = jnp.where(lane < 64, high[:, cut], turned_middle)
-        scales3[2 * column, :, 128:] = low[:, cut]
-        scales3[2 * column + 1, :, :128] = jnp.where(lane < 64, turned_middle, high[:, cut])
-        scales3[2 * column + 1, :, 128:] = low[:, cut]
+        if q % 2 == 0:
+            scales3[q, :, :128] = jnp.where(lane < 64, high[:, cut], turned_middle)
+        else:
+            scales3[q, :, :128] = jnp.where(lane < 64, turned_middle, high[:, cut])
+        scales3[q, :, 128:] = low[:, cut]
 
     slot8 = lax.broadcasted_iota(jnp.int32, (8, 256), 0)
     lane8 = lax.broadcasted_iota(jnp.int32, (8, 256), 1)
@@ -71,25 +68,25 @@
             first = which * packed + index * chunk
             left = []
             for row in range(chunk):
-                for q in range(slots // 8):
+                for q in range(groups):
                     line = jnp.broadcast_to(scales3[q, pl.ds(base + first + row, 1), :], (8, 256))
                     left.append(jnp.where(masks[q % 2], line, 0.0))
             left = jnp.concatenate(left, axis=0).astype(BF16)
             scale = jnp.dot(left, spread[...], preferred_element_type=F32)
-            piece = buffer[first : first + chunk].reshape(chunk * slots, cells)
-            dequant = (piece.astype(F32) * scale).astype(BF16)
-            part = jnp.dot(dequant, weights[which], preferred_element_type=F32)
-            total = part if total is None else total + part
+            piece = buffer[first : first + chunk].astype(F32).reshape(chunk * slots, cells)
+            dequant = (piece * scale).astype(BF16)
+            product = jnp.dot(dequant, weights[which], preferred_element_type=F32)
+            total = product if total is None else total + product
+        tiles = []
         for row in range(chunk):
             tile = total[row * slots : (row + 1) * slots]
-            tile = tile - jnp.where(slot >= 2, jnp.broadcast_to(tile[:1], tile.shape), 0.0)
-            result[index, :, row, :] = tile
-        put(index).start()
-    for index in range(chunks):
-        put(index).wait()
-
-
-def project(half, fields, scales, basis):
+            tiles.append(tile - jnp.where(slot >= 2, jnp.broadcast_to(tile[:1], tile.shape), 0.0))
+        turned = jnp.swapaxes(jnp.stack(tiles), 0, 1)
+        for group in range(4):
+            place = lax.rem(group + 4 - where_ref[1], 4)
+            out_ref[place, :, index * chunk : (index + 1) * chunk, :] = turned[8 * group : 8 * group + 8]
+
+def project(where, fields, scales, basis):
     rows, slots, cells = fields.shape
     modes = basis.shape[0]
     packed = rows // 4
@@ -97,34 +94,75 @@
     chunks = packed // chunk
     return pl.pallas_call(
         functools.partial(project_kernel, chunk),
-        in_specs=[SMEM, pl.BlockSpec(memory_space=pltpu.HBM), VMEM, VMEM],
-        out_specs=pl.BlockSpec(memory_space=pl.ANY),
-        out_shape=jax.ShapeDtypeStruct((slots, packed, 2 * modes), F32),
+        in_specs=[SMEM, pl.BlockSpec(memory_space=pl.ANY), VMEM, VMEM],
+        out_specs=VMEM,
+        out_shape=jax.ShapeDtypeStruct((4, slots // 4, packed, 2 * modes), F32),
         scratch_shapes=[
             pltpu.VMEM((rows // 2, slots, cells), BF16),
             pltpu.VMEM((2, cells, 2 * modes), BF16),
             pltpu.VMEM((256, cells), BF16),
             pltpu.VMEM((slots // 8, rows, 256), F32),
-            pltpu.VMEM((chunks, slots, chunk, 2 * modes), F32),
             pltpu.SemaphoreType.DMA((chunks, 2)),
-            pltpu.SemaphoreType.DMA((chunks,)),
         ],
-        compiler_params=pltpu.CompilerParams(vmem_limit_bytes=32 << 20),
+        compiler_params=pltpu.CompilerParams(vmem_limit_bytes=52 << 20),
         cost_estimate=pl.CostEstimate(
             flops=rows * slots * cells * modes, bytes_accessed=rows * slots * cells, transcendentals=0
         ),
         name="project",
-    )(half, fields, scales, basis)
-
-
-def moments_kernel(where_ref, parts_ref, second_ref, keep_ref, send_ref):
+    )(where, fields, scales, basis)
+
+
+def combine_kernel(where_ref, ours_ref, got_ref, *outs):
+    place = lax.rem(4 - where_ref[1], 4)
+    second = ours_ref[place, 1] + got_ref[place, 1]
+    for group, out in enumerate(outs):
+        out[:8] = ours_ref[group] + got_ref[group]
+        out[8] = second
+
+
+def combine(where, ours, got):
+    groups, count, packed, lanes = ours.shape
+    out = jax.ShapeDtypeStruct((count + 1, packed, lanes), F32)
+    return pl.pallas_call(
+        combine_kernel,
+        in_specs=[SMEM, VMEM, VMEM],
+        out_specs=[VMEM] * groups,
+        out_shape=[out] * groups,
+        compiler_params=pltpu.CompilerParams(vmem_limit_bytes=16 << 20),
+        cost_estimate=pl.CostEstimate(flops=1 << 18, bytes_accessed=1 << 21, transcendentals=0),
+        name="combine",
+    )(where, ours, got)
+
+
+def add_up_kernel(*refs):
+    *parts, out_ref = refs
+    total = parts[0][...]
+    for part in parts[1:]:
+        total = total + part[...]
+    packed = total.shape[1]
+    out_ref[:, :packed] = total[:8]
+    out_ref[:, packed:] = jnp.broadcast_to(total[8:], total[:8].shape)
+
+
+def add_up(parts):
+    count, packed, lanes = parts[0].shape
+    return pl.pallas_call(
+        add_up_kernel,
+        in_specs=[VMEM] * len(parts),
+        out_specs=VMEM,
+        out_shape=jax.ShapeDtypeStruct((count - 1, 2 * packed, lanes), F32),
+        compiler_params=pltpu.CompilerParams(vmem_limit_bytes=16 << 20),
+        cost_estimate=pl.CostEstimate(flops=1 << 18, bytes_accessed=1 << 20, transcendentals=0),
+        name="add_up",
+    )(*parts)
+
+
+def moments_kernel(where_ref, parts_ref, keep_ref, send_ref):
     slot, half = where_ref[0], where_ref[1]
-    own = parts_ref[0]
+    both = parts_ref[0]
     for source in range(1, parts_ref.shape[0]):
-        own = own + parts_ref[source]
-    second = second_ref[0]
-    for source in range(1, second_ref.shape[0]):
-        second = second + second_ref[source]
+        both = both + parts_ref[source]
+    own, second = both[:32], both[32:]
     left = jnp.where(slot == 0, own, second)
     wide = lax.dot_general(left, own, (((0,), (0,)), ((), ())), precision=HIGHEST, preferred_element_type=F32)
     matrix = wide[:64, :64] + wide[64:, 64:]
@@ -142,17 +180,17 @@
     send_ref[...] = jnp.where(half == 0, lower, upper)
 
 
-def moments(where, parts, second):
+def moments(where, parts):
     out = jax.ShapeDtypeStruct((16, 128), F32)
     return pl.pallas_call(
         moments_kernel,
-        in_specs=[SMEM, VMEM, VMEM],
+        in_specs=[SMEM, VMEM],
         out_specs=(VMEM, VMEM),
         out_shape=(out, out),
         compiler_params=pltpu.CompilerParams(vmem_limit_bytes=16 << 20),
         cost_estimate=pl.CostEstimate(flops=1 << 22, bytes_accessed=1 << 20, transcendentals=0),
         name="moments",
-    )(where, parts, second)
+    )(where, parts)
 
 
 def three(value):
@@ -248,27 +286,24 @@
     rows_total = float(rows * sizes["grp"])
     cell_total = float(cells * sizes["z"] * sizes["y"] * sizes["core"])
     core = lax.axis_index("core").astype(jnp.int32)
-    slot = (lax.axis_index("z") * sizes["y"] + lax.axis_index("y")).astype(jnp.int32)
+    slot = (lax.axis_index("y") * sizes["z"] + lax.axis_index("z")).astype(jnp.int32)
     by_slot = jnp.transpose(scales, (1, 2, 0)).reshape(slots * blocks, rows)
     basis = pod_basis.T
-    packed = rows // 4
-
-    theirs = project((1 - core)[None], fields, by_slot, basis)
+
+    height = lax.axis_index("y").astype(jnp.int32)
+    theirs = project(jnp.stack([1 - core, height]), fields, by_slot, basis)
     got = shifted(theirs, "core", 2, 1)
-    ours = project(core[None], fields, by_slot, basis)
-    halves = ours + got
-
-    parts = lax.all_to_all(halves, ("z", "y"), 0, 0, tiled=True)
-    second = halves[1]
-    second = second + sum(shifted(second, "y", sizes["y"], s) for s in range(1, sizes["y"]))
-    second = second + sum(shifted(second, "z", sizes["z"], s) for s in range(1, sizes["z"] // 2))
-    second = jnp.stack([second, shifted(second, "z", sizes["z"], sizes["z"] // 2)])
-
-    keep, send = moments(jnp.stack([slot, core]), parts, second)
+    where = jnp.stack([core, height])
+    ours = project(where, fields, by_slot, basis)
+    pieces = combine(where, ours, got)
+    parts = add_up([pieces[0]] + [shifted(pieces[s], "y", sizes["y"], s) for s in range(1, sizes["y"])])
+    parts = lax.all_to_all(parts, "z", 0, 0, tiled=True)
+
+    keep, send = moments(jnp.stack([slot, core]), parts)
     piece = keep + shifted(send, "core", 2, 1)
     piece = piece + sum(shifted(piece, "grp", sizes["grp"], s) for s in range(1, sizes["grp"]))
     copies = jnp.broadcast_to(piece[None], (slots,) + piece.shape)
-    mine = lax.all_to_all(copies, ("z", "y"), 0, 0, tiled=True)
+    mine = lax.all_to_all(copies, ("y", "z"), 0, 0, tiled=True)
     other = shifted(mine, "core", 2, 1)
     sobol, total = make_maps(rows_total, cell_total, core[None], param_order, mine, other, basis)
     return sobol, total.reshape(cells)

time: 90.6 us -> 79.5 us (0.88)
  starting transfers between devices: 34.7 us -> 24.3 us
  local copies, waits for them, and re-layouts: 5.94 us -> 1.85 us
  waiting for transfers between devices: 18.5 us -> 22.1 us
  Pallas kernels: 14 us -> 16.7 us
  other arithmetic: 1.7 us -> 0.23 us
  blocking collectives: 14.5 us -> 13.3 us
    all_to_all x1, waiting for transfers between devices: 0.01 us -> 10.1 us  [on_device(): parts = lax.all_to_all(parts, 'z', 0, 0, tiled=True)]
    ppermute x13 -> x9, starting transfers between devices: 25.2 us -> 16.9 us  [shifted(): lax.ppermute(value, axis, [(i, (i + shift) % size) for i in range(size)])]
    ppermute x13 -> x9, waiting for transfers between devices: 18.5 us -> 12 us  [shifted(): lax.ppermute(value, axis, [(i, (i + shift) % size) for i in range(size)])]
    unnamed x12 -> x10, local copies, waits for them, and re-layouts: 5.2 us -> 1.82 us
    all_to_all x1, starting transfers between devices: 9.49 us -> 7.37 us  [on_device(): parts = lax.all_to_all(parts, 'z', 0, 0, tiled=True)]
    add x3 -> x0, other arithmetic: 1.62 us -> none  [the longest x1 0.89 us: on_device(): halves = ours + got]
    pallas_call x2, Pallas kernels: 9.45 us -> 10.9 us  [project(): pl.pallas_call(functools.partial(project_kernel, chunk), in_specs=[SMEM,...]
    pallas_call x1 -> x3, Pallas kernels: 0.97 us -> 2.28 us  [the longest x1 0.94 us: moments(): pl.pallas_call(moments_kernel, in_specs=[SMEM, VMEM], out_specs=(VMEM, VM...]
  transfers between devices with their start and end apart: 14 -> 10, of which waited for: 10 -> 8; matrix products, arithmetic and copies ran while one was open for 2% -> 0% of each run, Pallas kernels for 5% -> 7%
where the time goes in v4:
time: 79.5 us; the launch traced here: 79.2 us
  starting transfers between devices  24.3 us (31%)
  waiting for transfers between devices  22.1 us (28%)
  Pallas kernels  16.7 us (21%)
  blocking collectives  13.3 us (17%)
  local copies, waits for them, and re-layouts  1.85 us (2%)
    ppermute x9, starting transfers between devices, shifted(): lax.ppermute(value, axis, [(i, (i + shift) % size) for i in range(size)])  16.9 us
    all_to_all x1, blocking collectives, on_device(): mine = lax.all_to_all(copies, ('y', 'z'), 0, 0, tiled=True)  13.3 us
    ppermute x9, waiting for transfers between devices, shifted(): lax.ppermute(value, axis, [(i, (i + shift) % size) for i in range(size)])  12 us
    pallas_call x2, Pallas kernels, project(): pl.pallas_call(functools.partial(project_kernel, chunk), in_specs=[SMEM,...  10.9 us
    all_to_all x1, waiting for transfers between devices, on_device(): parts = lax.all_to_all(parts, 'z', 0, 0, tiled=True)  10.1 us
    all_to_all x1, starting transfers between devices, on_device(): parts = lax.all_to_all(parts, 'z', 0, 0, tiled=True)  7.37 us
    pallas_call x1, Pallas kernels, make_maps(): pl.pallas_call(kernel, in_specs=[SMEM, SMEM, VMEM, VMEM, VMEM], out_specs...  3.58 us
    unnamed x10, local copies, waits for them, and re-layouts  1.82 us
  transfers between devices with their start and end apart: 10, of which 8 were waited for; matrix products, arithmetic and copies ran while one was open for 0% of the time, Pallas kernels for 7%

profile of v4, /device:TPU:1, one launch (start us, length us, event | category | flops | bytes accessed | tf_op | source)
XLA Modules:
  0.0 79.2 jit_solution(6219508653718346175)
XLA Ops:
  0.6 0.1 pad_add_fusion.2.where_ref
  0.7 0.0 copy-start
  0.7 0.9 %copy-done = f32[128,32,8]{0,2,1:T(8,128)S(1)} copy-done((f32[128,32,8]{0,2,1:T(8,128)S(1)}, f32[128,32,8]{0,2,1:T(8,128)}, u32[]{:S(2)}) %copy-start) | copy-done | bytes 131096
  1.6 0.0 copy-start.2
  1.6 0.9 %copy-done.2 = bf16[1024,64]{0,1:T(8,128)(2,1)S(1)} copy-done((bf16[1024,64]{0,1:T(8,128)(2,1)S(1)}, bf16[1024,64]{0,1:T(8,128)(2,1)}, u32[]{:S(2)}) %copy-start.2) | copy-done | bytes 131096
  2.5 0.0 copy-start.1
  2.5 5.4 %project.3 = f32[4,8,32,128]{3,2,1,0:T(8,128)S(1)} custom-call(s32[2]{0:T(128)S(1)} %pad_add_fusion.2.where_ref, bf16[128,32,1024]{2,1,0:T(8,128)(2,1)} %fields_ref.3, f32[256,128]{1,0:T(8,128)S(1)} %bitcast.9, bf16[64,1024]{1,0:T(8,128)(2,1)S(1)} %bitcast.11), custom_call_target="tpu_custom_call" | custom-call | flops 268435456 | bytes 4194304 | tf_op jit(solution)/shard_map/project/pallas_call | solution.py:95
  8.0 0.0 copy-start.3
  8.0 0.0 copy-start.4
  8.0 3.3 %collective-permute-start = (f32[4,8,32,128]{3,2,1,0:T(8,128)S(1)}, f32[4,8,32,128]{3,2,1,0:T(8,128)S(1)}, u32[]{:S(2)}, u32[]{:S(2)}) collective-permute-start(f32[4,8,32,128]{3,2,1,0:T(8,128)S(1)} %project.3), channel_id=1, source_target_pairs={{0,1},{1,0},{2,3},{3,2},{4,5},{5,4},{6,7},{7,6},{8,9},{9,8},{10,11... | collective-permute-start | bytes 1572872 | tf_op jit(solution)/shard_map/ppermute | solution.py:278
  11.3 0.1 pad_add_fusion.1.where_ref
  11.4 0.0 copy-done.1
  11.4 5.4 %project.2.ours_ref = f32[4,8,32,128]{3,2,1,0:T(8,128)S(1)} custom-call(s32[2]{0:T(128)S(1)} %pad_add_fusion.1.where_ref, bf16[128,32,1024]{2,1,0:T(8,128)(2,1)} %fields_ref.3, f32[256,128]{1,0:T(8,128)S(1)} %bitcast.10, bf16[64,1024]{1,0:T(8,128)(2,1)S(1)} %bitcast.12), custom_call_target="tpu_custom_call" | custom-call | flops 268435456 | bytes 4194304 | tf_op jit(solution)/shard_map/project/pallas_call | solution.py:95
  16.8 0.0 collective-permute-done.got_ref
  16.9 0.6 combine.1
  17.5 0.1 collective-permute-start.1
  17.6 2.2 %collective-permute-start.2 = (f32[9,32,128]{2,1,0:T(8,128)S(1)}, f32[9,32,128]{2,1,0:T(8,128)S(1)}, u32[]{:S(2)}, u32[]{:S(2)}) collective-permute-start(f32[9,32,128]{2,1,0:T(8,128)S(1)} %get-tuple-element.12), channel_id=1, source_target_pairs={{0,4},{2,6},{4,0},{6,2},{1,5},{3,7},{5,1},{7,3},{8,12},{10,14},{12... | collective-permute-start | bytes 442376 | tf_op jit(solution)/shard_map/ppermute | solution.py:278
  19.7 1.1 %collective-permute-start.3 = (f32[9,32,128]{2,1,0:T(8,128)S(1)}, f32[9,32,128]{2,1,0:T(8,128)S(1)}, u32[]{:S(2)}, u32[]{:S(2)}) collective-permute-start(f32[9,32,128]{2,1,0:T(8,128)S(1)} %get-tuple-element.13), channel_id=1, source_target_pairs={{0,6},{2,0},{4,2},{6,4},{1,7},{3,1},{5,3},{7,5},{8,14},{10,8},{12,... | collective-permute-start | bytes 442376 | tf_op jit(solution)/shard_map/ppermute | solution.py:278
  20.8 3.8 %collective-permute-done.1.refs_1_ = f32[9,32,128]{2,1,0:T(8,128)S(1)} collective-permute-done((f32[9,32,128]{2,1,0:T(8,128)S(1)}, f32[9,32,128]{2,1,0:T(8,128)S(1)}, u32[]{:S(2)}, u32[]{:S(2)}) %collective-permute-start.1) | collective-permute-done | bytes 147488 | tf_op jit(solution)/shard_map/ppermute | solution.py:278
  24.6 2.3 %collective-permute-done.2.refs_2_ = f32[9,32,128]{2,1,0:T(8,128)S(1)} collective-permute-done((f32[9,32,128]{2,1,0:T(8,128)S(1)}, f32[9,32,128]{2,1,0:T(8,128)S(1)}, u32[]{:S(2)}, u32[]{:S(2)}) %collective-permute-start.2) | collective-permute-done | bytes 147488 | tf_op jit(solution)/shard_map/ppermute | solution.py:278
  26.9 0.7 collective-permute-done.3.refs_3_
  27.7 0.7 add_up.1
  28.4 7.4 %all-to-all-start = ((f32[8,64,128]{2,1,0:T(8,128)}), f32[8,64,128]{2,1,0:T(8,128)S(1)}, u32[]{:S(2)}, u32[]{:S(2)}) async-start(f32[8,64,128]{2,1,0:T(8,128)} %add_up.1), calls=%async_computation | async-start | bytes 524288 | tf_op jit(solution)/shard_map/all_to_all | solution.py:300
  35.8 0.1 pad_add_fusion.where_ref
  35.9 10.1 %all-to-all-done.parts_ref = f32[8,64,128]{2,1,0:T(8,128)S(1)} async-done(((f32[8,64,128]{2,1,0:T(8,128)}), f32[8,64,128]{2,1,0:T(8,128)S(1)}, u32[]{:S(2)}, u32[]{:S(2)}) %all-to-all-start) | async-done | bytes 262176 | tf_op jit(solution)/shard_map/all_to_all | solution.py:300
  46.0 0.9 %moments.1 = (f32[16,128]{1,0:T(8,128)S(1)}, f32[16,128]{1,0:T(8,128)S(1)}) custom-call(s32[2]{0:T(128)S(1)} %pad_add_fusion.where_ref, f32[8,64,128]{2,1,0:T(8,128)S(1)} %all-to-all-done.parts_ref), custom_call_target="tpu_custom_call" | custom-call | flops 4194304 | bytes 1048576 | tf_op jit(solution)/shard_map/moments/pallas_call | solution.py:185
  46.9 2.7 %collective-permute-start.4 = (f32[16,128]{1,0:T(8,128)S(1)}, f32[16,128]{1,0:T(8,128)S(1)}, u32[]{:S(2)}, u32[]{:S(2)}) collective-permute-start(f32[16,128]{1,0:T(8,128)S(1)} %get-tuple-element.15), channel_id=1, source_target_pairs={{0,1},{1,0},{2,3},{3,2},{4,5},{5,4},{6,7},{7,6},{8,9},{9,8},{10,11... | collective-permute-start | bytes 24584 | tf_op jit(solution)/shard_map/ppermute | solution.py:278
  49.6 0.8 %collective-permute-done.4 = f32[16,128]{1,0:T(8,128)S(1)} collective-permute-done((f32[16,128]{1,0:T(8,128)S(1)}, f32[16,128]{1,0:T(8,128)S(1)}, u32[]{:S(2)}, u32[]{:S(2)}) %collective-permute-start.4) | collective-permute-done | bytes 8224 | tf_op jit(solution)/shard_map/ppermute | solution.py:278
  50.5 2.5 %collective-permute-start.7 = (f32[16,128]{1,0:T(8,128)S(1)}, f32[16,128]{1,0:T(8,128)S(1)}, u32[]{:S(2)}, u32[]{:S(2)}) collective-permute-start(f32[16,128]{1,0:T(8,128)S(1)} %add.16), channel_id=1, source_target_pairs={{0,192},{64,0},{128,64},{192,128},{1,193},{65,1},{129,65},{193,129... | collective-permute-start | bytes 24584 | tf_op jit(solution)/shard_map/ppermute | solution.py:278
  52.9 0.5 collective-permute-start.6
  53.5 0.6 collective-permute-start.5
  54.1 0.0 collective-permute-done.7
  54.1 2.9 %collective-permute-done.6 = f32[16,128]{1,0:T(8,128)S(1)} collective-permute-done((f32[16,128]{1,0:T(8,128)S(1)}, f32[16,128]{1,0:T(8,128)S(1)}, u32[]{:S(2)}, u32[]{:S(2)}) %collective-permute-start.6) | collective-permute-done | bytes 8224 | tf_op jit(solution)/shard_map/ppermute | solution.py:278
  56.9 0.2 collective-permute-done.5
  57.2 13.3 %all_to_all.10.refs_2_ = f32[32,16,128]{2,1,0:T(8,128)S(1)} all-to-all(f32[32,16,128]{2,1,0:T(8,128)S(1)} %broadcast_in_dim.10), channel_id=1, replica_groups=mesh['grp'=4,'z'=8,'y'=4,'core'=2] {'y','z'}, dimensions={0} | all-to-all | bytes 524288 | tf_op jit(solution)/shard_map/all_to_all | solution.py:306
  70.5 4.0 %collective-permute-start.8 = (f32[32,16,128]{2,1,0:T(8,128)S(1)}, f32[32,16,128]{2,1,0:T(8,128)S(1)}, u32[]{:S(2)}, u32[]{:S(2)}) collective-permute-start(f32[32,16,128]{2,1,0:T(8,128)S(1)} %all_to_all.10.refs_2_), channel_id=1, source_target_pairs={{0,1},{1,0},{2,3},{3,2},{4,5},{5,4},{6,7},{7,6},{8,9},{9,8},{10,11... | collective-permute-start | bytes 786440 | tf_op jit(solution)/shard_map/ppermute | solution.py:278
  74.5 1.2 %collective-permute-done.8.refs_3_ = f32[32,16,128]{2,1,0:T(8,128)S(1)} collective-permute-done((f32[32,16,128]{2,1,0:T(8,128)S(1)}, f32[32,16,128]{2,1,0:T(8,128)S(1)}, u32[]{:S(2)}, u32[]{:S(2)}) %collective-permute-start.8) | collective-permute-done | bytes 262176 | tf_op jit(solution)/shard_map/ppermute | solution.py:278
  75.6 0.0 copy-done.3
  75.6 0.0 copy-done.4
  75.6 3.6 %maps.1 = (f32[30,1024]{1,0:T(8,128)}, f32[1,1024]{1,0:T(1,128)}) custom-call(s32[1]{0:T(128)} %bitcast.refs_0_, s32[30]{0:T(128)S(1)} %copy-done.4, f32[32,16,128]{2,1,0:T(8,128)S(1)} %all_to_all.10.refs_2_, f32[32,16,128]{2,1,0:T(8,128)S(1)} %collective-permute-done.8.refs_3_, bf16[64,1024]{1,0:T(8,128)(2,1)S(1)} %bitcast.13), custom_call_target="tpu_custom_call" | custom-call | flops 268435456 | bytes 1048576 | tf_op jit(solution)/shard_map/maps/pallas_call | solution.py:266
  (3 shorter events, 0.0 us)
Async XLA Ops:
  0.7 0.9 %copy-start = (f32[128,32,8]{0,2,1:T(8,128)S(1)}, f32[128,32,8]{0,2,1:T(8,128)}, u32[]{:S(2)}) copy-start(f32[128,32,8]{0,2,1:T(8,128)} %param.5) | copy-start | bytes 393220
  1.6 0.9 %copy-start.2 = (bf16[1024,64]{0,1:T(8,128)(2,1)S(1)}, bf16[1024,64]{0,1:T(8,128)(2,1)}, u32[]{:S(2)}) copy-start(bf16[1024,64]{0,1:T(8,128)(2,1)} %param.6) | copy-start | bytes 393220
  2.5 8.9 %copy-start.1 = (f32[128,32,8]{0,2,1:T(8,128)S(1)}, f32[128,32,8]{0,2,1:T(8,128)}, u32[]{:S(2)}) copy-start(f32[128,32,8]{0,2,1:T(8,128)} %param.5) | copy-start | bytes 393220
  8.0 67.6 %copy-start.3 = (bf16[1024,64]{0,1:T(8,128)(2,1)S(1)}, bf16[1024,64]{0,1:T(8,128)(2,1)}, u32[]{:S(2)}) copy-start(bf16[1024,64]{0,1:T(8,128)(2,1)} %param.6) | copy-start | bytes 393220
  8.0 67.6 %copy-start.4 = (s32[30]{0:T(128)S(1)}, s32[30]{0:T(128)}, u32[]{:S(2)}) copy-start(s32[30]{0:T(128)} %refs_1_.1) | copy-start | bytes 364
  8.0 8.9 %collective-permute-start = (f32[4,8,32,128]{3,2,1,0:T(8,128)S(1)}, f32[4,8,32,128]{3,2,1,0:T(8,128)S(1)}, u32[]{:S(2)}, u32[]{:S(2)}) collective-permute-start(f32[4,8,32,128]{3,2,1,0:T(8,128)S(1)} %project.3), channel_id=1, source_target_pairs={{0,1},{1,0},{2,3},{3,2},{4,5},{5,4},{6,7},{7,6},{8,9},{9,8},{10,11... | collective-permute-start | bytes 1572872 | tf_op jit(solution)/shard_map/ppermute | solution.py:278
  17.5 7.2 %collective-permute-start.1 = (f32[9,32,128]{2,1,0:T(8,128)S(1)}, f32[9,32,128]{2,1,0:T(8,128)S(1)}, u32[]{:S(2)}, u32[]{:S(2)}) collective-permute-start(f32[9,32,128]{2,1,0:T(8,128)S(1)} %get-tuple-element.11), channel_id=1, source_target_pairs={{0,2},{2,4},{4,6},{6,0},{1,3},{3,5},{5,7},{7,1},{8,10},{10,12},{12... | collective-permute-start | bytes 442376 | tf_op jit(solution)/shard_map/ppermute | solution.py:278
  17.6 9.4 %collective-permute-start.2 = (f32[9,32,128]{2,1,0:T(8,128)S(1)}, f32[9,32,128]{2,1,0:T(8,128)S(1)}, u32[]{:S(2)}, u32[]{:S(2)}) collective-permute-start(f32[9,32,128]{2,1,0:T(8,128)S(1)} %get-tuple-element.12), channel_id=1, source_target_pairs={{0,4},{2,6},{4,0},{6,2},{1,5},{3,7},{5,1},{7,3},{8,12},{10,14},{12... | collective-permute-start | bytes 442376 | tf_op jit(solution)/shard_map/ppermute | solution.py:278
  19.7 8.0 %collective-permute-start.3 = (f32[9,32,128]{2,1,0:T(8,128)S(1)}, f32[9,32,128]{2,1,0:T(8,128)S(1)}, u32[]{:S(2)}, u32[]{:S(2)}) collective-permute-start(f32[9,32,128]{2,1,0:T(8,128)S(1)} %get-tuple-element.13), channel_id=1, source_target_pairs={{0,6},{2,0},{4,2},{6,4},{1,7},{3,1},{5,3},{7,5},{8,14},{10,8},{12,... | collective-permute-start | bytes 442376 | tf_op jit(solution)/shard_map/ppermute | solution.py:278
  28.4 17.6 %all-to-all-start = ((f32[8,64,128]{2,1,0:T(8,128)}), f32[8,64,128]{2,1,0:T(8,128)S(1)}, u32[]{:S(2)}, u32[]{:S(2)}) async-start(f32[8,64,128]{2,1,0:T(8,128)} %add_up.1), calls=%async_computation | async-start | bytes 524288 | tf_op jit(solution)/shard_map/all_to_all | solution.py:300
  46.9 3.5 %collective-permute-start.4 = (f32[16,128]{1,0:T(8,128)S(1)}, f32[16,128]{1,0:T(8,128)S(1)}, u32[]{:S(2)}, u32[]{:S(2)}) collective-permute-start(f32[16,128]{1,0:T(8,128)S(1)} %get-tuple-element.15), channel_id=1, source_target_pairs={{0,1},{1,0},{2,3},{3,2},{4,5},{5,4},{6,7},{7,6},{8,9},{9,8},{10,11... | collective-permute-start | bytes 24584 | tf_op jit(solution)/shard_map/ppermute | solution.py:278
  50.5 3.6 %collective-permute-start.7 = (f32[16,128]{1,0:T(8,128)S(1)}, f32[16,128]{1,0:T(8,128)S(1)}, u32[]{:S(2)}, u32[]{:S(2)}) collective-permute-start(f32[16,128]{1,0:T(8,128)S(1)} %add.16), channel_id=1, source_target_pairs={{0,192},{64,0},{128,64},{192,128},{1,193},{65,1},{129,65},{193,129... | collective-permute-start | bytes 24584 | tf_op jit(solution)/shard_map/ppermute | solution.py:278
  52.9 4.0 %collective-permute-start.6 = (f32[16,128]{1,0:T(8,128)S(1)}, f32[16,128]{1,0:T(8,128)S(1)}, u32[]{:S(2)}, u32[]{:S(2)}) collective-permute-start(f32[16,128]{1,0:T(8,128)S(1)} %add.16), channel_id=1, source_target_pairs={{0,128},{64,192},{128,0},{192,64},{1,129},{65,193},{129,1},{193,65... | collective-permute-start | bytes 24584 | tf_op jit(solution)/shard_map/ppermute | solution.py:278
  53.5 3.7 %collective-permute-start.5 = (f32[16,128]{1,0:T(8,128)S(1)}, f32[16,128]{1,0:T(8,128)S(1)}, u32[]{:S(2)}, u32[]{:S(2)}) collective-permute-start(f32[16,128]{1,0:T(8,128)S(1)} %add.16), channel_id=1, source_target_pairs={{0,64},{64,128},{128,192},{192,0},{1,65},{65,129},{129,193},{193,1... | collective-permute-start | bytes 24584 | tf_op jit(solution)/shard_map/ppermute | solution.py:278
  70.5 5.2 %collective-permute-start.8 = (f32[32,16,128]{2,1,0:T(8,128)S(1)}, f32[32,16,128]{2,1,0:T(8,128)S(1)}, u32[]{:S(2)}, u32[]{:S(2)}) collective-permute-start(f32[32,16,128]{2,1,0:T(8,128)S(1)} %all_to_all.10.refs_2_), channel_id=1, source_target_pairs={{0,1},{1,0},{2,3},{3,2},{4,5},{5,4},{6,7},{7,6},{8,9},{9,8},{10,11... | collective-permute-start | bytes 786440 | tf_op jit(solution)/shard_map/ppermute | solution.py:278

commit v5 on v4

--- a/solution.py
+++ b/solution.py
@@ -34,10 +34,7 @@
         for which in range(2):
             fetch(index, which).start()
 
-    turned = basis_ref[...].astype(F32).T.astype(BF16)
-    none = jnp.zeros_like(turned)
-    weights[0] = jnp.concatenate([turned, none], axis=1)
-    weights[1] = jnp.concatenate([none, turned], axis=1)
+    weights[...] = basis_ref[...].astype(F32).T.astype(BF16)
     block_of_row = lax.broadcasted_iota(jnp.int32, (256, lanes), 0) % blocks
     for block in range(blocks):
         spread[:, block * lanes : (block + 1) * lanes] = jnp.where(block_of_row == block, 1.0, 0.0).astype(BF16)
@@ -62,21 +59,20 @@
     masks = (own & (lane8 < 192), own & ((lane8 < 128) | (lane8 >= 192)))
     slot = lax.broadcasted_iota(jnp.int32, (slots, 2 * modes), 0)
     for index in range(chunks):
-        total = None
+        left, pieces = [], []
         for which in range(2):
             fetch(index, which).wait()
             first = which * packed + index * chunk
-            left = []
             for row in range(chunk):
                 for q in range(groups):
                     line = jnp.broadcast_to(scales3[q, pl.ds(base + first + row, 1), :], (8, 256))
                     left.append(jnp.where(masks[q % 2], line, 0.0))
-            left = jnp.concatenate(left, axis=0).astype(BF16)
-            scale = jnp.dot(left, spread[...], preferred_element_type=F32)
-            piece = buffer[first : first + chunk].astype(F32).reshape(chunk * slots, cells)
-            dequant = (piece * scale).astype(BF16)
-            product = jnp.dot(dequant, weights[which], preferred_element_type=F32)
-            total = product if total is None else total + product
+            pieces.append(buffer[first : first + chunk].astype(F32).reshape(chunk * slots, cells))
+        left = jnp.concatenate(left, axis=0).astype(BF16)
+        scale = jnp.dot(left, spread[...], preferred_element_type=F32)
+        dequant = (jnp.concatenate(pieces, axis=0) * scale).astype(BF16)
+        product = jnp.dot(dequant, weights[...], preferred_element_type=F32)
+        total = jnp.concatenate([product[: chunk * slots], product[chunk * slots :]], axis=1)
         tiles = []
         for row in range(chunk):
             tile = total[row * slots : (row + 1) * slots]
@@ -86,11 +82,11 @@
             place = lax.rem(group + 4 - where_ref[1], 4)
             out_ref[place, :, index * chunk : (index + 1) * chunk, :] = turned[8 * group : 8 * group + 8]
 
-def project(where, fields, scales, basis):
+def project(where, fields, scales, basis, room=52):
     rows, slots, cells = fields.shape
     modes = basis.shape[0]
     packed = rows // 4
-    chunk = 8
+    chunk = 16
     chunks = packed // chunk
     return pl.pallas_call(
         functools.partial(project_kernel, chunk),
@@ -99,12 +95,12 @@
         out_shape=jax.ShapeDtypeStruct((4, slots // 4, packed, 2 * modes), F32),
         scratch_shapes=[
             pltpu.VMEM((rows // 2, slots, cells), BF16),
-            pltpu.VMEM((2, cells, 2 * modes), BF16),
+            pltpu.VMEM((cells, modes), BF16),
             pltpu.VMEM((256, cells), BF16),
             pltpu.VMEM((slots // 8, rows, 256), F32),
             pltpu.SemaphoreType.DMA((chunks, 2)),
         ],
-        compiler_params=pltpu.CompilerParams(vmem_limit_bytes=52 << 20),
+        compiler_params=pltpu.CompilerParams(vmem_limit_bytes=room << 20),
         cost_estimate=pl.CostEstimate(
             flops=rows * slots * cells * modes, bytes_accessed=rows * slots * cells, transcendentals=0
         ),
@@ -200,78 +196,105 @@
     return high, middle, (rest - middle.astype(F32)).astype(BF16)
 
 
-def maps_kernel(rows_total, cell_total, half_ref, order_ref, mine_ref, other_ref, basis_ref, maps_ref, total_ref):
+def right_sides(phi):
+    none = jnp.zeros_like(phi)
+    return (
+        jnp.concatenate([phi, phi, phi, none], axis=0),
+        jnp.concatenate([phi, phi, none, phi], axis=0),
+    )
+
+
+def quadratic(piece, rights, rows):
+    count = piece.shape[0]
+    cells = rights[0].shape[1]
+    flat = piece.reshape(count * 16, 128)
+    lane = lax.broadcasted_iota(jnp.int32, flat.shape, 1)
+    high = flat.astype(BF16).astype(F32)
+    rest = flat - high
+    middle = rest.astype(BF16).astype(F32)
+    low = (rest - middle).astype(BF16)
+    turned = pltpu.roll(middle, 64, 1)
+    result = None
+    for side, right in enumerate(rights):
+        front = jnp.where((lane < 64) == (side == 0), high, turned).astype(BF16)
+        left = jnp.concatenate([front, low], axis=1)
+        product = jnp.dot(left, right, preferred_element_type=F32).reshape(count, 16, cells)
+        term = jnp.sum(product * rows[side][None], axis=1)
+        result = term if result is None else result + term
+    return result
+
+
+def half_rows(phi32, second):
+    return [
+        jnp.where(second, phi32[32 + 16 * side : 48 + 16 * side], phi32[16 * side : 16 + 16 * side])
+        for side in range(2)
+    ]
+
+
+def own_maps_kernel(half_ref, mine_ref, basis_ref, out_ref):
+    rights = right_sides(basis_ref[...])
+    rows = half_rows(basis_ref[...].astype(F32), half_ref[0] == 1)
+    for start in range(0, out_ref.shape[0], 8):
+        out_ref[start : start + 8] = quadratic(mine_ref[start : start + 8], rights, rows)
+
+
+def own_maps(half, mine, basis):
+    return pl.pallas_call(
+        own_maps_kernel,
+        in_specs=[SMEM, VMEM, VMEM],
+        out_specs=VMEM,
+        out_shape=jax.ShapeDtypeStruct((mine.shape[0], basis.shape[1]), F32),
+        compiler_params=pltpu.CompilerParams(vmem_limit_bytes=32 << 20),
+        cost_estimate=pl.CostEstimate(flops=1 << 28, bytes_accessed=1 << 20, transcendentals=0),
+        name="own_maps",
+    )(half, mine, basis)
+
+
+def maps_kernel(rows_total, cell_total, half_ref, order_ref, own_ref, mine_ref, other_ref, basis_ref, maps_ref, total_ref):
     half = half_ref[0]
-    mine, other = mine_ref[...], other_ref[...]
-    halves = (jnp.where(half == 0, mine, other), jnp.where(half == 0, other, mine))
-    slots = mine.shape[0]
-    modes, cells = basis_ref.shape
-    phi = basis_ref[...]
-    none = jnp.zeros_like(phi)
-    right_first = jnp.concatenate([phi, phi, phi, none], axis=0)
-    right_second = jnp.concatenate([phi, phi, none, phi], axis=0)
-    phi32 = phi.astype(F32)
-
-    def quadratic(pieces):
-        count = pieces[0].shape[0]
-        result = None
-        for part, piece in enumerate(pieces):
-            flat = piece.reshape(count * 16, 128)
-            lane = lax.broadcasted_iota(jnp.int32, flat.shape, 1)
-            high = flat.astype(BF16).astype(F32)
-            rest = flat - high
-            middle = rest.astype(BF16).astype(F32)
-            low = (rest - middle).astype(BF16)
-            turned = pltpu.roll(middle, 64, 1)
-            for side, right in enumerate((right_first, right_second)):
-                front = jnp.where((lane < 64) == (side == 0), high, turned).astype(BF16)
-                left = jnp.concatenate([front, low], axis=1)
-                product = jnp.dot(left, right, preferred_element_type=F32).reshape(count, 16, cells)
-                first = 32 * part + 16 * side
-                term = jnp.sum(product * phi32[None, first : first + 16], axis=1)
-                result = term if result is None else result + term
-        return result
-
-    group = 8
-    for start in range(0, slots, group):
-        found = cell_total / rows_total * quadratic([h[start : start + group] for h in halves])
-        for slot in range(max(start, 2), start + group):
+    rights = right_sides(basis_ref[...])
+    phi32 = basis_ref[...].astype(F32)
+    rows = half_rows(phi32, half == 0)
+    slots = other_ref.shape[0]
+    for start in range(0, slots, 8):
+        found = own_ref[start : start + 8] + quadratic(other_ref[start : start + 8], rights, rows)
+        found = cell_total / rows_total * found
+        for slot in range(max(start, 2), start + 8):
             maps_ref[pl.ds(order_ref[slot - 2], 1), :] = found[slot - start : slot - start + 1]
 
-    both = [h[0] + h[1] for h in halves]
-    sums = both[1][0:1, :64]
-    low = both[1][1:2, :64]
+    mine = mine_ref[0] + mine_ref[1]
+    other = other_ref[0] + other_ref[1]
+    upper, lower = jnp.where(half == 0, mine, other), jnp.where(half == 0, other, mine)
+    sums = lower[0:1, :64]
+    low = lower[1:2, :64]
     lane1 = lax.broadcasted_iota(jnp.int32, sums.shape, 1)
     sums = jnp.where(lane1 < 32, sums, jnp.concatenate([low[:, 32:], low[:, :32]], axis=1))
     average = sums / (2.0 * rows_total)
     outer = lax.dot_general(average, average, (((0,), (0,)), ((), ())), precision=HIGHEST, preferred_element_type=F32)
-    lane = lax.broadcasted_iota(jnp.int32, both[0].shape, 1)
+    lane = lax.broadcasted_iota(jnp.int32, upper.shape, 1)
     column = jnp.where(lane < 64, lane, lane - 64)
     weight = jnp.where(column < 32, 1.0, 2.0)
     outer_upper = jnp.concatenate([outer[:16], outer[16:32]], axis=1)
     outer_lower = jnp.concatenate([outer[32:48], outer[48:]], axis=1)
-    upper = (both[0] / (2.0 * rows_total) - outer_upper) * weight
-    lower = jnp.where(column < 32, 0.0, both[1] / (2.0 * rows_total) - outer_lower)
-    total = quadratic([upper[None], lower[None]])
+    upper = (upper / (2.0 * rows_total) - outer_upper) * weight
+    lower = jnp.where(column < 32, 0.0, lower / (2.0 * rows_total) - outer_lower)
+    total = quadratic(upper[None], rights, [phi32[:16], phi32[16:32]])
+    total = total + quadratic(lower[None], rights, [phi32[32:48], phi32[48:]])
     total_ref[...] = cell_total * total
 
 
-def make_maps(rows_total, cell_total, half, order, mine, other, basis):
+def make_maps(rows_total, cell_total, half, order, own, mine, other, basis):
     cells = basis.shape[1]
     params = order.shape[0]
-
-    def kernel(*refs):
-        maps_kernel(rows_total, cell_total, *refs)
-
-    return pl.pallas_call(
-        kernel,
-        in_specs=[SMEM, SMEM, VMEM, VMEM, VMEM],
+    return pl.pallas_call(
+        functools.partial(maps_kernel, rows_total, cell_total),
+        in_specs=[SMEM, SMEM, VMEM, VMEM, VMEM, VMEM],
         out_specs=(VMEM, VMEM),
         out_shape=(jax.ShapeDtypeStruct((params, cells), F32), jax.ShapeDtypeStruct((1, cells), F32)),
         compiler_params=pltpu.CompilerParams(vmem_limit_bytes=32 << 20),
         cost_estimate=pl.CostEstimate(flops=1 << 28, bytes_accessed=1 << 20, transcendentals=0),
         name="maps",
-    )(half, order, mine, other, basis)
+    )(half, order, own, mine, other, basis)
 
 
 def shifted(value, axis, size, shift):
@@ -291,7 +314,7 @@
     basis = pod_basis.T
 
     height = lax.axis_index("y").astype(jnp.int32)
-    theirs = project(jnp.stack([1 - core, height]), fields, by_slot, basis)
+    theirs = project(jnp.stack([1 - core, height]), fields, by_slot, basis, 56)
     got = shifted(theirs, "core", 2, 1)
     where = jnp.stack([core, height])
     ours = project(where, fields, by_slot, basis)
@@ -305,7 +328,8 @@
     copies = jnp.broadcast_to(piece[None], (slots,) + piece.shape)
     mine = lax.all_to_all(copies, ("y", "z"), 0, 0, tiled=True)
     other = shifted(mine, "core", 2, 1)
-    sobol, total = make_maps(rows_total, cell_total, core[None], param_order, mine, other, basis)
+    own = own_maps(core[None], mine, basis)
+    sobol, total = make_maps(rows_total, cell_total, core[None], param_order, own, mine, other, basis)
     return sobol, total.reshape(cells)
 
 

time: 79.5 us -> 78.1 us (0.982)
  local copies, waits for them, and re-layouts: 1.85 us -> 0.04 us
  Pallas kernels: 16.7 us -> 17.7 us
  waiting for transfers between devices: 22.1 us -> 21.1 us
    unnamed x10 -> x6, local copies, waits for them, and re-layouts: 1.82 us -> 0.02 us
    ppermute x9, waiting for transfers between devices: 12 us -> 10.9 us  [shifted(): lax.ppermute(value, axis, [(i, (i + shift) % size) for i in range(size)])]
    pallas_call x1 -> x2, Pallas kernels: 3.58 us -> 3.78 us  [the longest x1 2.74 us: make_maps(): pl.pallas_call(functools.partial(maps_kernel, rows_total, cell_total), in...]
  transfers between devices with their start and end apart: 10 -> 10, of which waited for: 8 -> 8; matrix products, arithmetic and copies ran while one was open for 0% -> 0% of each run, Pallas kernels for 7% -> 8%
where the time goes in v5:
time: 78.1 us; the launch traced here: 77.9 us
  starting transfers between devices  24.3 us (31%)
  waiting for transfers between devices  21.1 us (27%)
  Pallas kernels  17.7 us (23%)
  blocking collectives  13.3 us (17%)
    ppermute x9, starting transfers between devices, shifted(): lax.ppermute(value, axis, [(i, (i + shift) % size) for i in range(size)])  16.9 us
    all_to_all x1, blocking collectives, on_device(): mine = lax.all_to_all(copies, ('y', 'z'), 0, 0, tiled=True)  13.3 us
    pallas_call x2, Pallas kernels, project(): pl.pallas_call(functools.partial(project_kernel, chunk), in_specs=[SMEM,...  11.6 us
    ppermute x9, waiting for transfers between devices, shifted(): lax.ppermute(value, axis, [(i, (i + shift) % size) for i in range(size)])  10.9 us
    all_to_all x1, waiting for transfers between devices, on_device(): parts = lax.all_to_all(parts, 'z', 0, 0, tiled=True)  10.1 us
    all_to_all x1, starting transfers between devices, on_device(): parts = lax.all_to_all(parts, 'z', 0, 0, tiled=True)  7.39 us
    pallas_call x1, Pallas kernels, make_maps(): pl.pallas_call(functools.partial(maps_kernel, rows_total, cell_total), in...  2.74 us
  transfers between devices with their start and end apart: 10, of which 8 were waited for; matrix products, arithmetic and copies ran while one was open for 0% of the time, Pallas kernels for 8%

profile of v5, /device:TPU:1, one launch (start us, length us, event | category | flops | bytes accessed | tf_op | source)
XLA Modules:
  0.0 77.9 jit_solution(8580881864249959044)
XLA Ops:
  0.6 0.0 copy-start.1
  0.6 0.0 copy-start
  0.7 0.6 pad_add_fusion.2.where_ref
  1.3 6.4 %project.3 = f32[4,8,32,128]{3,2,1,0:T(8,128)} custom-call(s32[2]{0:T(128)} %pad_add_fusion.2.where_ref, bf16[128,32,1024]{2,1,0:T(8,128)(2,1)} %fields_ref.3, f32[256,128]{1,0:T(8,128)} %bitcast.9, bf16[64,1024]{1,0:T(8,128)(2,1)} %bitcast.11), custom_call_target="tpu_custom_call" | custom-call | flops 268435456 | bytes 4194304 | tf_op jit(solution)/shard_map/project/pallas_call | solution.py:91
  7.7 0.0 copy-start.2
  7.7 3.3 %collective-permute-start = (f32[4,8,32,128]{3,2,1,0:T(8,128)}, f32[4,8,32,128]{3,2,1,0:T(8,128)S(1)}, u32[]{:S(2)}, u32[]{:S(2)}) collective-permute-start(f32[4,8,32,128]{3,2,1,0:T(8,128)} %project.3), channel_id=1, source_target_pairs={{0,1},{1,0},{2,3},{3,2},{4,5},{5,4},{6,7},{7,6},{8,9},{9,8},{10,11... | collective-permute-start | bytes 1572872 | tf_op jit(solution)/shard_map/ppermute | solution.py:301
  11.1 0.1 pad_add_fusion.1.where_ref
  11.1 0.0 copy-done.1
  11.1 0.0 copy-done
  11.1 5.2 %project.2.ours_ref = f32[4,8,32,128]{3,2,1,0:T(8,128)S(1)} custom-call(s32[2]{0:T(128)S(1)} %pad_add_fusion.1.where_ref, bf16[128,32,1024]{2,1,0:T(8,128)(2,1)} %fields_ref.3, f32[256,128]{1,0:T(8,128)S(1)} %bitcast.10, bf16[64,1024]{1,0:T(8,128)(2,1)S(1)} %bitcast.12), custom_call_target="tpu_custom_call" | custom-call | flops 268435456 | bytes 4194304 | tf_op jit(solution)/shard_map/project/pallas_call | solution.py:91
  16.3 0.0 collective-permute-done.got_ref
  16.4 0.6 combine.1
  17.0 0.1 collective-permute-start.1
  17.1 2.2 %collective-permute-start.2 = (f32[9,32,128]{2,1,0:T(8,128)S(1)}, f32[9,32,128]{2,1,0:T(8,128)S(1)}, u32[]{:S(2)}, u32[]{:S(2)}) collective-permute-start(f32[9,32,128]{2,1,0:T(8,128)S(1)} %get-tuple-element.12), channel_id=1, source_target_pairs={{0,4},{2,6},{4,0},{6,2},{1,5},{3,7},{5,1},{7,3},{8,12},{10,14},{12... | collective-permute-start | bytes 442376 | tf_op jit(solution)/shard_map/ppermute | solution.py:301
  19.2 1.1 %collective-permute-start.3 = (f32[9,32,128]{2,1,0:T(8,128)S(1)}, f32[9,32,128]{2,1,0:T(8,128)S(1)}, u32[]{:S(2)}, u32[]{:S(2)}) collective-permute-start(f32[9,32,128]{2,1,0:T(8,128)S(1)} %get-tuple-element.13), channel_id=1, source_target_pairs={{0,6},{2,0},{4,2},{6,4},{1,7},{3,1},{5,3},{7,5},{8,14},{10,8},{12,... | collective-permute-start | bytes 442376 | tf_op jit(solution)/shard_map/ppermute | solution.py:301
  20.3 3.8 %collective-permute-done.1.refs_1_ = f32[9,32,128]{2,1,0:T(8,128)S(1)} collective-permute-done((f32[9,32,128]{2,1,0:T(8,128)S(1)}, f32[9,32,128]{2,1,0:T(8,128)S(1)}, u32[]{:S(2)}, u32[]{:S(2)}) %collective-permute-start.1) | collective-permute-done | bytes 147488 | tf_op jit(solution)/shard_map/ppermute | solution.py:301
  24.1 2.3 %collective-permute-done.2.refs_2_ = f32[9,32,128]{2,1,0:T(8,128)S(1)} collective-permute-done((f32[9,32,128]{2,1,0:T(8,128)S(1)}, f32[9,32,128]{2,1,0:T(8,128)S(1)}, u32[]{:S(2)}, u32[]{:S(2)}) %collective-permute-start.2) | collective-permute-done | bytes 147488 | tf_op jit(solution)/shard_map/ppermute | solution.py:301
  26.4 0.8 collective-permute-done.3.refs_3_
  27.2 0.7 add_up.1
  27.9 7.4 %all-to-all-start = ((f32[8,64,128]{2,1,0:T(8,128)}), f32[8,64,128]{2,1,0:T(8,128)S(1)}, u32[]{:S(2)}, u32[]{:S(2)}) async-start(f32[8,64,128]{2,1,0:T(8,128)} %add_up.1), calls=%async_computation | async-start | bytes 524288 | tf_op jit(solution)/shard_map/all_to_all | solution.py:323
  35.3 0.1 pad_add_fusion.where_ref
  35.4 10.1 %all-to-all-done.parts_ref = f32[8,64,128]{2,1,0:T(8,128)S(1)} async-done(((f32[8,64,128]{2,1,0:T(8,128)}), f32[8,64,128]{2,1,0:T(8,128)S(1)}, u32[]{:S(2)}, u32[]{:S(2)}) %all-to-all-start) | async-done | bytes 262176 | tf_op jit(solution)/shard_map/all_to_all | solution.py:323
  45.5 0.9 %moments.1 = (f32[16,128]{1,0:T(8,128)S(1)}, f32[16,128]{1,0:T(8,128)S(1)}) custom-call(s32[2]{0:T(128)S(1)} %pad_add_fusion.where_ref, f32[8,64,128]{2,1,0:T(8,128)S(1)} %all-to-all-done.parts_ref), custom_call_target="tpu_custom_call" | custom-call | flops 4194304 | bytes 1048576 | tf_op jit(solution)/shard_map/moments/pallas_call | solution.py:181
  46.4 2.7 %collective-permute-start.4 = (f32[16,128]{1,0:T(8,128)S(1)}, f32[16,128]{1,0:T(8,128)S(1)}, u32[]{:S(2)}, u32[]{:S(2)}) collective-permute-start(f32[16,128]{1,0:T(8,128)S(1)} %get-tuple-element.15), channel_id=1, source_target_pairs={{0,1},{1,0},{2,3},{3,2},{4,5},{5,4},{6,7},{7,6},{8,9},{9,8},{10,11... | collective-permute-start | bytes 24584 | tf_op jit(solution)/shard_map/ppermute | solution.py:301
  49.1 0.8 %collective-permute-done.4 = f32[16,128]{1,0:T(8,128)S(1)} collective-permute-done((f32[16,128]{1,0:T(8,128)S(1)}, f32[16,128]{1,0:T(8,128)S(1)}, u32[]{:S(2)}, u32[]{:S(2)}) %collective-permute-start.4) | collective-permute-done | bytes 8224 | tf_op jit(solution)/shard_map/ppermute | solution.py:301
  50.0 2.5 %collective-permute-start.7 = (f32[16,128]{1,0:T(8,128)S(1)}, f32[16,128]{1,0:T(8,128)S(1)}, u32[]{:S(2)}, u32[]{:S(2)}) collective-permute-start(f32[16,128]{1,0:T(8,128)S(1)} %add.16), channel_id=1, source_target_pairs={{0,192},{64,0},{128,64},{192,128},{1,193},{65,1},{129,65},{193,129... | collective-permute-start | bytes 24584 | tf_op jit(solution)/shard_map/ppermute | solution.py:301
  52.4 0.5 collective-permute-start.6
  53.0 0.6 collective-permute-start.5
  53.6 0.0 collective-permute-done.7
  53.6 2.9 %collective-permute-done.6 = f32[16,128]{1,0:T(8,128)S(1)} collective-permute-done((f32[16,128]{1,0:T(8,128)S(1)}, f32[16,128]{1,0:T(8,128)S(1)}, u32[]{:S(2)}, u32[]{:S(2)}) %collective-permute-start.6) | collective-permute-done | bytes 8224 | tf_op jit(solution)/shard_map/ppermute | solution.py:301
  56.4 0.2 collective-permute-done.5
  56.7 13.3 %all_to_all.10.mine_ref = f32[32,16,128]{2,1,0:T(8,128)S(1)} all-to-all(f32[32,16,128]{2,1,0:T(8,128)S(1)} %broadcast_in_dim.5), channel_id=1, replica_groups=mesh['grp'=4,'z'=8,'y'=4,'core'=2] {'y','z'}, dimensions={0} | all-to-all | bytes 524288 | tf_op jit(solution)/shard_map/all_to_all | solution.py:329
  70.0 4.0 %collective-permute-start.8 = (f32[32,16,128]{2,1,0:T(8,128)S(1)}, f32[32,16,128]{2,1,0:T(8,128)S(1)}, u32[]{:S(2)}, u32[]{:S(2)}) collective-permute-start(f32[32,16,128]{2,1,0:T(8,128)S(1)} %all_to_all.10.mine_ref), channel_id=1, source_target_pairs={{0,1},{1,0},{2,3},{3,2},{4,5},{5,4},{6,7},{7,6},{8,9},{9,8},{10,11... | collective-permute-start | bytes 786440 | tf_op jit(solution)/shard_map/ppermute | solution.py:301
  74.0 1.0 %own_maps.1.own_ref = f32[32,1024]{1,0:T(8,128)S(1)} custom-call(s32[1]{0:T(128)} %bitcast.half_ref, f32[32,16,128]{2,1,0:T(8,128)S(1)} %all_to_all.10.mine_ref, bf16[64,1024]{1,0:T(8,128)(2,1)S(1)} %bitcast.13), custom_call_target="tpu_custom_call" | custom-call | flops 268435456 | bytes 1048576 | tf_op jit(solution)/shard_map/own_maps/pallas_call | solution.py:242
  75.0 0.1 collective-permute-done.8.other_ref
  75.1 0.0 copy-done.2
  75.1 2.7 %maps.1 = (f32[30,1024]{1,0:T(8,128)}, f32[1,1024]{1,0:T(1,128)}) custom-call(s32[1]{0:T(128)} %bitcast.half_ref, s32[30]{0:T(128)S(1)} %copy-done.2, f32[32,1024]{1,0:T(8,128)S(1)} %own_maps.1.own_ref, f32[32,16,128]{2,1,0:T(8,128)S(1)} %all_to_all.10.mine_ref, f32[32,16,128]{2,1,0:T(8,128)S(1)} %collective-permute-done.8.other_ref, ...), custom_call_target="tpu_custom_call" | custom-call | flops 268435456 | bytes 1048576 | tf_op jit(solution)/shard_map/maps/pallas_call | solution.py:289
  (3 shorter events, 0.0 us)
Async XLA Ops:
  0.6 10.5 %copy-start.1 = (bf16[1024,64]{0,1:T(8,128)(2,1)S(1)}, bf16[1024,64]{0,1:T(8,128)(2,1)}, u32[]{:S(2)}) copy-start(bf16[1024,64]{0,1:T(8,128)(2,1)} %param.6) | copy-start | bytes 393220
  0.6 10.5 %copy-start = (f32[128,32,8]{0,2,1:T(8,128)S(1)}, f32[128,32,8]{0,2,1:T(8,128)}, u32[]{:S(2)}) copy-start(f32[128,32,8]{0,2,1:T(8,128)} %param.5) | copy-start | bytes 393220
  7.7 67.4 %copy-start.2 = (s32[30]{0:T(128)S(1)}, s32[30]{0:T(128)}, u32[]{:S(2)}) copy-start(s32[30]{0:T(128)} %order_ref.1) | copy-start | bytes 364
  7.7 8.6 %collective-permute-start = (f32[4,8,32,128]{3,2,1,0:T(8,128)}, f32[4,8,32,128]{3,2,1,0:T(8,128)S(1)}, u32[]{:S(2)}, u32[]{:S(2)}) collective-permute-start(f32[4,8,32,128]{3,2,1,0:T(8,128)} %project.3), channel_id=1, source_target_pairs={{0,1},{1,0},{2,3},{3,2},{4,5},{5,4},{6,7},{7,6},{8,9},{9,8},{10,11... | collective-permute-start | bytes 1572872 | tf_op jit(solution)/shard_map/ppermute | solution.py:301
  17.0 7.2 %collective-permute-start.1 = (f32[9,32,128]{2,1,0:T(8,128)S(1)}, f32[9,32,128]{2,1,0:T(8,128)S(1)}, u32[]{:S(2)}, u32[]{:S(2)}) collective-permute-start(f32[9,32,128]{2,1,0:T(8,128)S(1)} %get-tuple-element.11), channel_id=1, source_target_pairs={{0,2},{2,4},{4,6},{6,0},{1,3},{3,5},{5,7},{7,1},{8,10},{10,12},{12... | collective-permute-start | bytes 442376 | tf_op jit(solution)/shard_map/ppermute | solution.py:301
  17.1 9.4 %collective-permute-start.2 = (f32[9,32,128]{2,1,0:T(8,128)S(1)}, f32[9,32,128]{2,1,0:T(8,128)S(1)}, u32[]{:S(2)}, u32[]{:S(2)}) collective-permute-start(f32[9,32,128]{2,1,0:T(8,128)S(1)} %get-tuple-element.12), channel_id=1, source_target_pairs={{0,4},{2,6},{4,0},{6,2},{1,5},{3,7},{5,1},{7,3},{8,12},{10,14},{12... | collective-permute-start | bytes 442376 | tf_op jit(solution)/shard_map/ppermute | solution.py:301
  19.2 8.0 %collective-permute-start.3 = (f32[9,32,128]{2,1,0:T(8,128)S(1)}, f32[9,32,128]{2,1,0:T(8,128)S(1)}, u32[]{:S(2)}, u32[]{:S(2)}) collective-permute-start(f32[9,32,128]{2,1,0:T(8,128)S(1)} %get-tuple-element.13), channel_id=1, source_target_pairs={{0,6},{2,0},{4,2},{6,4},{1,7},{3,1},{5,3},{7,5},{8,14},{10,8},{12,... | collective-permute-start | bytes 442376 | tf_op jit(solution)/shard_map/ppermute | solution.py:301
  27.9 17.6 %all-to-all-start = ((f32[8,64,128]{2,1,0:T(8,128)}), f32[8,64,128]{2,1,0:T(8,128)S(1)}, u32[]{:S(2)}, u32[]{:S(2)}) async-start(f32[8,64,128]{2,1,0:T(8,128)} %add_up.1), calls=%async_computation | async-start | bytes 524288 | tf_op jit(solution)/shard_map/all_to_all | solution.py:323
  46.4 3.5 %collective-permute-start.4 = (f32[16,128]{1,0:T(8,128)S(1)}, f32[16,128]{1,0:T(8,128)S(1)}, u32[]{:S(2)}, u32[]{:S(2)}) collective-permute-start(f32[16,128]{1,0:T(8,128)S(1)} %get-tuple-element.15), channel_id=1, source_target_pairs={{0,1},{1,0},{2,3},{3,2},{4,5},{5,4},{6,7},{7,6},{8,9},{9,8},{10,11... | collective-permute-start | bytes 24584 | tf_op jit(solution)/shard_map/ppermute | solution.py:301
  50.0 3.6 %collective-permute-start.7 = (f32[16,128]{1,0:T(8,128)S(1)}, f32[16,128]{1,0:T(8,128)S(1)}, u32[]{:S(2)}, u32[]{:S(2)}) collective-permute-start(f32[16,128]{1,0:T(8,128)S(1)} %add.16), channel_id=1, source_target_pairs={{0,192},{64,0},{128,64},{192,128},{1,193},{65,1},{129,65},{193,129... | collective-permute-start | bytes 24584 | tf_op jit(solution)/shard_map/ppermute | solution.py:301
  52.4 4.0 %collective-permute-start.6 = (f32[16,128]{1,0:T(8,128)S(1)}, f32[16,128]{1,0:T(8,128)S(1)}, u32[]{:S(2)}, u32[]{:S(2)}) collective-permute-start(f32[16,128]{1,0:T(8,128)S(1)} %add.16), channel_id=1, source_target_pairs={{0,128},{64,192},{128,0},{192,64},{1,129},{65,193},{129,1},{193,65... | collective-permute-start | bytes 24584 | tf_op jit(solution)/shard_map/ppermute | solution.py:301
  53.0 3.7 %collective-permute-start.5 = (f32[16,128]{1,0:T(8,128)S(1)}, f32[16,128]{1,0:T(8,128)S(1)}, u32[]{:S(2)}, u32[]{:S(2)}) collective-permute-start(f32[16,128]{1,0:T(8,128)S(1)} %add.16), channel_id=1, source_target_pairs={{0,64},{64,128},{128,192},{192,0},{1,65},{65,129},{129,193},{193,1... | collective-permute-start | bytes 24584 | tf_op jit(solution)/shard_map/ppermute | solution.py:301
  70.0 5.2 %collective-permute-start.8 = (f32[32,16,128]{2,1,0:T(8,128)S(1)}, f32[32,16,128]{2,1,0:T(8,128)S(1)}, u32[]{:S(2)}, u32[]{:S(2)}) collective-permute-start(f32[32,16,128]{2,1,0:T(8,128)S(1)} %all_to_all.10.mine_ref), channel_id=1, source_target_pairs={{0,1},{1,0},{2,3},{3,2},{4,5},{5,4},{6,7},{7,6},{8,9},{9,8},{10,11... | collective-permute-start | bytes 786440 | tf_op jit(solution)/shard_map/ppermute | solution.py:301

commit v6 on v5

--- a/solution.py
+++ b/solution.py
@@ -14,7 +14,7 @@
 SMEM = pl.BlockSpec(memory_space=pltpu.SMEM)
 
 
-def project_kernel(chunk, where_ref, fields_ref, scale_ref, basis_ref, out_ref, buffer, weights, spread, scales3, sems):
+def project_kernel(chunk, half_ref, height_ref, fields_ref, scale_ref, basis_ref, out_ref, buffer, weights, spread, scales3, sems):
     rows, slots, cells = buffer.shape
     packed = rows // 2
     modes = basis_ref.shape[0]
@@ -22,7 +22,7 @@
     blocks = cells // lanes
     chunks = packed // chunk
     groups = slots // 8
-    base = where_ref[0] * rows
+    base = half_ref[0] * rows
 
     def fetch(index, which):
         first = which * packed + index * chunk
@@ -79,10 +79,10 @@
             tiles.append(tile - jnp.where(slot >= 2, jnp.broadcast_to(tile[:1], tile.shape), 0.0))
         turned = jnp.swapaxes(jnp.stack(tiles), 0, 1)
         for group in range(4):
-            place = lax.rem(group + 4 - where_ref[1], 4)
+            place = lax.rem(group + 4 - height_ref[0], 4)
             out_ref[place, :, index * chunk : (index + 1) * chunk, :] = turned[8 * group : 8 * group + 8]
 
-def project(where, fields, scales, basis, room=52):
+def project(half, height, fields, scales, basis, room):
     rows, slots, cells = fields.shape
     modes = basis.shape[0]
     packed = rows // 4
@@ -90,7 +90,7 @@
     chunks = packed // chunk
     return pl.pallas_call(
         functools.partial(project_kernel, chunk),
-        in_specs=[SMEM, pl.BlockSpec(memory_space=pl.ANY), VMEM, VMEM],
+        in_specs=[SMEM, SMEM, pl.BlockSpec(memory_space=pl.ANY), VMEM, VMEM],
         out_specs=VMEM,
         out_shape=jax.ShapeDtypeStruct((4, slots // 4, packed, 2 * modes), F32),
         scratch_shapes=[
@@ -105,18 +105,18 @@
             flops=rows * slots * cells * modes, bytes_accessed=rows * slots * cells, transcendentals=0
         ),
         name="project",
-    )(where, fields, scales, basis)
-
-
-def combine_kernel(where_ref, ours_ref, got_ref, *outs):
-    place = lax.rem(4 - where_ref[1], 4)
+    )(half, height, fields, scales, basis)
+
+
+def combine_kernel(height_ref, ours_ref, got_ref, *outs):
+    place = lax.rem(4 - height_ref[0], 4)
     second = ours_ref[place, 1] + got_ref[place, 1]
     for group, out in enumerate(outs):
         out[:8] = ours_ref[group] + got_ref[group]
         out[8] = second
 
 
-def combine(where, ours, got):
+def combine(height, ours, got):
     groups, count, packed, lanes = ours.shape
     out = jax.ShapeDtypeStruct((count + 1, packed, lanes), F32)
     return pl.pallas_call(
@@ -127,7 +127,7 @@
         compiler_params=pltpu.CompilerParams(vmem_limit_bytes=16 << 20),
         cost_estimate=pl.CostEstimate(flops=1 << 18, bytes_accessed=1 << 21, transcendentals=0),
         name="combine",
-    )(where, ours, got)
+    )(height, ours, got)
 
 
 def add_up_kernel(*refs):
@@ -153,8 +153,8 @@
     )(*parts)
 
 
-def moments_kernel(where_ref, parts_ref, keep_ref, send_ref):
-    slot, half = where_ref[0], where_ref[1]
+def moments_kernel(slot_ref, half_ref, parts_ref, keep_ref, send_ref):
+    slot, half = slot_ref[0], half_ref[0]
     both = parts_ref[0]
     for source in range(1, parts_ref.shape[0]):
         both = both + parts_ref[source]
@@ -176,17 +176,17 @@
     send_ref[...] = jnp.where(half == 0, lower, upper)
 
 
-def moments(where, parts):
+def moments(slot, half, parts):
     out = jax.ShapeDtypeStruct((16, 128), F32)
     return pl.pallas_call(
         moments_kernel,
-        in_specs=[SMEM, VMEM],
+        in_specs=[SMEM, SMEM, VMEM],
         out_specs=(VMEM, VMEM),
         out_shape=(out, out),
         compiler_params=pltpu.CompilerParams(vmem_limit_bytes=16 << 20),
         cost_estimate=pl.CostEstimate(flops=1 << 22, bytes_accessed=1 << 20, transcendentals=0),
         name="moments",
-    )(where, parts)
+    )(slot, half, parts)
 
 
 def three(value):
@@ -219,7 +219,7 @@
         front = jnp.where((lane < 64) == (side == 0), high, turned).astype(BF16)
         left = jnp.concatenate([front, low], axis=1)
         product = jnp.dot(left, right, preferred_element_type=F32).reshape(count, 16, cells)
-        term = jnp.sum(product * rows[side][None], axis=1)
+        term = jnp.sum(product * rows[side], axis=1)
         result = term if result is None else result + term
     return result
 
@@ -233,7 +233,7 @@
 
 def own_maps_kernel(half_ref, mine_ref, basis_ref, out_ref):
     rights = right_sides(basis_ref[...])
-    rows = half_rows(basis_ref[...].astype(F32), half_ref[0] == 1)
+    rows = [r[None] for r in half_rows(basis_ref[...].astype(F32), half_ref[0] == 1)]
     for start in range(0, out_ref.shape[0], 8):
         out_ref[start : start + 8] = quadratic(mine_ref[start : start + 8], rights, rows)
 
@@ -255,13 +255,6 @@
     rights = right_sides(basis_ref[...])
     phi32 = basis_ref[...].astype(F32)
     rows = half_rows(phi32, half == 0)
-    slots = other_ref.shape[0]
-    for start in range(0, slots, 8):
-        found = own_ref[start : start + 8] + quadratic(other_ref[start : start + 8], rights, rows)
-        found = cell_total / rows_total * found
-        for slot in range(max(start, 2), start + 8):
-            maps_ref[pl.ds(order_ref[slot - 2], 1), :] = found[slot - start : slot - start + 1]
-
     mine = mine_ref[0] + mine_ref[1]
     other = other_ref[0] + other_ref[1]
     upper, lower = jnp.where(half == 0, mine, other), jnp.where(half == 0, other, mine)
@@ -269,8 +262,8 @@
     low = lower[1:2, :64]
     lane1 = lax.broadcasted_iota(jnp.int32, sums.shape, 1)
     sums = jnp.where(lane1 < 32, sums, jnp.concatenate([low[:, 32:], low[:, :32]], axis=1))
-    average = sums / (2.0 * rows_total)
-    outer = lax.dot_general(average, average, (((0,), (0,)), ((), ())), precision=HIGHEST, preferred_element_type=F32)
+    average = jnp.broadcast_to(sums / (2.0 * rows_total), (64, 64))
+    outer = average.T * average
     lane = lax.broadcasted_iota(jnp.int32, upper.shape, 1)
     column = jnp.where(lane < 64, lane, lane - 64)
     weight = jnp.where(column < 32, 1.0, 2.0)
@@ -278,9 +271,21 @@
     outer_lower = jnp.concatenate([outer[32:48], outer[48:]], axis=1)
     upper = (upper / (2.0 * rows_total) - outer_upper) * weight
     lower = jnp.where(column < 32, 0.0, lower / (2.0 * rows_total) - outer_lower)
-    total = quadratic(upper[None], rights, [phi32[:16], phi32[16:32]])
-    total = total + quadratic(lower[None], rights, [phi32[32:48], phi32[48:]])
-    total_ref[...] = cell_total * total
+
+    for start in range(0, other_ref.shape[0], 8):
+        if start == 0:
+            piece = jnp.concatenate([upper[None], lower[None], other_ref[2:8]], axis=0)
+            first = [
+                jnp.stack([phi32[16 * side : 16 * side + 16], phi32[32 + 16 * side : 48 + 16 * side]] + [rows[side]] * 6)
+                for side in range(2)
+            ]
+            found = quadratic(piece, rights, first)
+            total_ref[...] = cell_total * (found[0:1] + found[1:2])
+        else:
+            found = quadratic(other_ref[start : start + 8], rights, [r[None] for r in rows])
+        found = cell_total / rows_total * (own_ref[start : start + 8] + found)
+        for slot in range(max(start, 2), start + 8):
+            maps_ref[pl.ds(order_ref[slot - 2], 1), :] = found[slot - start : slot - start + 1]
 
 
 def make_maps(rows_total, cell_total, half, order, own, mine, other, basis):
@@ -313,16 +318,15 @@
     by_slot = jnp.transpose(scales, (1, 2, 0)).reshape(slots * blocks, rows)
     basis = pod_basis.T
 
-    height = lax.axis_index("y").astype(jnp.int32)
-    theirs = project(jnp.stack([1 - core, height]), fields, by_slot, basis, 56)
+    height = lax.axis_index("y").astype(jnp.int32)[None]
+    theirs = project((1 - core)[None], height, fields, by_slot, basis, 56)
     got = shifted(theirs, "core", 2, 1)
-    where = jnp.stack([core, height])
-    ours = project(where, fields, by_slot, basis)
-    pieces = combine(where, ours, got)
-    parts = add_up([pieces[0]] + [shifted(pieces[s], "y", sizes["y"], s) for s in range(1, sizes["y"])])
+    ours = project(core[None], height, fields, by_slot, basis, 52)
+    pieces = combine(height, ours, got)
+    parts = add_up([pieces[0]] + [shifted(pieces[s], "y", sizes["y"], s) for s in (2, 1, 3)])
     parts = lax.all_to_all(parts, "z", 0, 0, tiled=True)
 
-    keep, send = moments(jnp.stack([slot, core]), parts)
+    keep, send = moments(slot[None], core[None], parts)
     piece = keep + shifted(send, "core", 2, 1)
     piece = piece + sum(shifted(piece, "grp", sizes["grp"], s) for s in range(1, sizes["grp"]))
     copies = jnp.broadcast_to(piece[None], (slots,) + piece.shape)

time: 78.1 us -> 75.2 us (0.963)
  Pallas kernels: 17.7 us -> 15.9 us
    all_to_all x1, starting transfers between devices: 7.39 us -> 6.44 us  [on_device(): parts = lax.all_to_all(parts, 'z', 0, 0, tiled=True)]
  transfers between devices with their start and end apart: 10 -> 10, of which waited for: 8 -> 7; matrix products, arithmetic and copies ran while one was open for 0% -> 0% of each run, Pallas kernels for 8% -> 8%
where the time goes in v6:
time: 75.2 us; the launch traced here: 74.9 us
  starting transfers between devices  24 us (32%)
  waiting for transfers between devices  20.8 us (28%)
  Pallas kernels  15.9 us (21%)
  blocking collectives  13.5 us (18%)
    ppermute x9, starting transfers between devices, shifted(): lax.ppermute(value, axis, [(i, (i + shift) % size) for i in range(size)])  17.6 us
    all_to_all x1, blocking collectives, on_device(): mine = lax.all_to_all(copies, ('y', 'z'), 0, 0, tiled=True)  13.5 us
    pallas_call x2, Pallas kernels, project(): pl.pallas_call(functools.partial(project_kernel, chunk), in_specs=[SMEM,...  11.1 us
    ppermute x9, waiting for transfers between devices, shifted(): lax.ppermute(value, axis, [(i, (i + shift) % size) for i in range(size)])  10.6 us
    all_to_all x1, waiting for transfers between devices, on_device(): parts = lax.all_to_all(parts, 'z', 0, 0, tiled=True)  10.2 us
    all_to_all x1, starting transfers between devices, on_device(): parts = lax.all_to_all(parts, 'z', 0, 0, tiled=True)  6.44 us
    pallas_call x1, Pallas kernels, make_maps(): pl.pallas_call(functools.partial(maps_kernel, rows_total, cell_total), in...  2.49 us
  transfers between devices with their start and end apart: 10, of which 7 were waited for; matrix products, arithmetic and copies ran while one was open for 0% of the time, Pallas kernels for 8%

profile of v6, /device:TPU:1, one launch (start us, length us, event | category | flops | bytes accessed | tf_op | source)
XLA Modules:
  0.0 74.9 jit_solution(6467161661944238062)
XLA Ops:
  0.6 0.0 copy-start.1
  0.6 0.0 copy-start
  0.7 6.5 %project.3 = f32[4,8,32,128]{3,2,1,0:T(8,128)} custom-call(s32[1]{0:T(128)} %bitcast.6.half_ref, s32[1]{0:T(128)} %bitcast.2.height_ref, bf16[128,32,1024]{2,1,0:T(8,128)(2,1)} %fields_ref.3, f32[256,128]{1,0:T(8,128)} %bitcast.9, bf16[64,1024]{1,0:T(8,128)(2,1)} %bitcast.11), custom_call_target="tpu_custom_call" | custom-call | flops 268435456 | bytes 4194304 | tf_op jit(solution)/shard_map/project/pallas_call | solution.py:91
  7.1 0.0 copy-start.2
  7.1 3.3 %collective-permute-start = (f32[4,8,32,128]{3,2,1,0:T(8,128)}, f32[4,8,32,128]{3,2,1,0:T(8,128)S(1)}, u32[]{:S(2)}, u32[]{:S(2)}) collective-permute-start(f32[4,8,32,128]{3,2,1,0:T(8,128)} %project.3), channel_id=1, source_target_pairs={{0,1},{1,0},{2,3},{3,2},{4,5},{5,4},{6,7},{7,6},{8,9},{9,8},{10,11... | collective-permute-start | bytes 1572872 | tf_op jit(solution)/shard_map/ppermute | solution.py:306
  10.5 0.0 copy-done.1
  10.5 0.0 copy-done
  10.5 4.7 %project.2.ours_ref = f32[4,8,32,128]{3,2,1,0:T(8,128)S(1)} custom-call(s32[1]{0:T(128)} %bitcast.half_ref, s32[1]{0:T(128)} %bitcast.2.height_ref, bf16[128,32,1024]{2,1,0:T(8,128)(2,1)} %fields_ref.3, f32[256,128]{1,0:T(8,128)S(1)} %bitcast.10, bf16[64,1024]{1,0:T(8,128)(2,1)S(1)} %bitcast.12), custom_call_target="tpu_custom_call" | custom-call | flops 268435456 | bytes 4194304 | tf_op jit(solution)/shard_map/project/pallas_call | solution.py:91
  15.1 0.0 collective-permute-done.got_ref
  15.2 0.1 combine.1
  15.2 1.3 %collective-permute-start.1 = (f32[9,32,128]{2,1,0:T(8,128)S(1)}, f32[9,32,128]{2,1,0:T(8,128)S(1)}, u32[]{:S(2)}, u32[]{:S(2)}) collective-permute-start(f32[9,32,128]{2,1,0:T(8,128)S(1)} %get-tuple-element.11), channel_id=1, source_target_pairs={{0,4},{2,6},{4,0},{6,2},{1,5},{3,7},{5,1},{7,3},{8,12},{10,14},{12... | collective-permute-start | bytes 442376 | tf_op jit(solution)/shard_map/ppermute | solution.py:306
  16.5 0.4 collective-permute-start.2
  16.9 2.3 %collective-permute-start.3 = (f32[9,32,128]{2,1,0:T(8,128)S(1)}, f32[9,32,128]{2,1,0:T(8,128)S(1)}, u32[]{:S(2)}, u32[]{:S(2)}) collective-permute-start(f32[9,32,128]{2,1,0:T(8,128)S(1)} %get-tuple-element.13), channel_id=1, source_target_pairs={{0,6},{2,0},{4,2},{6,4},{1,7},{3,1},{5,3},{7,5},{8,14},{10,8},{12,... | collective-permute-start | bytes 442376 | tf_op jit(solution)/shard_map/ppermute | solution.py:306
  19.2 3.1 %collective-permute-done.1.refs_1_ = f32[9,32,128]{2,1,0:T(8,128)S(1)} collective-permute-done((f32[9,32,128]{2,1,0:T(8,128)S(1)}, f32[9,32,128]{2,1,0:T(8,128)S(1)}, u32[]{:S(2)}, u32[]{:S(2)}) %collective-permute-start.1) | collective-permute-done | bytes 147488 | tf_op jit(solution)/shard_map/ppermute | solution.py:306
  22.3 3.5 %collective-permute-done.2.refs_2_ = f32[9,32,128]{2,1,0:T(8,128)S(1)} collective-permute-done((f32[9,32,128]{2,1,0:T(8,128)S(1)}, f32[9,32,128]{2,1,0:T(8,128)S(1)}, u32[]{:S(2)}, u32[]{:S(2)}) %collective-permute-start.2) | collective-permute-done | bytes 147488 | tf_op jit(solution)/shard_map/ppermute | solution.py:306
  25.8 0.0 collective-permute-done.3.refs_3_
  25.8 0.7 add_up.1
  26.5 6.4 %all-to-all-start = ((f32[8,64,128]{2,1,0:T(8,128)}), f32[8,64,128]{2,1,0:T(8,128)S(1)}, u32[]{:S(2)}, u32[]{:S(2)}) async-start(f32[8,64,128]{2,1,0:T(8,128)} %add_up.1), calls=%async_computation | async-start | bytes 524288 | tf_op jit(solution)/shard_map/all_to_all | solution.py:327
  33.0 10.2 %all-to-all-done.parts_ref = f32[8,64,128]{2,1,0:T(8,128)S(1)} async-done(((f32[8,64,128]{2,1,0:T(8,128)}), f32[8,64,128]{2,1,0:T(8,128)S(1)}, u32[]{:S(2)}, u32[]{:S(2)}) %all-to-all-start) | async-done | bytes 262176 | tf_op jit(solution)/shard_map/all_to_all | solution.py:327
  43.1 0.4 moments.1
  43.5 2.7 %collective-permute-start.4 = (f32[16,128]{1,0:T(8,128)S(1)}, f32[16,128]{1,0:T(8,128)S(1)}, u32[]{:S(2)}, u32[]{:S(2)}) collective-permute-start(f32[16,128]{1,0:T(8,128)S(1)} %get-tuple-element.15), channel_id=1, source_target_pairs={{0,1},{1,0},{2,3},{3,2},{4,5},{5,4},{6,7},{7,6},{8,9},{9,8},{10,11... | collective-permute-start | bytes 24584 | tf_op jit(solution)/shard_map/ppermute | solution.py:306
  46.2 0.8 %collective-permute-done.4 = f32[16,128]{1,0:T(8,128)S(1)} collective-permute-done((f32[16,128]{1,0:T(8,128)S(1)}, f32[16,128]{1,0:T(8,128)S(1)}, u32[]{:S(2)}, u32[]{:S(2)}) %collective-permute-start.4) | collective-permute-done | bytes 8224 | tf_op jit(solution)/shard_map/ppermute | solution.py:306
  47.1 2.5 %collective-permute-start.7 = (f32[16,128]{1,0:T(8,128)S(1)}, f32[16,128]{1,0:T(8,128)S(1)}, u32[]{:S(2)}, u32[]{:S(2)}) collective-permute-start(f32[16,128]{1,0:T(8,128)S(1)} %add.16), channel_id=1, source_target_pairs={{0,192},{64,0},{128,64},{192,128},{1,193},{65,1},{129,65},{193,129... | collective-permute-start | bytes 24584 | tf_op jit(solution)/shard_map/ppermute | solution.py:306
  49.5 0.5 collective-permute-start.6
  50.1 0.6 collective-permute-start.5
  50.7 0.0 collective-permute-done.7
  50.7 2.9 %collective-permute-done.6 = f32[16,128]{1,0:T(8,128)S(1)} collective-permute-done((f32[16,128]{1,0:T(8,128)S(1)}, f32[16,128]{1,0:T(8,128)S(1)}, u32[]{:S(2)}, u32[]{:S(2)}) %collective-permute-start.6) | collective-permute-done | bytes 8224 | tf_op jit(solution)/shard_map/ppermute | solution.py:306
  53.5 0.2 collective-permute-done.5
  53.8 13.5 %all_to_all.10.mine_ref = f32[32,16,128]{2,1,0:T(8,128)S(1)} all-to-all(f32[32,16,128]{2,1,0:T(8,128)S(1)} %broadcast_in_dim.25), channel_id=1, replica_groups=mesh['grp'=4,'z'=8,'y'=4,'core'=2] {'y','z'}, dimensions={0} | all-to-all | bytes 524288 | tf_op jit(solution)/shard_map/all_to_all | solution.py:333
  67.3 4.0 %collective-permute-start.8 = (f32[32,16,128]{2,1,0:T(8,128)S(1)}, f32[32,16,128]{2,1,0:T(8,128)S(1)}, u32[]{:S(2)}, u32[]{:S(2)}) collective-permute-start(f32[32,16,128]{2,1,0:T(8,128)S(1)} %all_to_all.10.mine_ref), channel_id=1, source_target_pairs={{0,1},{1,0},{2,3},{3,2},{4,5},{5,4},{6,7},{7,6},{8,9},{9,8},{10,11... | collective-permute-start | bytes 786440 | tf_op jit(solution)/shard_map/ppermute | solution.py:306
  71.3 1.0 %own_maps.1.own_ref = f32[32,1024]{1,0:T(8,128)S(1)} custom-call(s32[1]{0:T(128)} %bitcast.half_ref, f32[32,16,128]{2,1,0:T(8,128)S(1)} %all_to_all.10.mine_ref, bf16[64,1024]{1,0:T(8,128)(2,1)S(1)} %bitcast.13), custom_call_target="tpu_custom_call" | custom-call | flops 268435456 | bytes 1048576 | tf_op jit(solution)/shard_map/own_maps/pallas_call | solution.py:242
  72.3 0.1 collective-permute-done.8.other_ref
  72.4 0.0 copy-done.2
  72.4 2.5 %maps.1 = (f32[30,1024]{1,0:T(8,128)}, f32[1,1024]{1,0:T(1,128)}) custom-call(s32[1]{0:T(128)} %bitcast.half_ref, s32[30]{0:T(128)S(1)} %copy-done.2, f32[32,1024]{1,0:T(8,128)S(1)} %own_maps.1.own_ref, f32[32,16,128]{2,1,0:T(8,128)S(1)} %all_to_all.10.mine_ref, f32[32,16,128]{2,1,0:T(8,128)S(1)} %collective-permute-done.8.other_ref, ...), custom_call_target="tpu_custom_call" | custom-call | flops 268435456 | bytes 1048576 | tf_op jit(solution)/shard_map/maps/pallas_call | solution.py:294
  (3 shorter events, 0.0 us)
Async XLA Ops:
  0.6 9.8 %copy-start.1 = (bf16[1024,64]{0,1:T(8,128)(2,1)S(1)}, bf16[1024,64]{0,1:T(8,128)(2,1)}, u32[]{:S(2)}) copy-start(bf16[1024,64]{0,1:T(8,128)(2,1)} %param.6) | copy-start | bytes 393220
  0.6 9.8 %copy-start = (f32[128,32,8]{0,2,1:T(8,128)S(1)}, f32[128,32,8]{0,2,1:T(8,128)}, u32[]{:S(2)}) copy-start(f32[128,32,8]{0,2,1:T(8,128)} %param.5) | copy-start | bytes 393220
  7.1 65.3 %copy-start.2 = (s32[30]{0:T(128)S(1)}, s32[30]{0:T(128)}, u32[]{:S(2)}) copy-start(s32[30]{0:T(128)} %order_ref.1) | copy-start | bytes 364
  7.1 8.0 %collective-permute-start = (f32[4,8,32,128]{3,2,1,0:T(8,128)}, f32[4,8,32,128]{3,2,1,0:T(8,128)S(1)}, u32[]{:S(2)}, u32[]{:S(2)}) collective-permute-start(f32[4,8,32,128]{3,2,1,0:T(8,128)} %project.3), channel_id=1, source_target_pairs={{0,1},{1,0},{2,3},{3,2},{4,5},{5,4},{6,7},{7,6},{8,9},{9,8},{10,11... | collective-permute-start | bytes 1572872 | tf_op jit(solution)/shard_map/ppermute | solution.py:306
  15.2 7.1 %collective-permute-start.1 = (f32[9,32,128]{2,1,0:T(8,128)S(1)}, f32[9,32,128]{2,1,0:T(8,128)S(1)}, u32[]{:S(2)}, u32[]{:S(2)}) collective-permute-start(f32[9,32,128]{2,1,0:T(8,128)S(1)} %get-tuple-element.11), channel_id=1, source_target_pairs={{0,4},{2,6},{4,0},{6,2},{1,5},{3,7},{5,1},{7,3},{8,12},{10,14},{12... | collective-permute-start | bytes 442376 | tf_op jit(solution)/shard_map/ppermute | solution.py:306
  16.5 9.3 %collective-permute-start.2 = (f32[9,32,128]{2,1,0:T(8,128)S(1)}, f32[9,32,128]{2,1,0:T(8,128)S(1)}, u32[]{:S(2)}, u32[]{:S(2)}) collective-permute-start(f32[9,32,128]{2,1,0:T(8,128)S(1)} %get-tuple-element.12), channel_id=1, source_target_pairs={{0,2},{2,4},{4,6},{6,0},{1,3},{3,5},{5,7},{7,1},{8,10},{10,12},{12... | collective-permute-start | bytes 442376 | tf_op jit(solution)/shard_map/ppermute | solution.py:306
  16.9 8.9 %collective-permute-start.3 = (f32[9,32,128]{2,1,0:T(8,128)S(1)}, f32[9,32,128]{2,1,0:T(8,128)S(1)}, u32[]{:S(2)}, u32[]{:S(2)}) collective-permute-start(f32[9,32,128]{2,1,0:T(8,128)S(1)} %get-tuple-element.13), channel_id=1, source_target_pairs={{0,6},{2,0},{4,2},{6,4},{1,7},{3,1},{5,3},{7,5},{8,14},{10,8},{12,... | collective-permute-start | bytes 442376 | tf_op jit(solution)/shard_map/ppermute | solution.py:306
  26.5 16.6 %all-to-all-start = ((f32[8,64,128]{2,1,0:T(8,128)}), f32[8,64,128]{2,1,0:T(8,128)S(1)}, u32[]{:S(2)}, u32[]{:S(2)}) async-start(f32[8,64,128]{2,1,0:T(8,128)} %add_up.1), calls=%async_computation | async-start | bytes 524288 | tf_op jit(solution)/shard_map/all_to_all | solution.py:327
  43.5 3.5 %collective-permute-start.4 = (f32[16,128]{1,0:T(8,128)S(1)}, f32[16,128]{1,0:T(8,128)S(1)}, u32[]{:S(2)}, u32[]{:S(2)}) collective-permute-start(f32[16,128]{1,0:T(8,128)S(1)} %get-tuple-element.15), channel_id=1, source_target_pairs={{0,1},{1,0},{2,3},{3,2},{4,5},{5,4},{6,7},{7,6},{8,9},{9,8},{10,11... | collective-permute-start | bytes 24584 | tf_op jit(solution)/shard_map/ppermute | solution.py:306
  47.1 3.6 %collective-permute-start.7 = (f32[16,128]{1,0:T(8,128)S(1)}, f32[16,128]{1,0:T(8,128)S(1)}, u32[]{:S(2)}, u32[]{:S(2)}) collective-permute-start(f32[16,128]{1,0:T(8,128)S(1)} %add.16), channel_id=1, source_target_pairs={{0,192},{64,0},{128,64},{192,128},{1,193},{65,1},{129,65},{193,129... | collective-permute-start | bytes 24584 | tf_op jit(solution)/shard_map/ppermute | solution.py:306
  49.5 4.0 %collective-permute-start.6 = (f32[16,128]{1,0:T(8,128)S(1)}, f32[16,128]{1,0:T(8,128)S(1)}, u32[]{:S(2)}, u32[]{:S(2)}) collective-permute-start(f32[16,128]{1,0:T(8,128)S(1)} %add.16), channel_id=1, source_target_pairs={{0,128},{64,192},{128,0},{192,64},{1,129},{65,193},{129,1},{193,65... | collective-permute-start | bytes 24584 | tf_op jit(solution)/shard_map/ppermute | solution.py:306
  50.1 3.7 %collective-permute-start.5 = (f32[16,128]{1,0:T(8,128)S(1)}, f32[16,128]{1,0:T(8,128)S(1)}, u32[]{:S(2)}, u32[]{:S(2)}) collective-permute-start(f32[16,128]{1,0:T(8,128)S(1)} %add.16), channel_id=1, source_target_pairs={{0,64},{64,128},{128,192},{192,0},{1,65},{65,129},{129,193},{193,1... | collective-permute-start | bytes 24584 | tf_op jit(solution)/shard_map/ppermute | solution.py:306
  67.3 5.2 %collective-permute-start.8 = (f32[32,16,128]{2,1,0:T(8,128)S(1)}, f32[32,16,128]{2,1,0:T(8,128)S(1)}, u32[]{:S(2)}, u32[]{:S(2)}) collective-permute-start(f32[32,16,128]{2,1,0:T(8,128)S(1)} %all_to_all.10.mine_ref), channel_id=1, source_target_pairs={{0,1},{1,0},{2,3},{3,2},{4,5},{5,4},{6,7},{7,6},{8,9},{9,8},{10,11... | collective-permute-start | bytes 786440 | tf_op jit(solution)/shard_map/ppermute | solution.py:306

commit v7 on v6

--- a/solution.py
+++ b/solution.py
@@ -14,7 +14,10 @@
 SMEM = pl.BlockSpec(memory_space=pltpu.SMEM)
 
 
-def project_kernel(chunk, half_ref, height_ref, fields_ref, scale_ref, basis_ref, out_ref, buffer, weights, spread, scales3, sems):
+def project_kernel(
+    chunk, half_ref, height_ref, fields_ref, scale_in, basis_in, out_ref,
+    buffer, scale_ref, basis_ref, weights, spread, scales3, scale_rows, dequant, sems, small_sems,
+):
     rows, slots, cells = buffer.shape
     packed = rows // 2
     modes = basis_ref.shape[0]
@@ -30,14 +33,22 @@
             fields_ref.at[pl.ds(base + first, chunk)], buffer.at[pl.ds(first, chunk)], sems.at[index, which]
         )
 
+    small = [
+        pltpu.make_async_copy(scale_in, scale_ref, small_sems.at[0]),
+        pltpu.make_async_copy(basis_in, basis_ref, small_sems.at[1]),
+    ]
+    for copy in small:
+        copy.start()
     for index in range(chunks):
         for which in range(2):
             fetch(index, which).start()
 
-    weights[...] = basis_ref[...].astype(F32).T.astype(BF16)
     block_of_row = lax.broadcasted_iota(jnp.int32, (256, lanes), 0) % blocks
     for block in range(blocks):
         spread[:, block * lanes : (block + 1) * lanes] = jnp.where(block_of_row == block, 1.0, 0.0).astype(BF16)
+    for copy in small:
+        copy.wait()
+    weights[...] = basis_ref[...].astype(F32).T.astype(BF16)
     by_row = scale_ref[...].T
     high = by_row.astype(BF16).astype(F32)
     rest = by_row - high
@@ -58,20 +69,33 @@
     own = (lane8 % 64) // 8 == slot8
     masks = (own & (lane8 < 192), own & ((lane8 < 128) | (lane8 >= 192)))
     slot = lax.broadcasted_iota(jnp.int32, (slots, 2 * modes), 0)
+    few = 4
+    wide = 256
     for index in range(chunks):
-        left, pieces = [], []
         for which in range(2):
             fetch(index, which).wait()
             first = which * packed + index * chunk
-            for row in range(chunk):
-                for q in range(groups):
-                    line = jnp.broadcast_to(scales3[q, pl.ds(base + first + row, 1), :], (8, 256))
-                    left.append(jnp.where(masks[q % 2], line, 0.0))
-            pieces.append(buffer[first : first + chunk].astype(F32).reshape(chunk * slots, cells))
-        left = jnp.concatenate(left, axis=0).astype(BF16)
-        scale = jnp.dot(left, spread[...], preferred_element_type=F32)
-        dequant = (jnp.concatenate(pieces, axis=0) * scale).astype(BF16)
-        product = jnp.dot(dequant, weights[...], preferred_element_type=F32)
+            for row in range(0, chunk, few):
+                left = []
+                for line_row in range(first + row, first + row + few):
+                    for q in range(groups):
+                        line = jnp.broadcast_to(scales3[q, pl.ds(base + line_row, 1), :], (8, 256))
+                        left.append(jnp.where(masks[q % 2], line, 0.0))
+                scale_rows[(which * chunk + row) * slots : (which * chunk + row + few) * slots] = jnp.concatenate(
+                    left, axis=0
+                ).astype(BF16)
+        for column in range(0, cells, wide):
+            for which in range(2):
+                first = which * packed + index * chunk
+                for row in range(0, chunk, few):
+                    place = slice((which * chunk + row) * slots, (which * chunk + row + few) * slots)
+                    scale = jnp.dot(
+                        scale_rows[place], spread[:, column : column + wide], preferred_element_type=F32
+                    )
+                    piece = buffer[first + row : first + row + few, :, column : column + wide]
+                    piece = piece.astype(F32).reshape(few * slots, wide)
+                    dequant[place, column : column + wide] = (piece * scale).astype(BF16)
+        product = jnp.dot(dequant[...], weights[...], preferred_element_type=F32)
         total = jnp.concatenate([product[: chunk * slots], product[chunk * slots :]], axis=1)
         tiles = []
         for row in range(chunk):
@@ -90,15 +114,20 @@
     chunks = packed // chunk
     return pl.pallas_call(
         functools.partial(project_kernel, chunk),
-        in_specs=[SMEM, SMEM, pl.BlockSpec(memory_space=pl.ANY), VMEM, VMEM],
+        in_specs=[SMEM, SMEM] + [pl.BlockSpec(memory_space=pl.ANY)] * 3,
         out_specs=VMEM,
         out_shape=jax.ShapeDtypeStruct((4, slots // 4, packed, 2 * modes), F32),
         scratch_shapes=[
             pltpu.VMEM((rows // 2, slots, cells), BF16),
+            pltpu.VMEM(scales.shape, F32),
+            pltpu.VMEM(basis.shape, BF16),
             pltpu.VMEM((cells, modes), BF16),
             pltpu.VMEM((256, cells), BF16),
             pltpu.VMEM((slots // 8, rows, 256), F32),
+            pltpu.VMEM((2 * chunk * slots, 256), BF16),
+            pltpu.VMEM((2 * chunk * slots, cells), BF16),
             pltpu.SemaphoreType.DMA((chunks, 2)),
+            pltpu.SemaphoreType.DMA((2,)),
         ],
         compiler_params=pltpu.CompilerParams(vmem_limit_bytes=room << 20),
         cost_estimate=pl.CostEstimate(

time: 75.2 us -> 75.1 us (level)
  no operation moved by 1% of the time
where the time goes in v7:
time: 75.1 us; the launch traced here: 74.9 us
  starting transfers between devices  24 us (32%)
  waiting for transfers between devices  20.9 us (28%)
  Pallas kernels  15.6 us (21%)
  blocking collectives  13.7 us (18%)
    ppermute x9, starting transfers between devices, shifted(): lax.ppermute(value, axis, [(i, (i + shift) % size) for i in range(size)])  17.6 us
    all_to_all x1, blocking collectives, on_device(): mine = lax.all_to_all(copies, ('y', 'z'), 0, 0, tiled=True)  13.7 us
    pallas_call x2, Pallas kernels, project(): pl.pallas_call(functools.partial(project_kernel, chunk), in_specs=[SMEM,...  10.9 us
    ppermute x9, waiting for transfers between devices, shifted(): lax.ppermute(value, axis, [(i, (i + shift) % size) for i in range(size)])  10.7 us
    all_to_all x1, waiting for transfers between devices, on_device(): parts = lax.all_to_all(parts, 'z', 0, 0, tiled=True)  10.2 us
    all_to_all x1, starting transfers between devices, on_device(): parts = lax.all_to_all(parts, 'z', 0, 0, tiled=True)  6.43 us
    pallas_call x1, Pallas kernels, make_maps(): pl.pallas_call(functools.partial(maps_kernel, rows_total, cell_total), in...  2.49 us
  transfers between devices with their start and end apart: 10, of which 7 were waited for; matrix products, arithmetic and copies ran while one was open for 0% of the time, Pallas kernels for 8%

profile of v7, /device:TPU:1, one launch (start us, length us, event | category | flops | bytes accessed | tf_op | source)
XLA Modules:
  0.0 74.9 jit_solution(10875191778343260008)
XLA Ops:
  0.6 0.0 copy-start.1
  0.6 0.0 copy-start
  0.7 6.1 %project.3 = f32[4,8,32,128]{3,2,1,0:T(8,128)} custom-call(s32[1]{0:T(128)} %bitcast.6.half_ref, s32[1]{0:T(128)} %bitcast.2.height_ref, bf16[128,32,1024]{2,1,0:T(8,128)(2,1)} %fields_ref.3, f32[256,128]{1,0:T(8,128)} %bitcast.9, bf16[64,1024]{1,0:T(8,128)(2,1)} %bitcast.11), custom_call_target="tpu_custom_call" | custom-call | flops 268435456 | bytes 4194304 | tf_op jit(solution)/shard_map/project/pallas_call | solution.py:115
  6.8 0.0 copy-start.2
  6.8 3.4 %collective-permute-start = (f32[4,8,32,128]{3,2,1,0:T(8,128)}, f32[4,8,32,128]{3,2,1,0:T(8,128)S(1)}, u32[]{:S(2)}, u32[]{:S(2)}) collective-permute-start(f32[4,8,32,128]{3,2,1,0:T(8,128)} %project.3), channel_id=1, source_target_pairs={{0,1},{1,0},{2,3},{3,2},{4,5},{5,4},{6,7},{7,6},{8,9},{9,8},{10,11... | collective-permute-start | bytes 1572872 | tf_op jit(solution)/shard_map/ppermute | solution.py:335
  10.1 0.0 copy-done.1
  10.2 0.0 copy-done
  10.2 4.8 %project.2.ours_ref = f32[4,8,32,128]{3,2,1,0:T(8,128)S(1)} custom-call(s32[1]{0:T(128)} %bitcast.half_ref, s32[1]{0:T(128)} %bitcast.2.height_ref, bf16[128,32,1024]{2,1,0:T(8,128)(2,1)} %fields_ref.3, f32[256,128]{1,0:T(8,128)S(1)} %bitcast.10, bf16[64,1024]{1,0:T(8,128)(2,1)S(1)} %bitcast.12), custom_call_target="tpu_custom_call" | custom-call | flops 268435456 | bytes 4194304 | tf_op jit(solution)/shard_map/project/pallas_call | solution.py:115
  14.9 0.0 collective-permute-done.got_ref
  15.0 0.1 combine.1
  15.0 1.3 %collective-permute-start.1 = (f32[9,32,128]{2,1,0:T(8,128)S(1)}, f32[9,32,128]{2,1,0:T(8,128)S(1)}, u32[]{:S(2)}, u32[]{:S(2)}) collective-permute-start(f32[9,32,128]{2,1,0:T(8,128)S(1)} %get-tuple-element.11), channel_id=1, source_target_pairs={{0,4},{2,6},{4,0},{6,2},{1,5},{3,7},{5,1},{7,3},{8,12},{10,14},{12... | collective-permute-start | bytes 442376 | tf_op jit(solution)/shard_map/ppermute | solution.py:335
  16.3 0.4 collective-permute-start.2
  16.7 2.3 %collective-permute-start.3 = (f32[9,32,128]{2,1,0:T(8,128)S(1)}, f32[9,32,128]{2,1,0:T(8,128)S(1)}, u32[]{:S(2)}, u32[]{:S(2)}) collective-permute-start(f32[9,32,128]{2,1,0:T(8,128)S(1)} %get-tuple-element.13), channel_id=1, source_target_pairs={{0,6},{2,0},{4,2},{6,4},{1,7},{3,1},{5,3},{7,5},{8,14},{10,8},{12,... | collective-permute-start | bytes 442376 | tf_op jit(solution)/shard_map/ppermute | solution.py:335
  19.0 3.1 %collective-permute-done.1.refs_1_ = f32[9,32,128]{2,1,0:T(8,128)S(1)} collective-permute-done((f32[9,32,128]{2,1,0:T(8,128)S(1)}, f32[9,32,128]{2,1,0:T(8,128)S(1)}, u32[]{:S(2)}, u32[]{:S(2)}) %collective-permute-start.1) | collective-permute-done | bytes 147488 | tf_op jit(solution)/shard_map/ppermute | solution.py:335
  22.1 3.5 %collective-permute-done.2.refs_2_ = f32[9,32,128]{2,1,0:T(8,128)S(1)} collective-permute-done((f32[9,32,128]{2,1,0:T(8,128)S(1)}, f32[9,32,128]{2,1,0:T(8,128)S(1)}, u32[]{:S(2)}, u32[]{:S(2)}) %collective-permute-start.2) | collective-permute-done | bytes 147488 | tf_op jit(solution)/shard_map/ppermute | solution.py:335
  25.6 0.0 collective-permute-done.3.refs_3_
  25.6 0.7 add_up.1
  26.3 6.4 %all-to-all-start = ((f32[8,64,128]{2,1,0:T(8,128)}), f32[8,64,128]{2,1,0:T(8,128)S(1)}, u32[]{:S(2)}, u32[]{:S(2)}) async-start(f32[8,64,128]{2,1,0:T(8,128)} %add_up.1), calls=%async_computation | async-start | bytes 524288 | tf_op jit(solution)/shard_map/all_to_all | solution.py:356
  32.7 10.2 %all-to-all-done.parts_ref = f32[8,64,128]{2,1,0:T(8,128)S(1)} async-done(((f32[8,64,128]{2,1,0:T(8,128)}), f32[8,64,128]{2,1,0:T(8,128)S(1)}, u32[]{:S(2)}, u32[]{:S(2)}) %all-to-all-start) | async-done | bytes 262176 | tf_op jit(solution)/shard_map/all_to_all | solution.py:356
  42.9 0.4 moments.1
  43.3 2.7 %collective-permute-start.4 = (f32[16,128]{1,0:T(8,128)S(1)}, f32[16,128]{1,0:T(8,128)S(1)}, u32[]{:S(2)}, u32[]{:S(2)}) collective-permute-start(f32[16,128]{1,0:T(8,128)S(1)} %get-tuple-element.15), channel_id=1, source_target_pairs={{0,1},{1,0},{2,3},{3,2},{4,5},{5,4},{6,7},{7,6},{8,9},{9,8},{10,11... | collective-permute-start | bytes 24584 | tf_op jit(solution)/shard_map/ppermute | solution.py:335
  46.0 0.8 %collective-permute-done.4 = f32[16,128]{1,0:T(8,128)S(1)} collective-permute-done((f32[16,128]{1,0:T(8,128)S(1)}, f32[16,128]{1,0:T(8,128)S(1)}, u32[]{:S(2)}, u32[]{:S(2)}) %collective-permute-start.4) | collective-permute-done | bytes 8224 | tf_op jit(solution)/shard_map/ppermute | solution.py:335
  46.8 2.5 %collective-permute-start.7 = (f32[16,128]{1,0:T(8,128)S(1)}, f32[16,128]{1,0:T(8,128)S(1)}, u32[]{:S(2)}, u32[]{:S(2)}) collective-permute-start(f32[16,128]{1,0:T(8,128)S(1)} %add.16), channel_id=1, source_target_pairs={{0,192},{64,0},{128,64},{192,128},{1,193},{65,1},{129,65},{193,129... | collective-permute-start | bytes 24584 | tf_op jit(solution)/shard_map/ppermute | solution.py:335
  49.3 0.5 collective-permute-start.6
  49.8 0.6 collective-permute-start.5
  50.4 0.0 collective-permute-done.7
  50.5 2.9 %collective-permute-done.6 = f32[16,128]{1,0:T(8,128)S(1)} collective-permute-done((f32[16,128]{1,0:T(8,128)S(1)}, f32[16,128]{1,0:T(8,128)S(1)}, u32[]{:S(2)}, u32[]{:S(2)}) %collective-permute-start.6) | collective-permute-done | bytes 8224 | tf_op jit(solution)/shard_map/ppermute | solution.py:335
  53.3 0.2 collective-permute-done.5
  53.6 13.7 %all_to_all.10.mine_ref = f32[32,16,128]{2,1,0:T(8,128)S(1)} all-to-all(f32[32,16,128]{2,1,0:T(8,128)S(1)} %broadcast_in_dim.25), channel_id=1, replica_groups=mesh['grp'=4,'z'=8,'y'=4,'core'=2] {'y','z'}, dimensions={0} | all-to-all | bytes 524288 | tf_op jit(solution)/shard_map/all_to_all | solution.py:362
  67.3 4.0 %collective-permute-start.8 = (f32[32,16,128]{2,1,0:T(8,128)S(1)}, f32[32,16,128]{2,1,0:T(8,128)S(1)}, u32[]{:S(2)}, u32[]{:S(2)}) collective-permute-start(f32[32,16,128]{2,1,0:T(8,128)S(1)} %all_to_all.10.mine_ref), channel_id=1, source_target_pairs={{0,1},{1,0},{2,3},{3,2},{4,5},{5,4},{6,7},{7,6},{8,9},{9,8},{10,11... | collective-permute-start | bytes 786440 | tf_op jit(solution)/shard_map/ppermute | solution.py:335
  71.2 1.0 %own_maps.1.own_ref = f32[32,1024]{1,0:T(8,128)S(1)} custom-call(s32[1]{0:T(128)} %bitcast.half_ref, f32[32,16,128]{2,1,0:T(8,128)S(1)} %all_to_all.10.mine_ref, bf16[64,1024]{1,0:T(8,128)(2,1)S(1)} %bitcast.13), custom_call_target="tpu_custom_call" | custom-call | flops 268435456 | bytes 1048576 | tf_op jit(solution)/shard_map/own_maps/pallas_call | solution.py:271
  72.3 0.1 collective-permute-done.8.other_ref
  72.4 0.0 copy-done.2
  72.4 2.5 %maps.1 = (f32[30,1024]{1,0:T(8,128)}, f32[1,1024]{1,0:T(1,128)}) custom-call(s32[1]{0:T(128)} %bitcast.half_ref, s32[30]{0:T(128)S(1)} %copy-done.2, f32[32,1024]{1,0:T(8,128)S(1)} %own_maps.1.own_ref, f32[32,16,128]{2,1,0:T(8,128)S(1)} %all_to_all.10.mine_ref, f32[32,16,128]{2,1,0:T(8,128)S(1)} %collective-permute-done.8.other_ref, ...), custom_call_target="tpu_custom_call" | custom-call | flops 268435456 | bytes 1048576 | tf_op jit(solution)/shard_map/maps/pallas_call | solution.py:323
  (3 shorter events, 0.0 us)
Async XLA Ops:
  0.6 9.5 %copy-start.1 = (bf16[1024,64]{0,1:T(8,128)(2,1)S(1)}, bf16[1024,64]{0,1:T(8,128)(2,1)}, u32[]{:S(2)}) copy-start(bf16[1024,64]{0,1:T(8,128)(2,1)} %param.6) | copy-start | bytes 393220
  0.6 9.5 %copy-start = (f32[128,32,8]{0,2,1:T(8,128)S(1)}, f32[128,32,8]{0,2,1:T(8,128)}, u32[]{:S(2)}) copy-start(f32[128,32,8]{0,2,1:T(8,128)} %param.5) | copy-start | bytes 393220
  6.8 65.7 %copy-start.2 = (s32[30]{0:T(128)S(1)}, s32[30]{0:T(128)}, u32[]{:S(2)}) copy-start(s32[30]{0:T(128)} %order_ref.1) | copy-start | bytes 364
  6.8 8.2 %collective-permute-start = (f32[4,8,32,128]{3,2,1,0:T(8,128)}, f32[4,8,32,128]{3,2,1,0:T(8,128)S(1)}, u32[]{:S(2)}, u32[]{:S(2)}) collective-permute-start(f32[4,8,32,128]{3,2,1,0:T(8,128)} %project.3), channel_id=1, source_target_pairs={{0,1},{1,0},{2,3},{3,2},{4,5},{5,4},{6,7},{7,6},{8,9},{9,8},{10,11... | collective-permute-start | bytes 1572872 | tf_op jit(solution)/shard_map/ppermute | solution.py:335
  15.0 7.1 %collective-permute-start.1 = (f32[9,32,128]{2,1,0:T(8,128)S(1)}, f32[9,32,128]{2,1,0:T(8,128)S(1)}, u32[]{:S(2)}, u32[]{:S(2)}) collective-permute-start(f32[9,32,128]{2,1,0:T(8,128)S(1)} %get-tuple-element.11), channel_id=1, source_target_pairs={{0,4},{2,6},{4,0},{6,2},{1,5},{3,7},{5,1},{7,3},{8,12},{10,14},{12... | collective-permute-start | bytes 442376 | tf_op jit(solution)/shard_map/ppermute | solution.py:335
  16.3 9.3 %collective-permute-start.2 = (f32[9,32,128]{2,1,0:T(8,128)S(1)}, f32[9,32,128]{2,1,0:T(8,128)S(1)}, u32[]{:S(2)}, u32[]{:S(2)}) collective-permute-start(f32[9,32,128]{2,1,0:T(8,128)S(1)} %get-tuple-element.12), channel_id=1, source_target_pairs={{0,2},{2,4},{4,6},{6,0},{1,3},{3,5},{5,7},{7,1},{8,10},{10,12},{12... | collective-permute-start | bytes 442376 | tf_op jit(solution)/shard_map/ppermute | solution.py:335
  16.7 8.9 %collective-permute-start.3 = (f32[9,32,128]{2,1,0:T(8,128)S(1)}, f32[9,32,128]{2,1,0:T(8,128)S(1)}, u32[]{:S(2)}, u32[]{:S(2)}) collective-permute-start(f32[9,32,128]{2,1,0:T(8,128)S(1)} %get-tuple-element.13), channel_id=1, source_target_pairs={{0,6},{2,0},{4,2},{6,4},{1,7},{3,1},{5,3},{7,5},{8,14},{10,8},{12,... | collective-permute-start | bytes 442376 | tf_op jit(solution)/shard_map/ppermute | solution.py:335
  26.3 16.6 %all-to-all-start = ((f32[8,64,128]{2,1,0:T(8,128)}), f32[8,64,128]{2,1,0:T(8,128)S(1)}, u32[]{:S(2)}, u32[]{:S(2)}) async-start(f32[8,64,128]{2,1,0:T(8,128)} %add_up.1), calls=%async_computation | async-start | bytes 524288 | tf_op jit(solution)/shard_map/all_to_all | solution.py:356
  43.3 3.5 %collective-permute-start.4 = (f32[16,128]{1,0:T(8,128)S(1)}, f32[16,128]{1,0:T(8,128)S(1)}, u32[]{:S(2)}, u32[]{:S(2)}) collective-permute-start(f32[16,128]{1,0:T(8,128)S(1)} %get-tuple-element.15), channel_id=1, source_target_pairs={{0,1},{1,0},{2,3},{3,2},{4,5},{5,4},{6,7},{7,6},{8,9},{9,8},{10,11... | collective-permute-start | bytes 24584 | tf_op jit(solution)/shard_map/ppermute | solution.py:335
  46.8 3.6 %collective-permute-start.7 = (f32[16,128]{1,0:T(8,128)S(1)}, f32[16,128]{1,0:T(8,128)S(1)}, u32[]{:S(2)}, u32[]{:S(2)}) collective-permute-start(f32[16,128]{1,0:T(8,128)S(1)} %add.16), channel_id=1, source_target_pairs={{0,192},{64,0},{128,64},{192,128},{1,193},{65,1},{129,65},{193,129... | collective-permute-start | bytes 24584 | tf_op jit(solution)/shard_map/ppermute | solution.py:335
  49.3 4.0 %collective-permute-start.6 = (f32[16,128]{1,0:T(8,128)S(1)}, f32[16,128]{1,0:T(8,128)S(1)}, u32[]{:S(2)}, u32[]{:S(2)}) collective-permute-start(f32[16,128]{1,0:T(8,128)S(1)} %add.16), channel_id=1, source_target_pairs={{0,128},{64,192},{128,0},{192,64},{1,129},{65,193},{129,1},{193,65... | collective-permute-start | bytes 24584 | tf_op jit(solution)/shard_map/ppermute | solution.py:335
  49.8 3.7 %collective-permute-start.5 = (f32[16,128]{1,0:T(8,128)S(1)}, f32[16,128]{1,0:T(8,128)S(1)}, u32[]{:S(2)}, u32[]{:S(2)}) collective-permute-start(f32[16,128]{1,0:T(8,128)S(1)} %add.16), channel_id=1, source_target_pairs={{0,64},{64,128},{128,192},{192,0},{1,65},{65,129},{129,193},{193,1... | collective-permute-start | bytes 24584 | tf_op jit(solution)/shard_map/ppermute | solution.py:335
  67.3 5.2 %collective-permute-start.8 = (f32[32,16,128]{2,1,0:T(8,128)S(1)}, f32[32,16,128]{2,1,0:T(8,128)S(1)}, u32[]{:S(2)}, u32[]{:S(2)}) collective-permute-start(f32[32,16,128]{2,1,0:T(8,128)S(1)} %all_to_all.10.mine_ref), channel_id=1, source_target_pairs={{0,1},{1,0},{2,3},{3,2},{4,5},{5,4},{6,7},{7,6},{8,9},{9,8},{10,11... | collective-permute-start | bytes 786440 | tf_op jit(solution)/shard_map/ppermute | solution.py:335

commit v8 on v7

--- a/solution.py
+++ b/solution.py
@@ -357,7 +357,7 @@
 
     keep, send = moments(slot[None], core[None], parts)
     piece = keep + shifted(send, "core", 2, 1)
-    piece = piece + sum(shifted(piece, "grp", sizes["grp"], s) for s in range(1, sizes["grp"]))
+    piece = piece + sum(shifted(piece, "grp", sizes["grp"], s) for s in (1, 3, 2))
     copies = jnp.broadcast_to(piece[None], (slots,) + piece.shape)
     mine = lax.all_to_all(copies, ("y", "z"), 0, 0, tiled=True)
     other = shifted(mine, "core", 2, 1)

time: 75.1 us -> 75.7 us (level)
  no operation moved by 1% of the time
where the time goes in v8:
time: 75.7 us; the launch traced here: 75.5 us
  starting transfers between devices  24.6 us (32%)
  waiting for transfers between devices  20.9 us (28%)
  Pallas kernels  15.6 us (21%)
  blocking collectives  13.7 us (18%)
    ppermute x9, starting transfers between devices, shifted(): lax.ppermute(value, axis, [(i, (i + shift) % size) for i in range(size)])  18.2 us
    all_to_all x1, blocking collectives, on_device(): mine = lax.all_to_all(copies, ('y', 'z'), 0, 0, tiled=True)  13.7 us
    pallas_call x2, Pallas kernels, project(): pl.pallas_call(functools.partial(project_kernel, chunk), in_specs=[SMEM,...  10.9 us
    ppermute x9, waiting for transfers between devices, shifted(): lax.ppermute(value, axis, [(i, (i + shift) % size) for i in range(size)])  10.7 us
    all_to_all x1, waiting for transfers between devices, on_device(): parts = lax.all_to_all(parts, 'z', 0, 0, tiled=True)  10.2 us
    all_to_all x1, starting transfers between devices, on_device(): parts = lax.all_to_all(parts, 'z', 0, 0, tiled=True)  6.43 us
    pallas_call x1, Pallas kernels, make_maps(): pl.pallas_call(functools.partial(maps_kernel, rows_total, cell_total), in...  2.5 us
  transfers between devices with their start and end apart: 10, of which 7 were waited for; matrix products, arithmetic and copies ran while one was open for 0% of the time, Pallas kernels for 8%

profile of v8, /device:TPU:1, one launch (start us, length us, event | category | flops | bytes accessed | tf_op | source)
XLA Modules:
  0.0 75.5 jit_solution(15939701096117551808)
XLA Ops:
  0.6 0.0 copy-start.1
  0.6 0.0 copy-start
  0.7 6.1 %project.3 = f32[4,8,32,128]{3,2,1,0:T(8,128)} custom-call(s32[1]{0:T(128)} %bitcast.6.half_ref, s32[1]{0:T(128)} %bitcast.2.height_ref, bf16[128,32,1024]{2,1,0:T(8,128)(2,1)} %fields_ref.3, f32[256,128]{1,0:T(8,128)} %bitcast.9, bf16[64,1024]{1,0:T(8,128)(2,1)} %bitcast.11), custom_call_target="tpu_custom_call" | custom-call | flops 268435456 | bytes 4194304 | tf_op jit(solution)/shard_map/project/pallas_call | solution.py:115
  6.8 0.0 copy-start.2
  6.8 3.4 %collective-permute-start = (f32[4,8,32,128]{3,2,1,0:T(8,128)}, f32[4,8,32,128]{3,2,1,0:T(8,128)S(1)}, u32[]{:S(2)}, u32[]{:S(2)}) collective-permute-start(f32[4,8,32,128]{3,2,1,0:T(8,128)} %project.3), channel_id=1, source_target_pairs={{0,1},{1,0},{2,3},{3,2},{4,5},{5,4},{6,7},{7,6},{8,9},{9,8},{10,11... | collective-permute-start | bytes 1572872 | tf_op jit(solution)/shard_map/ppermute | solution.py:335
  10.1 0.0 copy-done.1
  10.2 0.0 copy-done
  10.2 4.8 %project.2.ours_ref = f32[4,8,32,128]{3,2,1,0:T(8,128)S(1)} custom-call(s32[1]{0:T(128)} %bitcast.half_ref, s32[1]{0:T(128)} %bitcast.2.height_ref, bf16[128,32,1024]{2,1,0:T(8,128)(2,1)} %fields_ref.3, f32[256,128]{1,0:T(8,128)S(1)} %bitcast.10, bf16[64,1024]{1,0:T(8,128)(2,1)S(1)} %bitcast.12), custom_call_target="tpu_custom_call" | custom-call | flops 268435456 | bytes 4194304 | tf_op jit(solution)/shard_map/project/pallas_call | solution.py:115
  14.9 0.0 collective-permute-done.got_ref
  15.0 0.1 combine.1
  15.0 1.3 %collective-permute-start.1 = (f32[9,32,128]{2,1,0:T(8,128)S(1)}, f32[9,32,128]{2,1,0:T(8,128)S(1)}, u32[]{:S(2)}, u32[]{:S(2)}) collective-permute-start(f32[9,32,128]{2,1,0:T(8,128)S(1)} %get-tuple-element.11), channel_id=1, source_target_pairs={{0,4},{2,6},{4,0},{6,2},{1,5},{3,7},{5,1},{7,3},{8,12},{10,14},{12... | collective-permute-start | bytes 442376 | tf_op jit(solution)/shard_map/ppermute | solution.py:335
  16.3 0.4 collective-permute-start.2
  16.7 2.3 %collective-permute-start.3 = (f32[9,32,128]{2,1,0:T(8,128)S(1)}, f32[9,32,128]{2,1,0:T(8,128)S(1)}, u32[]{:S(2)}, u32[]{:S(2)}) collective-permute-start(f32[9,32,128]{2,1,0:T(8,128)S(1)} %get-tuple-element.13), channel_id=1, source_target_pairs={{0,6},{2,0},{4,2},{6,4},{1,7},{3,1},{5,3},{7,5},{8,14},{10,8},{12,... | collective-permute-start | bytes 442376 | tf_op jit(solution)/shard_map/ppermute | solution.py:335
  19.0 3.1 %collective-permute-done.1.refs_1_ = f32[9,32,128]{2,1,0:T(8,128)S(1)} collective-permute-done((f32[9,32,128]{2,1,0:T(8,128)S(1)}, f32[9,32,128]{2,1,0:T(8,128)S(1)}, u32[]{:S(2)}, u32[]{:S(2)}) %collective-permute-start.1) | collective-permute-done | bytes 147488 | tf_op jit(solution)/shard_map/ppermute | solution.py:335
  22.1 3.5 %collective-permute-done.2.refs_2_ = f32[9,32,128]{2,1,0:T(8,128)S(1)} collective-permute-done((f32[9,32,128]{2,1,0:T(8,128)S(1)}, f32[9,32,128]{2,1,0:T(8,128)S(1)}, u32[]{:S(2)}, u32[]{:S(2)}) %collective-permute-start.2) | collective-permute-done | bytes 147488 | tf_op jit(solution)/shard_map/ppermute | solution.py:335
  25.6 0.0 collective-permute-done.3.refs_3_
  25.6 0.7 add_up.1
  26.3 6.4 %all-to-all-start = ((f32[8,64,128]{2,1,0:T(8,128)}), f32[8,64,128]{2,1,0:T(8,128)S(1)}, u32[]{:S(2)}, u32[]{:S(2)}) async-start(f32[8,64,128]{2,1,0:T(8,128)} %add_up.1), calls=%async_computation | async-start | bytes 524288 | tf_op jit(solution)/shard_map/all_to_all | solution.py:356
  32.7 10.2 %all-to-all-done.parts_ref = f32[8,64,128]{2,1,0:T(8,128)S(1)} async-done(((f32[8,64,128]{2,1,0:T(8,128)}), f32[8,64,128]{2,1,0:T(8,128)S(1)}, u32[]{:S(2)}, u32[]{:S(2)}) %all-to-all-start) | async-done | bytes 262176 | tf_op jit(solution)/shard_map/all_to_all | solution.py:356
  42.9 0.4 moments.1
  43.3 2.7 %collective-permute-start.4 = (f32[16,128]{1,0:T(8,128)S(1)}, f32[16,128]{1,0:T(8,128)S(1)}, u32[]{:S(2)}, u32[]{:S(2)}) collective-permute-start(f32[16,128]{1,0:T(8,128)S(1)} %get-tuple-element.15), channel_id=1, source_target_pairs={{0,1},{1,0},{2,3},{3,2},{4,5},{5,4},{6,7},{7,6},{8,9},{9,8},{10,11... | collective-permute-start | bytes 24584 | tf_op jit(solution)/shard_map/ppermute | solution.py:335
  46.0 0.8 %collective-permute-done.4 = f32[16,128]{1,0:T(8,128)S(1)} collective-permute-done((f32[16,128]{1,0:T(8,128)S(1)}, f32[16,128]{1,0:T(8,128)S(1)}, u32[]{:S(2)}, u32[]{:S(2)}) %collective-permute-start.4) | collective-permute-done | bytes 8224 | tf_op jit(solution)/shard_map/ppermute | solution.py:335
  46.8 2.7 %collective-permute-start.7 = (f32[16,128]{1,0:T(8,128)S(1)}, f32[16,128]{1,0:T(8,128)S(1)}, u32[]{:S(2)}, u32[]{:S(2)}) collective-permute-start(f32[16,128]{1,0:T(8,128)S(1)} %add.16), channel_id=1, source_target_pairs={{0,128},{64,192},{128,0},{192,64},{1,129},{65,193},{129,1},{193,65... | collective-permute-start | bytes 24584 | tf_op jit(solution)/shard_map/ppermute | solution.py:335
  49.6 0.9 %collective-permute-start.6 = (f32[16,128]{1,0:T(8,128)S(1)}, f32[16,128]{1,0:T(8,128)S(1)}, u32[]{:S(2)}, u32[]{:S(2)}) collective-permute-start(f32[16,128]{1,0:T(8,128)S(1)} %add.16), channel_id=1, source_target_pairs={{0,192},{64,0},{128,64},{192,128},{1,193},{65,1},{129,65},{193,129... | collective-permute-start | bytes 24584 | tf_op jit(solution)/shard_map/ppermute | solution.py:335
  50.5 0.6 collective-permute-start.5
  51.1 0.0 collective-permute-done.7
  51.1 1.0 %collective-permute-done.6 = f32[16,128]{1,0:T(8,128)S(1)} collective-permute-done((f32[16,128]{1,0:T(8,128)S(1)}, f32[16,128]{1,0:T(8,128)S(1)}, u32[]{:S(2)}, u32[]{:S(2)}) %collective-permute-start.6) | collective-permute-done | bytes 8224 | tf_op jit(solution)/shard_map/ppermute | solution.py:335
  52.1 2.1 %collective-permute-done.5 = f32[16,128]{1,0:T(8,128)S(1)} collective-permute-done((f32[16,128]{1,0:T(8,128)S(1)}, f32[16,128]{1,0:T(8,128)S(1)}, u32[]{:S(2)}, u32[]{:S(2)}) %collective-permute-start.5) | collective-permute-done | bytes 8224 | tf_op jit(solution)/shard_map/ppermute | solution.py:335
  54.2 13.7 %all_to_all.10.mine_ref = f32[32,16,128]{2,1,0:T(8,128)S(1)} all-to-all(f32[32,16,128]{2,1,0:T(8,128)S(1)} %broadcast_in_dim.25), channel_id=1, replica_groups=mesh['grp'=4,'z'=8,'y'=4,'core'=2] {'y','z'}, dimensions={0} | all-to-all | bytes 524288 | tf_op jit(solution)/shard_map/all_to_all | solution.py:362
  67.9 4.0 %collective-permute-start.8 = (f32[32,16,128]{2,1,0:T(8,128)S(1)}, f32[32,16,128]{2,1,0:T(8,128)S(1)}, u32[]{:S(2)}, u32[]{:S(2)}) collective-permute-start(f32[32,16,128]{2,1,0:T(8,128)S(1)} %all_to_all.10.mine_ref), channel_id=1, source_target_pairs={{0,1},{1,0},{2,3},{3,2},{4,5},{5,4},{6,7},{7,6},{8,9},{9,8},{10,11... | collective-permute-start | bytes 786440 | tf_op jit(solution)/shard_map/ppermute | solution.py:335
  71.9 1.0 %own_maps.1.own_ref = f32[32,1024]{1,0:T(8,128)S(1)} custom-call(s32[1]{0:T(128)} %bitcast.half_ref, f32[32,16,128]{2,1,0:T(8,128)S(1)} %all_to_all.10.mine_ref, bf16[64,1024]{1,0:T(8,128)(2,1)S(1)} %bitcast.13), custom_call_target="tpu_custom_call" | custom-call | flops 268435456 | bytes 1048576 | tf_op jit(solution)/shard_map/own_maps/pallas_call | solution.py:271
  72.9 0.1 collective-permute-done.8.other_ref
  73.0 0.0 copy-done.2
  73.0 2.5 %maps.1 = (f32[30,1024]{1,0:T(8,128)}, f32[1,1024]{1,0:T(1,128)}) custom-call(s32[1]{0:T(128)} %bitcast.half_ref, s32[30]{0:T(128)S(1)} %copy-done.2, f32[32,1024]{1,0:T(8,128)S(1)} %own_maps.1.own_ref, f32[32,16,128]{2,1,0:T(8,128)S(1)} %all_to_all.10.mine_ref, f32[32,16,128]{2,1,0:T(8,128)S(1)} %collective-permute-done.8.other_ref, ...), custom_call_target="tpu_custom_call" | custom-call | flops 268435456 | bytes 1048576 | tf_op jit(solution)/shard_map/maps/pallas_call | solution.py:323
  (3 shorter events, 0.0 us)
Async XLA Ops:
  0.6 9.5 %copy-start.1 = (bf16[1024,64]{0,1:T(8,128)(2,1)S(1)}, bf16[1024,64]{0,1:T(8,128)(2,1)}, u32[]{:S(2)}) copy-start(bf16[1024,64]{0,1:T(8,128)(2,1)} %param.6) | copy-start | bytes 393220
  0.6 9.5 %copy-start = (f32[128,32,8]{0,2,1:T(8,128)S(1)}, f32[128,32,8]{0,2,1:T(8,128)}, u32[]{:S(2)}) copy-start(f32[128,32,8]{0,2,1:T(8,128)} %param.5) | copy-start | bytes 393220
  6.8 66.3 %copy-start.2 = (s32[30]{0:T(128)S(1)}, s32[30]{0:T(128)}, u32[]{:S(2)}) copy-start(s32[30]{0:T(128)} %order_ref.1) | copy-start | bytes 364
  6.8 8.2 %collective-permute-start = (f32[4,8,32,128]{3,2,1,0:T(8,128)}, f32[4,8,32,128]{3,2,1,0:T(8,128)S(1)}, u32[]{:S(2)}, u32[]{:S(2)}) collective-permute-start(f32[4,8,32,128]{3,2,1,0:T(8,128)} %project.3), channel_id=1, source_target_pairs={{0,1},{1,0},{2,3},{3,2},{4,5},{5,4},{6,7},{7,6},{8,9},{9,8},{10,11... | collective-permute-start | bytes 1572872 | tf_op jit(solution)/shard_map/ppermute | solution.py:335
  15.0 7.1 %collective-permute-start.1 = (f32[9,32,128]{2,1,0:T(8,128)S(1)}, f32[9,32,128]{2,1,0:T(8,128)S(1)}, u32[]{:S(2)}, u32[]{:S(2)}) collective-permute-start(f32[9,32,128]{2,1,0:T(8,128)S(1)} %get-tuple-element.11), channel_id=1, source_target_pairs={{0,4},{2,6},{4,0},{6,2},{1,5},{3,7},{5,1},{7,3},{8,12},{10,14},{12... | collective-permute-start | bytes 442376 | tf_op jit(solution)/shard_map/ppermute | solution.py:335
  16.3 9.3 %collective-permute-start.2 = (f32[9,32,128]{2,1,0:T(8,128)S(1)}, f32[9,32,128]{2,1,0:T(8,128)S(1)}, u32[]{:S(2)}, u32[]{:S(2)}) collective-permute-start(f32[9,32,128]{2,1,0:T(8,128)S(1)} %get-tuple-element.12), channel_id=1, source_target_pairs={{0,2},{2,4},{4,6},{6,0},{1,3},{3,5},{5,7},{7,1},{8,10},{10,12},{12... | collective-permute-start | bytes 442376 | tf_op jit(solution)/shard_map/ppermute | solution.py:335
  16.7 8.9 %collective-permute-start.3 = (f32[9,32,128]{2,1,0:T(8,128)S(1)}, f32[9,32,128]{2,1,0:T(8,128)S(1)}, u32[]{:S(2)}, u32[]{:S(2)}) collective-permute-start(f32[9,32,128]{2,1,0:T(8,128)S(1)} %get-tuple-element.13), channel_id=1, source_target_pairs={{0,6},{2,0},{4,2},{6,4},{1,7},{3,1},{5,3},{7,5},{8,14},{10,8},{12,... | collective-permute-start | bytes 442376 | tf_op jit(solution)/shard_map/ppermute | solution.py:335
  26.3 16.6 %all-to-all-start = ((f32[8,64,128]{2,1,0:T(8,128)}), f32[8,64,128]{2,1,0:T(8,128)S(1)}, u32[]{:S(2)}, u32[]{:S(2)}) async-start(f32[8,64,128]{2,1,0:T(8,128)} %add_up.1), calls=%async_computation | async-start | bytes 524288 | tf_op jit(solution)/shard_map/all_to_all | solution.py:356
  43.3 3.5 %collective-permute-start.4 = (f32[16,128]{1,0:T(8,128)S(1)}, f32[16,128]{1,0:T(8,128)S(1)}, u32[]{:S(2)}, u32[]{:S(2)}) collective-permute-start(f32[16,128]{1,0:T(8,128)S(1)} %get-tuple-element.15), channel_id=1, source_target_pairs={{0,1},{1,0},{2,3},{3,2},{4,5},{5,4},{6,7},{7,6},{8,9},{9,8},{10,11... | collective-permute-start | bytes 24584 | tf_op jit(solution)/shard_map/ppermute | solution.py:335
  46.8 4.2 %collective-permute-start.7 = (f32[16,128]{1,0:T(8,128)S(1)}, f32[16,128]{1,0:T(8,128)S(1)}, u32[]{:S(2)}, u32[]{:S(2)}) collective-permute-start(f32[16,128]{1,0:T(8,128)S(1)} %add.16), channel_id=1, source_target_pairs={{0,128},{64,192},{128,0},{192,64},{1,129},{65,193},{129,1},{193,65... | collective-permute-start | bytes 24584 | tf_op jit(solution)/shard_map/ppermute | solution.py:335
  49.6 2.5 %collective-permute-start.6 = (f32[16,128]{1,0:T(8,128)S(1)}, f32[16,128]{1,0:T(8,128)S(1)}, u32[]{:S(2)}, u32[]{:S(2)}) collective-permute-start(f32[16,128]{1,0:T(8,128)S(1)} %add.16), channel_id=1, source_target_pairs={{0,192},{64,0},{128,64},{192,128},{1,193},{65,1},{129,65},{193,129... | collective-permute-start | bytes 24584 | tf_op jit(solution)/shard_map/ppermute | solution.py:335
  50.5 3.7 %collective-permute-start.5 = (f32[16,128]{1,0:T(8,128)S(1)}, f32[16,128]{1,0:T(8,128)S(1)}, u32[]{:S(2)}, u32[]{:S(2)}) collective-permute-start(f32[16,128]{1,0:T(8,128)S(1)} %add.16), channel_id=1, source_target_pairs={{0,64},{64,128},{128,192},{192,0},{1,65},{65,129},{129,193},{193,1... | collective-permute-start | bytes 24584 | tf_op jit(solution)/shard_map/ppermute | solution.py:335
  67.9 5.2 %collective-permute-start.8 = (f32[32,16,128]{2,1,0:T(8,128)S(1)}, f32[32,16,128]{2,1,0:T(8,128)S(1)}, u32[]{:S(2)}, u32[]{:S(2)}) collective-permute-start(f32[32,16,128]{2,1,0:T(8,128)S(1)} %all_to_all.10.mine_ref), channel_id=1, source_target_pairs={{0,1},{1,0},{2,3},{3,2},{4,5},{5,4},{6,7},{7,6},{8,9},{9,8},{10,11... | collective-permute-start | bytes 786440 | tf_op jit(solution)/shard_map/ppermute | solution.py:335
